TPU v7x, 32 devices: a whole 2x2x4 slice. The times are simulated.
32 devices in a mesh: clip: 4 (over x, core), seq: 2 (over y), tensor: 4 (over z).
Axes of the slice: x: 2, y: 2, z: 4, core: 2. Of those that a mesh axis runs over, the one named last changes fastest.
Arguments:
- clips_in: bfloat16 [16, 8, 4, 16, 384], P('clip', None, 'seq', 'tensor'), may hold values from -6 to 6
- cotangent: bfloat16 [16, 8, 2, 8, 768], P('clip', None, 'seq', 'tensor'), may hold values from -6 to 6
- resets: int32 [16], replicated, may hold values 0 or 1
- videos: int32 [16], replicated, may hold values from 0 to 3, never falling along the last dimension, each value on 1 to 8 neighbouring positions
- attend_gain_a: float32 [384], replicated, may hold values from 0.5 to 1.5
- project_a: bfloat16 [384, 1152], replicated, may hold values from -0.4375 to 0.4375
- pooling_a: float32 [2, 4, 384], replicated, may hold values from 0.2 to 0.6
- squeeze_a: float32 [2, 4, 384], replicated, may hold values from 0.1 to 0.5
- offsets_a: float32 [4, 31], replicated, may hold values from -4 to 4
- output_a: bfloat16 [384, 384], replicated, may hold values from -0.21875 to 0.21875
- mixer_gain_a: float32 [384], replicated, may hold values from 0.5 to 1.5
- expand_a: bfloat16 [384, 1536], P(None, 'tensor'), may hold values from -0.3125 to 0.3125
- reduce_a: bfloat16 [1536, 384], P('tensor'), may hold values from -0.15625 to 0.15625
- attend_gain_b: float32 [384], replicated, may hold values from 0.5 to 1.5
- project_b: bfloat16 [384, 2304], replicated, may hold values from -0.4375 to 0.4375
- pooling_b: float32 [3, 4, 768], replicated, may hold values from 0.2 to 0.6
- squeeze_b: float32 [2, 4, 768], replicated, may hold values from 0.1 to 0.5
- offsets_b: float32 [8, 31], replicated, may hold values from -4 to 4
- output_b: bfloat16 [768, 768], replicated, may hold values from -0.15625 to 0.15625
- shortcut_b: bfloat16 [384, 768], replicated, may hold values from -0.3125 to 0.3125
- mixer_gain_b: float32 [768], replicated, may hold values from 0.5 to 1.5
- expand_b: bfloat16 [768, 3072], P(None, 'tensor'), may hold values from -0.21875 to 0.21875
- reduce_b: bfloat16 [3072, 768], P('tensor'), may hold values from -0.109375 to 0.109375
Outputs:
- out_field: float32 [16, 8, 2, 8, 768], P('clip', None, 'seq', 'tensor')
- grad_input: float32 [16, 8, 4, 16, 384], P('clip', None, 'seq', 'tensor')
- grad_attend_gain_a: float32 [384], replicated
- grad_project_a: float32 [384, 1152], P('tensor')
- grad_pooling_a: float32 [2, 4, 384], replicated
- grad_squeeze_a: float32 [2, 4, 384], replicated
- grad_offsets_a: float32 [4, 31], replicated
- grad_output_a: float32 [384, 384], P('tensor')
- grad_mixer_gain_a: float32 [384], replicated
- grad_expand_a: float32 [384, 1536], P(None, 'tensor')
- grad_reduce_a: float32 [1536, 384], P('tensor')
- grad_attend_gain_b: float32 [384], replicated
- grad_project_b: float32 [384, 2304], P('tensor')
- grad_pooling_b: float32 [3, 4, 768], replicated
- grad_squeeze_b: float32 [2, 4, 768], replicated
- grad_offsets_b: float32 [8, 31], replicated
- grad_output_b: float32 [768, 768], P('tensor')
- grad_shortcut_b: float32 [384, 768], P('tensor')
- grad_mixer_gain_b: float32 [768], replicated
- grad_expand_b: float32 [768, 3072], P(None, 'tensor')
- grad_reduce_b: float32 [3072, 768], P('tensor')
Inputs may be any that keep to these rules, and one draw needn't show every extreme that they name: `videos`: video ids never fall along the clips; a video has 1 to 8 clips in a row, one has exactly 8.
All inputs are finite; a program needn't handle non-finite values.
Results may differ from a plain program's by a relative error of at most 0.029.
Values may be sent and summed in bfloat16 or wider, within the bound.
No kernel may reach another device: no remote copies, remote signals or barrier semaphores. Data moves between devices by JAX's collectives and lax.ppermute only.
A program may use at most 128 MiB of HBM per device.

v0:
```python
import jax
import jax.numpy as jnp
from jax import lax
from jax.sharding import PartitionSpec as P

HIGHEST = lax.Precision.HIGHEST
EPSILON = 1e-06
MASKED = -1000000000.0
LOG_FOUR = 1.3862943611198906


def passed_along(shard, axis, by):
    devices = lax.axis_size(axis)
    pairs = [(i, i + by) for i in range(devices) if 0 <= i + by < devices]
    return lax.ppermute(shard, axis, pairs)


def inner_left(left, right):
    return lax.dot_general(
        left, right, (((0,), (0,)), ((), ())), preferred_element_type=jnp.float32
    )


def inner_right(left, right):
    return lax.dot_general(
        left, right, (((1,), (1,)), ((), ())), preferred_element_type=jnp.float32
    )


def layer_norm(field, gain):
    mean = jnp.mean(field, axis=-1, keepdims=True)
    centered = field - mean
    inverse = lax.rsqrt(jnp.mean(centered * centered, axis=-1, keepdims=True) + EPSILON)
    normed = centered * inverse
    return (normed * gain, (normed, inverse))


def norm_back(grad, gain, kept):
    normed, inverse = kept
    scaled = grad * gain
    grad_field = inverse * (
        scaled
        - jnp.mean(scaled, axis=-1, keepdims=True)
        - normed * jnp.mean(scaled * normed, axis=-1, keepdims=True)
    )
    grad_gain = jnp.sum((grad * normed).reshape(-1, grad.shape[-1]), axis=0)
    return (grad_field, grad_gain)


def pool_grid(field, weights):
    total = field[..., 0::2, 0::2, :] * weights[0]
    total = total + field[..., 0::2, 1::2, :] * weights[1]
    total = total + field[..., 1::2, 0::2, :] * weights[2]
    total = total + field[..., 1::2, 1::2, :] * weights[3]
    return total


def compress_time(field, weights):
    total = field[..., 0::4, :, :, :] * weights[0]
    total = total + field[..., 1::4, :, :, :] * weights[1]
    total = total + field[..., 2::4, :, :, :] * weights[2]
    total = total + field[..., 3::4, :, :, :] * weights[3]
    return total


def pool_squeeze(raw, pair_weights, pair_squeeze):
    pooled = pool_grid(raw, pair_weights)
    return (pooled, compress_time(pooled, pair_squeeze))


def smooth_max(field):
    stacked = jnp.stack(
        [
            field[..., 0::2, 0::2, :],
            field[..., 0::2, 1::2, :],
            field[..., 1::2, 0::2, :],
            field[..., 1::2, 1::2, :],
        ],
        axis=0,
    )
    highest = jnp.max(stacked, axis=0)
    return highest + jnp.log(jnp.sum(jnp.exp(stacked - highest), axis=0)) - LOG_FOUR


def gaussian_gate(values):
    return jax.nn.gelu(values, approximate=False)


def memory_valid(resets, videos, clip_ids):
    before = jnp.maximum(clip_ids - 1, 0)
    earlier = jnp.maximum(clip_ids - 2, 0)
    first = (clip_ids >= 1) & (videos[clip_ids] == videos[before]) & (resets[clip_ids] == 0)
    second = first & (clip_ids >= 2) & (videos[before] == videos[earlier]) & (resets[before] == 0)
    return (first, second)


def key_layout(count, per_frame, frames):
    index = jnp.arange(count, dtype=jnp.int32)
    current = frames * per_frame
    memory = frames // 4 * per_frame
    offset = index % (current + 2 * memory)
    first = offset - current
    second = first - memory
    times = jnp.where(
        offset < current,
        offset // per_frame,
        jnp.where(
            first < memory,
            4 * (first // per_frame) - frames,
            4 * (second // per_frame) - 2 * frames,
        ),
    )
    kind = jnp.where(offset < current, 0, jnp.where(first < memory, 1, 2))
    return (times, kind)


def relative_onehot(times, frames, entries):
    index = jnp.arange(frames, dtype=jnp.int32)[:, None] - times[None, :] + frames - 1
    return (index[:, :, None] == jnp.arange(entries, dtype=jnp.int32)[None, None, :]).astype(
        jnp.float32
    )


def key_mask(kind, first_ok, second_ok):
    return (
        (kind[None, :] == 0)
        | (kind[None, :] == 1) & first_ok[:, None]
        | (kind[None, :] == 2) & second_ok[:, None]
    )


def split_groups(values, steps):
    return values.reshape((steps, values.shape[0] // steps) + values.shape[1:])


def gather_keys(block):
    return lax.all_gather(block, ("seq", "tensor"), axis=1, tiled=True)


def tensor_rows(values):
    return lax.all_gather(values, "tensor", axis=0, tiled=True)


def score_block(query_rows, keys_all, bias, mask, heads):
    clips, rows, width = query_rows.shape
    size = width // heads
    count = keys_all.shape[1]
    frames = bias.shape[1]
    query_heads = query_rows.reshape(clips, rows, heads, size)
    key_heads = keys_all[:, :, :width].reshape(clips, count, heads, size)
    value_heads = keys_all[:, :, width:].reshape(clips, count, heads, size)
    scores = jnp.einsum(
        "cqhd,ckhd->chqk", query_heads, key_heads, preferred_element_type=jnp.float32
    ) * size ** (-0.5)
    scores = scores.reshape(clips, heads, frames, rows // frames, count) + bias[None, :, :, None, :]
    scores = jnp.where(mask[:, None, None, None, :], scores, MASKED)
    return (scores.reshape(clips, heads, rows, count), query_heads, key_heads, value_heads)


def attend(query_rows, keys_all, bias, mask, heads):
    scores, query_heads, key_heads, value_heads = score_block(
        query_rows, keys_all, bias, mask, heads
    )
    highest = jnp.max(scores, axis=-1, keepdims=True)
    log_total = highest + jnp.log(jnp.sum(jnp.exp(scores - highest), axis=-1, keepdims=True))
    probs_r = jnp.exp(scores - log_total).astype(jnp.bfloat16)
    mixed = jnp.einsum("chqk,ckhd->cqhd", probs_r, value_heads, preferred_element_type=jnp.float32)
    return (mixed.reshape(query_rows.shape) + query_rows.astype(jnp.float32), log_total)


def attend_back(grad_out, query_rows, keys_all, bias, mask, log_total, heads):
    clips, rows, width = query_rows.shape
    size = width // heads
    frames = bias.shape[1]
    scores, query_heads, key_heads, value_heads = score_block(
        query_rows, keys_all, bias, mask, heads
    )
    probs = jnp.exp(scores - log_total)
    probs_r = probs.astype(jnp.bfloat16)
    grad_heads_r = grad_out.astype(jnp.bfloat16).reshape(clips, rows, heads, size)
    grad_probs = jnp.einsum(
        "cqhd,ckhd->chqk", grad_heads_r, value_heads, preferred_element_type=jnp.float32
    )
    grad_values = jnp.einsum(
        "chqk,cqhd->ckhd", probs_r, grad_heads_r, preferred_element_type=jnp.float32
    )
    grad_scores = probs * (grad_probs - jnp.sum(probs * grad_probs, axis=-1, keepdims=True))
    grad_scores_r = grad_scores.astype(jnp.bfloat16)
    grad_bias = jnp.sum(
        grad_scores_r.reshape(clips, heads, frames, rows // frames, -1),
        axis=(0, 3),
        dtype=jnp.float32,
    )
    grad_query = jnp.einsum(
        "chqk,ckhd->cqhd", grad_scores_r, key_heads, preferred_element_type=jnp.float32
    ) * size ** (-0.5)
    grad_query = grad_query.reshape(clips, rows, width) + grad_out
    grad_keys = jnp.einsum(
        "chqk,cqhd->ckhd", grad_scores_r, query_heads, preferred_element_type=jnp.float32
    ) * size ** (-0.5)
    grad_pairs = jnp.concatenate(
        [grad_keys.reshape(clips, -1, width), grad_values.reshape(clips, -1, width)], axis=-1
    )
    return (grad_query, grad_pairs, grad_bias)


def layer_forward(field, params, first_ok, second_ok, pooled_query, group):
    (
        gain_in,
        in_weights,
        pool_weights,
        squeeze_weights,
        table,
        out_weights,
        skip_weights,
        gain_mid,
        up_weights,
        down_weights,
    ) = params
    clips, frames, rows_h, rows_w, width_in = field.shape
    width = out_weights.shape[0]
    heads = table.shape[0]
    normed, norm_kept = layer_norm(field, gain_in)
    flat_r = normed.astype(jnp.bfloat16).reshape(-1, width_in)
    projected = jnp.dot(flat_r, in_weights, preferred_element_type=jnp.float32).reshape(
        clips, frames, rows_h, rows_w, 3 * width
    )
    pair_weights = jnp.concatenate([pool_weights[-2], pool_weights[-1]], axis=-1)
    pair_squeeze = jnp.concatenate([squeeze_weights[0], squeeze_weights[1]], axis=-1)
    pooled, compact = pool_squeeze(projected[..., width:], pair_weights, pair_squeeze)
    if pooled_query:
        query = pool_grid(projected[..., :width], pool_weights[0])
    else:
        query = projected[..., :width]
    query_r = query.astype(jnp.bfloat16)
    compact_r = compact.astype(jnp.bfloat16)
    arrived = passed_along(compact_r[clips - 2 :], "clip", 1)
    chain = jnp.concatenate([arrived, compact_r], axis=0)
    block = jnp.concatenate(
        [
            pooled.astype(jnp.bfloat16).reshape(clips, -1, 2 * width),
            chain[1 : clips + 1].reshape(clips, -1, 2 * width),
            chain[0:clips].reshape(clips, -1, 2 * width),
        ],
        axis=1,
    )
    per_frame = pooled.shape[2] * pooled.shape[3]
    times, kind = key_layout(lax.axis_size(("seq", "tensor")) * block.shape[1], per_frame, frames)
    onehot = relative_onehot(times, frames, table.shape[1])
    bias = jnp.einsum("hr,tkr->htk", table, onehot, precision=HIGHEST)
    mask = key_mask(kind, first_ok, second_ok)
    query_rows = query_r.reshape(clips, -1, width)
    steps = clips // group

    def forward_step(items):
        return attend(items[0], gather_keys(items[1]), bias, items[2], heads)

    mixed, record = lax.map(
        forward_step,
        (split_groups(query_rows, steps), split_groups(block, steps), split_groups(mask, steps)),
    )
    mixed_r = mixed.astype(jnp.bfloat16).reshape(-1, width)
    branch = jnp.dot(mixed_r, out_weights, preferred_element_type=jnp.float32)
    if pooled_query:
        skip_raw = jnp.dot(flat_r, skip_weights, preferred_element_type=jnp.float32).reshape(
            clips, frames, rows_h, rows_w, width
        )
        base = smooth_max(skip_raw)
    else:
        skip_raw = None
        base = field
    middle = base.reshape(-1, width) + branch
    normed2, norm2_kept = layer_norm(middle, gain_mid)
    rows_all = tensor_rows(normed2.astype(jnp.bfloat16))
    hidden_pre = jnp.dot(rows_all, up_weights, preferred_element_type=jnp.float32)
    hidden_r = gaussian_gate(hidden_pre).astype(jnp.bfloat16)
    mlp_out = lax.psum_scatter(
        jnp.dot(hidden_r, down_weights, preferred_element_type=jnp.float32).astype(jnp.bfloat16),
        "tensor",
        scatter_dimension=0,
        tiled=True,
    ).astype(jnp.float32)
    result = (middle + mlp_out).reshape(base.shape)
    kept = (
        field,
        norm_kept,
        flat_r,
        projected,
        query_r,
        block,
        onehot,
        bias,
        mask,
        record,
        mixed_r,
        skip_raw,
        norm2_kept,
        rows_all,
        hidden_pre,
        hidden_r,
        pair_weights,
        pair_squeeze,
        pooled.shape,
        compact.shape,
    )
    return (result, kept)


def layer_backward(grad, kept, params, pooled_query, group):
    (
        gain_in,
        in_weights,
        pool_weights,
        squeeze_weights,
        table,
        out_weights,
        skip_weights,
        gain_mid,
        up_weights,
        down_weights,
    ) = params
    (
        field,
        norm_kept,
        flat_r,
        projected,
        query_r,
        block,
        onehot,
        bias,
        mask,
        record,
        mixed_r,
        skip_raw,
        norm2_kept,
        rows_all,
        hidden_pre,
        hidden_r,
        pair_weights,
        pair_squeeze,
        pooled_shape,
        compact_shape,
    ) = kept
    clips, frames = (field.shape[0], field.shape[1])
    width = out_weights.shape[0]
    heads = table.shape[0]
    grad_rows = grad.reshape(-1, width)
    grad_all = tensor_rows(grad_rows.astype(jnp.bfloat16))
    grad_down = inner_left(hidden_r, grad_all)
    grad_hidden = inner_right(grad_all, down_weights)
    gate_back = jax.vjp(gaussian_gate, hidden_pre)[1]
    grad_pre_r = gate_back(grad_hidden)[0].astype(jnp.bfloat16)
    grad_up = inner_left(rows_all, grad_pre_r)
    grad_normed2 = lax.psum_scatter(
        inner_right(grad_pre_r, up_weights).astype(jnp.bfloat16),
        "tensor",
        scatter_dimension=0,
        tiled=True,
    ).astype(jnp.float32)
    grad_mid_part, grad_gain_mid = norm_back(grad_normed2, gain_mid, norm2_kept)
    grad_middle = grad_rows + grad_mid_part
    grad_middle_r = grad_middle.astype(jnp.bfloat16)
    grad_out_weights = inner_left(mixed_r, grad_middle_r)
    grad_mixed = inner_right(grad_middle_r, out_weights).reshape(clips, -1, width)
    query_rows = query_r.reshape(clips, -1, width)
    steps = clips // group

    def backward_step(bias_total, items):
        grad_part, query_part, block_part, mask_part, total_part = items
        grad_query_part, grad_pairs, grad_bias_part = attend_back(
            grad_part, query_part, gather_keys(block_part), bias, mask_part, total_part, heads
        )
        grad_block_part = lax.psum_scatter(
            grad_pairs.astype(jnp.bfloat16), ("seq", "tensor"), scatter_dimension=1, tiled=True
        ).astype(jnp.float32)
        return (bias_total + grad_bias_part, (grad_query_part, grad_block_part))

    grad_bias, (grad_query, grad_block) = lax.scan(
        backward_step,
        jnp.zeros_like(bias),
        (
            split_groups(grad_mixed, steps),
            split_groups(query_rows, steps),
            split_groups(block, steps),
            split_groups(mask, steps),
            record,
        ),
    )
    grad_query = grad_query.reshape(query_r.shape)
    grad_block = grad_block.reshape(clips, -1, 2 * width)
    grad_table = jnp.einsum("htk,tkr->hr", grad_bias, onehot, precision=HIGHEST)
    per_frame = pooled_shape[2] * pooled_shape[3]
    lead = frames * per_frame
    part = frames // 4 * per_frame
    grad_pooled = grad_block[:, :lead].reshape(pooled_shape)
    grad_first = grad_block[:, lead : lead + part].reshape(compact_shape)
    grad_second = grad_block[:, lead + part :].reshape(compact_shape)
    grad_chain = jnp.pad(grad_first, [(1, 1), (0, 0), (0, 0), (0, 0), (0, 0)]) + jnp.pad(
        grad_second, [(0, 2), (0, 0), (0, 0), (0, 0), (0, 0)]
    )
    returned = passed_along(grad_chain[:2].astype(jnp.bfloat16), "clip", -1).astype(jnp.float32)
    grad_compact = grad_chain[2:] + jnp.pad(
        returned, [(clips - 2, 0), (0, 0), (0, 0), (0, 0), (0, 0)]
    )
    pair_back = jax.vjp(pool_squeeze, projected[..., width:], pair_weights, pair_squeeze)[1]
    grad_pair_raw, grad_pair_weights, grad_pair_squeeze = pair_back((grad_pooled, grad_compact))
    if pooled_query:
        query_back = jax.vjp(pool_grid, projected[..., :width], pool_weights[0])[1]
        grad_query_raw, grad_query_pool = query_back(grad_query)
        grad_pool = jnp.stack(
            [grad_query_pool, grad_pair_weights[:, :width], grad_pair_weights[:, width:]]
        )
    else:
        grad_query_raw = grad_query
        grad_pool = jnp.stack([grad_pair_weights[:, :width], grad_pair_weights[:, width:]])
    grad_squeeze = jnp.stack([grad_pair_squeeze[:, :width], grad_pair_squeeze[:, width:]])
    grad_projected_r = (
        jnp.concatenate([grad_query_raw, grad_pair_raw], axis=-1)
        .astype(jnp.bfloat16)
        .reshape(-1, 3 * width)
    )
    grad_in_weights = inner_left(flat_r, grad_projected_r)
    grad_normed = inner_right(grad_projected_r, in_weights)
    if pooled_query:
        skip_back = jax.vjp(smooth_max, skip_raw)[1]
        grad_skip_r = (
            skip_back(grad_middle.reshape(grad.shape))[0].astype(jnp.bfloat16).reshape(-1, width)
        )
        grad_skip = inner_left(flat_r, grad_skip_r)
        grad_normed = grad_normed + inner_right(grad_skip_r, skip_weights)
        grad_field, grad_gain_in = norm_back(grad_normed.reshape(field.shape), gain_in, norm_kept)
    else:
        grad_skip = None
        grad_norm_part, grad_gain_in = norm_back(
            grad_normed.reshape(field.shape), gain_in, norm_kept
        )
        grad_field = grad_norm_part + grad_middle.reshape(field.shape)
    return (
        grad_field,
        (
            grad_gain_in,
            grad_in_weights,
            grad_pool,
            grad_squeeze,
            grad_table,
            grad_out_weights,
            grad_skip,
            grad_gain_mid,
            grad_up,
            grad_down,
        ),
    )


def local(
    clips_in,
    cotangent,
    resets,
    videos,
    attend_gain_a,
    project_a,
    pooling_a,
    squeeze_a,
    offsets_a,
    output_a,
    mixer_gain_a,
    expand_a,
    reduce_a,
    attend_gain_b,
    project_b,
    pooling_b,
    squeeze_b,
    offsets_b,
    output_b,
    shortcut_b,
    mixer_gain_b,
    expand_b,
    reduce_b,
):
    clips = clips_in.shape[0]
    clip_ids = lax.axis_index("clip") * clips + jnp.arange(clips, dtype=jnp.int32)
    first_ok, second_ok = memory_valid(resets, videos, clip_ids)
    params_a = (
        attend_gain_a,
        project_a,
        pooling_a,
        squeeze_a,
        offsets_a,
        output_a,
        None,
        mixer_gain_a,
        expand_a,
        reduce_a,
    )
    params_b = (
        attend_gain_b,
        project_b,
        pooling_b,
        squeeze_b,
        offsets_b,
        output_b,
        shortcut_b,
        mixer_gain_b,
        expand_b,
        reduce_b,
    )
    group_first = min(clips, 4)
    group_second = min(clips, 2)

    def run_forward(field_in):
        middle_field, kept_first = layer_forward(
            field_in, params_a, first_ok, second_ok, False, group_first
        )
        final_field, kept_second = layer_forward(
            middle_field, params_b, first_ok, second_ok, True, group_second
        )
        return (final_field, kept_first, kept_second)

    field = clips_in.astype(jnp.float32)
    result, kept_a, kept_b = run_forward(field)
    field_again, cot_held = lax.optimization_barrier((field, cotangent))
    unused, kept_a, kept_b = run_forward(field_again)
    grad_middle_field, grads_b = layer_backward(
        cot_held.astype(jnp.float32), kept_b, params_b, True, group_second
    )
    grad_field, grads_a = layer_backward(grad_middle_field, kept_a, params_a, False, group_first)
    shares = (
        lax.psum_scatter(
            grads_a[1].astype(jnp.bfloat16), "tensor", scatter_dimension=0, tiled=True
        ).astype(jnp.float32),
        lax.psum_scatter(
            grads_a[5].astype(jnp.bfloat16), "tensor", scatter_dimension=0, tiled=True
        ).astype(jnp.float32),
        lax.psum_scatter(
            grads_b[1].astype(jnp.bfloat16), "tensor", scatter_dimension=0, tiled=True
        ).astype(jnp.float32),
        lax.psum_scatter(
            grads_b[5].astype(jnp.bfloat16), "tensor", scatter_dimension=0, tiled=True
        ).astype(jnp.float32),
        lax.psum_scatter(
            grads_b[6].astype(jnp.bfloat16), "tensor", scatter_dimension=0, tiled=True
        ).astype(jnp.float32),
    )
    small = lax.psum(
        (
            grads_a[0],
            grads_a[2],
            grads_a[3],
            grads_a[4],
            grads_a[7],
            grads_b[0],
            grads_b[2],
            grads_b[3],
            grads_b[4],
            grads_b[7],
        ),
        ("clip", "seq", "tensor"),
    )
    split = lax.psum(
        (
            grads_a[8],
            grads_a[9],
            grads_b[8],
            grads_b[9],
            shares[0],
            shares[1],
            shares[2],
            shares[3],
            shares[4],
        ),
        ("clip", "seq"),
    )
    return (
        result,
        grad_field,
        small[0],
        split[4],
        small[1],
        small[2],
        small[3],
        split[5],
        small[4],
        split[0],
        split[1],
        small[5],
        split[6],
        small[6],
        small[7],
        small[8],
        split[7],
        split[8],
        small[9],
        split[2],
        split[3],
    )


def solution(mesh):
    placed = (
        P("clip", None, "seq", "tensor", None),
        P("clip", None, "seq", "tensor", None),
        P(),
        P(),
        P(),
        P(),
        P(),
        P(),
        P(),
        P(),
        P(),
        P(None, "tensor"),
        P("tensor", None),
        P(),
        P(),
        P(),
        P(),
        P(),
        P(),
        P(),
        P(),
        P(None, "tensor"),
        P("tensor", None),
    )
    return jax.shard_map(
        local,
        mesh=mesh,
        in_specs=placed,
        out_specs=(
            P("clip", None, "seq", "tensor", None),
            P("clip", None, "seq", "tensor", None),
            P(),
            P("tensor", None),
            P(),
            P(),
            P(),
            P("tensor", None),
            P(),
            P(None, "tensor"),
            P("tensor", None),
            P(),
            P("tensor", None),
            P(),
            P(),
            P(),
            P("tensor", None),
            P("tensor", None),
            P(),
            P(None, "tensor"),
            P("tensor", None),
        ),
        check_vma=False,
    )
```

profile of v0, /device:TPU:0, one launch (start us, length us, event | category | flops | bytes accessed | tf_op | source)
XLA Modules:
  0.0 1485.5 jit_solution(1159620852177973890)
XLA Ops:
  65.9 18.0 %all-gather.21.cloned.1.call-done = bf16[4,192,768]{2,0,1:T(4,128)(2,1)} async-done(((bf16[4,24,768]{2,0,1:T(4,128)(2,1)}), bf16[4,192,768]{2,0,1:T(4,128)(2,1)}) %all-gather.21.cloned.1.call-update) | async-done | bytes 1179664 | tf_op jit(solution)/shard_map/while/body/eval_jaxpr/all_gather | solution.py:137
  88.6 37.8 %all-gather.19.cloned.1.call-done = bf16[4,192,768]{2,0,1:T(4,128)(2,1)} async-done(((bf16[4,24,768]{2,0,1:T(4,128)(2,1)}), bf16[4,192,768]{2,0,1:T(4,128)(2,1)}) %all-gather.19.cloned.1.call-update) | async-done | bytes 1179664 | tf_op jit(solution)/shard_map/while/body/eval_jaxpr/all_gather | solution.py:137
  148.8 19.0 %all_gather.38 = bf16[1024,384]{1,0:T(8,128)(2,1)} all-gather(bf16[256,384]{1,0:T(8,128)(2,1)S(1)} %get-tuple-element.805), channel_id=1, replica_groups=mesh['clip'=4,'seq'=2,'tensor'=4] {'tensor'}, dimensions={0}, use_global_device_ids=true | all-gather | bytes 983040 | tf_op jit(solution)/shard_map/all_gather | solution.py:141
  167.8 6.4 convolution_convert_fusion.5
  174.3 24.1 %all_gather.41 = bf16[1024,384]{1,0:T(8,128)(2,1)S(1)} all-gather(bf16[256,384]{1,0:T(8,128)(2,1)S(1)} %get-tuple-element.804), channel_id=1, replica_groups=mesh['clip'=4,'seq'=2,'tensor'=4] {'tensor'}, dimensions={0}, use_global_device_ids=true | all-gather | bytes 983040 | tf_op jit(solution)/shard_map/all_gather | solution.py:141
  198.4 6.2 multiply_convert_fusion.3
  208.5 18.0 %all_gather.43 = bf16[256,768]{1,0:T(8,128)(2,1)} all-gather(bf16[64,768]{1,0:T(8,128)(2,1)S(1)} %copy-done.94), channel_id=1, replica_groups=mesh['clip'=4,'seq'=2,'tensor'=4] {'tensor'}, dimensions={0}, use_global_device_ids=true | all-gather | bytes 491520 | tf_op jit(solution)/shard_map/all_gather | solution.py:141
  267.7 105.3 %while.11 = (s32[]{:T(128)}, bf16[2,2,16,768]{3,2,1,0:T(8,128)(2,1)}, f32[2,2,8,16,1]{3,2,1,4,0:T(8,128)}, bf16[2,2,24,1536]{3,2,1,0:T(8,128)(2,1)}, pred[2,2,19...) while((s32[]{:T(128)}, ...), condition=%wide.region_30.31_spmd.clone, body=%wide.region_27.30_spmd.sunk.clone | while | flops 19316480 | bytes 12992841 | solution.py:258
  271.0 40.6 %all-gather.25.cloned.1.call-done = bf16[1,2,192,1536]{3,2,1,0:T(8,128)(2,1)} async-done(((bf16[1,2,24,1536]{3,2,1,0:T(8,128)(2,1)}), bf16[1,2,192,1536]{3,2,1,0:T(8,128)(2,1)}) %all-gather.25.cloned.1.call-update) | async-done | bytes 1179664 | tf_op jit(solution)/shard_map/while/body/eval_jaxpr/all_gather | solution.py:137
  324.1 39.7 %all-gather.25.cloned.1.call-done = bf16[1,2,192,1536]{3,2,1,0:T(8,128)(2,1)} async-done(((bf16[1,2,24,1536]{3,2,1,0:T(8,128)(2,1)}), bf16[1,2,192,1536]{3,2,1,0:T(8,128)(2,1)}) %all-gather.25.cloned.1.call-update) | async-done | bytes 1179664 | tf_op jit(solution)/shard_map/while/body/eval_jaxpr/all_gather | solution.py:137
  375.2 15.2 %all_gather.42 = bf16[256,768]{1,0:T(8,128)(2,1)S(1)} all-gather(bf16[64,768]{1,0:T(8,128)(2,1)S(1)} %multiply_convert_fusion.14), channel_id=1, replica_groups=mesh['clip'=4,'seq'=2,'tensor'=4] {'tensor'}, dimensions={0}, use_global_device_ids=true | all-gather | bytes 491520 | tf_op jit(solution)/shard_map/all_gather | solution.py:141
  421.8 278.7 %while.12 = (s32[]{:T(128)}, f32[8,8,192]{2,1,0:T(8,128)}, f32[2,2,16,768]{3,2,1,0:T(8,128)}, f32[2,2,24,1536]{3,2,1,0:T(8,128)}, pred[2,2,192]{2,1,0:T(4,128)(4...) while((s32[]{:T(128)}, f32[8,8,192]{2,1,0:T(8,128)}, ...), condition=%wide.region_41.42_spmd.clone.clone, body=%wide.region_36.41_spmd.clone.sunk.clone | while | flops 51744512 | bytes 32601296 | solution.py:378
  426.7 38.0 %all-gather.27.cloned.1.call-done = bf16[1,2,192,1536]{3,2,1,0:T(8,128)(2,1)} async-done(((bf16[1,2,24,1536]{3,2,1,0:T(8,128)(2,1)}), bf16[1,2,192,1536]{3,2,1,0:T(8,128)(2,1)}) %all-gather.27.cloned.1.call-update) | async-done | bytes 1179664 | tf_op jit(solution)/shard_map/while/body/eval_jaxpr/all_gather | solution.py:137
  481.8 77.2 %all-reduce.70.cloned.1.call-done = bf16[2,192,1536]{2,0,1:T(2,128)(2,1)} async-done(((bf16[2,192,1536]{2,0,1:T(2,128)(2,1)}), bf16[2,192,1536]{2,0,1:T(2,128)(2,1)}) %all-reduce.70.cloned.1.call-update) | async-done | bytes 1179664 | tf_op jit(solution)/shard_map/while
  565.7 38.7 %all-gather.27.cloned.1.call-done = bf16[1,2,192,1536]{3,2,1,0:T(8,128)(2,1)} async-done(((bf16[1,2,24,1536]{3,2,1,0:T(8,128)(2,1)}), bf16[1,2,192,1536]{3,2,1,0:T(8,128)(2,1)}) %all-gather.27.cloned.1.call-update) | async-done | bytes 1179664 | tf_op jit(solution)/shard_map/while/body/eval_jaxpr/all_gather | solution.py:137
  621.4 77.2 %all-reduce.70.cloned.1.call-done = bf16[2,192,1536]{2,0,1:T(2,128)(2,1)} async-done(((bf16[2,192,1536]{2,0,1:T(2,128)(2,1)}), bf16[2,192,1536]{2,0,1:T(2,128)(2,1)}) %all-reduce.70.cloned.1.call-update) | async-done | bytes 1179664 | tf_op jit(solution)/shard_map/while
  800.2 5.7 pad.190
  815.3 17.9 %all_gather.44 = bf16[1024,384]{1,0:T(8,128)(2,1)S(1)} all-gather(bf16[256,384]{1,0:T(8,128)(2,1)S(1)} %get-tuple-element.694), channel_id=1, replica_groups=mesh['clip'=4,'seq'=2,'tensor'=4] {'tensor'}, dimensions={0}, use_global_device_ids=true | all-gather | bytes 983040 | tf_op jit(solution)/shard_map/all_gather | solution.py:141
  837.8 96.0 %while.10 = (s32[]{:T(128)}, bf16[2,2,16,768]{3,2,1,0:T(8,128)(2,1)S(1)}, bf16[2,2,24,1536]{3,2,1,0:T(8,128)(2,1)}, pred[2,2,192]{2,1,0:T(4,128)(4,1)S(1)}, bf16...) while((s32[]{:T(128)}, bf16[2,2,16,768]{3,2,1,0:T(8,128)(2,1)S(1)}, ...), condition=%wide.region_13.14_spmd.clone, body=%wide.region_10.13_spmd.sunk.clone | while | flops 19316480 | bytes 12198149 | solution.py:258
  839.8 41.9 %all-gather.23.cloned.1.call-done = bf16[1,2,192,1536]{3,2,1,0:T(8,128)(2,1)} async-done(((bf16[1,2,24,1536]{3,2,1,0:T(8,128)(2,1)}), bf16[1,2,192,1536]{3,2,1,0:T(8,128)(2,1)}) %all-gather.23.cloned.1.call-update) | async-done | bytes 1179664 | tf_op jit(solution)/shard_map/while/body/eval_jaxpr/all_gather | solution.py:137
  888.0 41.4 %all-gather.23.cloned.1.call-done = bf16[1,2,192,1536]{3,2,1,0:T(8,128)(2,1)} async-done(((bf16[1,2,24,1536]{3,2,1,0:T(8,128)(2,1)}), bf16[1,2,192,1536]{3,2,1,0:T(8,128)(2,1)}) %all-gather.23.cloned.1.call-update) | async-done | bytes 1179664 | tf_op jit(solution)/shard_map/while/body/eval_jaxpr/all_gather | solution.py:137
  939.0 20.1 %reduce-scatter.19.cloned.1.call-done = bf16[256,384]{1,0:T(8,128)(2,1)} async-done(((bf16[1024,384]{1,0:T(8,128)(2,1)}), bf16[256,384]{1,0:T(8,128)(2,1)}) %reduce-scatter.19.cloned.1.call-update) | async-done | bytes 196624 | tf_op jit(solution)/shard_map/reduce_scatter | solution.py:354
  974.8 17.8 %all_gather.39 = bf16[256,768]{1,0:T(8,128)(2,1)S(1)} all-gather(bf16[64,768]{1,0:T(8,128)(2,1)S(1)} %multiply_convert_fusion.15), channel_id=1, replica_groups=mesh['clip'=4,'seq'=2,'tensor'=4] {'tensor'}, dimensions={0}, use_global_device_ids=true | all-gather | bytes 491520 | tf_op jit(solution)/shard_map/all_gather | solution.py:141
  1015.7 42.3 %all-reduce.64.cloned.1.call-done = bf16[4,192,768]{2,0,1:T(4,128)(2,1)} async-done(((bf16[4,192,768]{2,0,1:T(4,128)(2,1)}), bf16[4,192,768]{2,0,1:T(4,128)(2,1)}) %all-reduce.64.cloned.1.call-update) | async-done | bytes 1179664
  1087.3 16.5 %reduce-scatter.29.cloned.1.call-done = bf16[96,768]{1,0:T(8,128)(2,1)} async-done(((bf16[384,768]{1,0:T(8,128)(2,1)}), bf16[96,768]{1,0:T(8,128)(2,1)}) %reduce-scatter.29.cloned.1.call-update) | async-done | bytes 147472 | tf_op jit(solution)/shard_map/reduce_scatter | solution.py:540
  1103.9 21.2 %reduce-scatter.23.cloned.1.call-done = bf16[96,384]{1,0:T(8,128)(2,1)} async-done(((bf16[384,384]{1,0:T(8,128)(2,1)}), bf16[96,384]{1,0:T(8,128)(2,1)}) %reduce-scatter.23.cloned.1.call-update) | async-done | bytes 73744 | tf_op jit(solution)/shard_map/reduce_scatter | solution.py:531
  1125.2 29.9 %reduce-scatter.27.cloned.1.call-done = bf16[192,768]{1,0:T(8,128)(2,1)} async-done(((bf16[768,768]{1,0:T(8,128)(2,1)}), bf16[192,768]{1,0:T(8,128)(2,1)}) %reduce-scatter.27.cloned.1.call-update) | async-done | bytes 294928 | tf_op jit(solution)/shard_map/reduce_scatter | solution.py:537
  1156.2 38.2 %reduce-scatter.25.cloned.1.call-done = bf16[96,2304]{1,0:T(8,128)(2,1)} async-done(((bf16[384,2304]{1,0:T(8,128)(2,1)}), bf16[96,2304]{1,0:T(8,128)(2,1)}) %reduce-scatter.25.cloned.1.call-update) | async-done | bytes 442384 | tf_op jit(solution)/shard_map/reduce_scatter | solution.py:534
  1194.4 26.6 %reduce-scatter.21.cloned.1.call-done = bf16[96,1152]{1,0:T(8,128)(2,1)} async-done(((bf16[384,1152]{1,0:T(8,128)(2,1)}), bf16[96,1152]{1,0:T(8,128)(2,1)}) %reduce-scatter.21.cloned.1.call-update) | async-done | bytes 221200 | tf_op jit(solution)/shard_map/reduce_scatter | solution.py:528
  1221.0 98.1 %all-reduce.71 = (f32[96,1152]{1,0:T(8,128)}, f32[96,384]{1,0:T(8,128)}, f32[96,2304]{1,0:T(8,128)}, f32[192,768]{1,0:T(8,128)}, f32[96,768]{1,0:T(8,128)}) all-reduce(bf16[96,1152]{1,0:T(8,128)(2,1)} %reduce-scatter.21.cloned.1.call-done, ...), channel_id=1, replica_groups=mesh['clip'=4,'seq'=2,'tensor'=4] {'clip','seq'}, use_global_device_ids=true, to_apply=%region_56.57 | all-reduce | flops 589824 | bytes 3538944 | tf_op jit(solution)/shard_map/psum | solution.py:559
  1319.1 36.8 %all-reduce.66.cloned.1.call-done = (f32[384]{0:T(512)}, f32[2,4,384]{2,1,0:T(4,128)}, f32[2,4,384]{2,1,0:T(4,128)}, f32[4,31]{1,0:T(4,128)}, f32[384]{0:T(512)}...) async-done(((f32[384]{0:T(512)}, f32[2,4,384]{2,1,0:T(4,128)}, f32[2,4,384]{2,1,0:T(4,128)}, ...) | async-done | bytes 95200 | tf_op jit(solution)/shard_map/psum | solution.py:544
  1355.9 105.5 %all-reduce.68.cloned.1.call-done = (f32[384,384]{1,0:T(8,128)}, f32[384,384]{1,0:T(8,128)}, f32[768,768]{1,0:T(8,128)}, f32[768,768]{1,0:T(8,128)}) async-done(((f32[384,384]{1,0:T(8,128)}, f32[384,384]{1,0:T(8,128)}, f32[768,768]{1,0:T(8,128)}, f32[768,768]{1,0:T(8,128)}), (f32[384,384]{1,0:T(8,128)}, f32[384,384]{1,0:T(8,128)}, f32[768,768]{1,0:T(8,128)}, ...) | async-done | bytes 5898256 | tf_op jit(solution)/shard_map/psum | solution.py:559
  (1057 shorter events, 449.1 us)
Async XLA Ops:
  7.2 230.6 %copy-start = (bf16[384,2304]{1,0:T(8,128)(2,1)S(1)}, bf16[384,2304]{1,0:T(8,128)(2,1)}, u32[]{:S(2)}) copy-start(bf16[384,2304]{1,0:T(8,128)(2,1)} %param.43) | copy-start | bytes 5308420
  7.2 76.7 %all-gather.21.cloned.1.call-start = ((), (), s32[]{:S(2)}) async-start(), calls=%async_computation.13 | async-start | bytes 1327104 | tf_op jit(solution)/shard_map/while/body/eval_jaxpr/all_gather | solution.py:137
  34.0 3.4 collective-permute-start.2
  38.3 88.1 %all-gather.19.cloned.1.call-start = ((), (), s32[]{:S(2)}) async-start(), calls=%async_computation.10 | async-start | bytes 1327104 | tf_op jit(solution)/shard_map/while/body/eval_jaxpr/all_gather | solution.py:137
  38.4 15.5 %collective-permute-start = (bf16[2,2,1,2,768]{4,1,3,2,0:T(2,128)(2,1)S(1)}, bf16[2,2,1,2,768]{4,1,3,2,0:T(2,128)(2,1)S(1)}, u32[]{:S(2)}, u32[]{:S(2)}) collective-permute-start(bf16[2,2,1,2,768]{4,1,3,2,0:T(2,128)(2,1)S(1)} %slice.652), channel_id=1, source_target_pairs={{0,8},{8,16},{16,24},{1,9},{9,17},{17,25},{2,10},{10,18},{18,26},{... | collective-permute-start | bytes 36872 | tf_op jit(solution)/shard_map/ppermute | solution.py:15
  54.8 173.1 %reduce-scatter.11.cloned.1.call-start = ((), (), s32[]{:S(2)}) async-start(), calls=%async_computation.11 | async-start | bytes 983040 | tf_op jit(solution)/shard_map/reduce_scatter | solution.py:277
  174.3 56.7 %reduce-scatter.15.cloned.1.call-start = ((), (), s32[]{:S(2)}) async-start(), calls=%async_computation.14 | async-start | bytes 983040 | tf_op jit(solution)/shard_map/reduce_scatter | solution.py:277
  258.9 6.9 collective-permute-start.3
  267.7 43.9 %all-gather.25.cloned.1.call-start = ((), (), s32[]{:S(2)}) async-start(), calls=%async_computation.26 | async-start | bytes 1327104 | tf_op jit(solution)/shard_map/while/body/eval_jaxpr/all_gather | solution.py:137
  320.7 43.1 %all-gather.25.cloned.1.call-start = ((), (), s32[]{:S(2)}) async-start(), calls=%async_computation.26 | async-start | bytes 1327104 | tf_op jit(solution)/shard_map/while/body/eval_jaxpr/all_gather | solution.py:137
  373.0 42.8 %reduce-scatter.17.cloned.1.call-start = ((), (), s32[]{:S(2)}) async-start(), calls=%async_computation.15 | async-start | bytes 491520 | tf_op jit(solution)/shard_map/reduce_scatter | solution.py:354
  421.8 42.9 %all-gather.27.cloned.1.call-start = ((), (), s32[]{:S(2)}) async-start(), calls=%async_computation.27 | async-start | bytes 1327104 | tf_op jit(solution)/shard_map/while/body/eval_jaxpr/all_gather | solution.py:137
  423.5 135.5 %all-reduce.70.cloned.1.call-start = ((), (), s32[]{:S(2)}) async-start(), calls=%async_computation.28 | async-start | bytes 2359296 | tf_op jit(solution)/shard_map/while
  560.8 43.6 %all-gather.27.cloned.1.call-start = ((), (), s32[]{:S(2)}) async-start(), calls=%async_computation.27 | async-start | bytes 1327104 | tf_op jit(solution)/shard_map/while/body/eval_jaxpr/all_gather | solution.py:137
  562.5 136.2 %all-reduce.70.cloned.1.call-start = ((), (), s32[]{:S(2)}) async-start(), calls=%async_computation.28 | async-start | bytes 2359296 | tf_op jit(solution)/shard_map/while
  704.4 48.8 %collective-permute-start.4 = (bf16[2,2,1,2,1536]{4,1,3,2,0:T(2,128)(2,1)}, bf16[2,2,1,2,1536]{4,1,3,2,0:T(2,128)(2,1)}, u32[]{:S(2)}, u32[]{:S(2)}) collective-permute-start(bf16[2,2,1,2,1536]{4,1,3,2,0:T(2,128)(2,1)} %fusion.192), channel_id=1, source_target_pairs={{8,0},{16,8},{24,16},{9,1},{17,9},{25,17},{10,2},{18,10},{26,18},{... | collective-permute-start | bytes 73736 | tf_op jit(solution)/shard_map/ppermute | solution.py:15
  758.3 77.7 %collective-permute-start.1 = (bf16[2,2,1,2,1536]{4,1,3,2,0:T(2,128)(2,1)}, bf16[2,2,1,2,1536]{4,1,3,2,0:T(2,128)(2,1)}, u32[]{:S(2)}, u32[]{:S(2)}) collective-permute-start(bf16[2,2,1,2,1536]{4,1,3,2,0:T(2,128)(2,1)} %slice.670), channel_id=1, source_target_pairs={{0,8},{8,16},{16,24},{1,9},{9,17},{17,25},{2,10},{10,18},{18,26},{... | collective-permute-start | bytes 73736 | tf_op jit(solution)/shard_map/ppermute | solution.py:15
  837.8 43.8 %all-gather.23.cloned.1.call-start = ((), (), s32[]{:S(2)}) async-start(), calls=%async_computation.25 | async-start | bytes 1327104 | tf_op jit(solution)/shard_map/while/body/eval_jaxpr/all_gather | solution.py:137
  886.0 43.4 %all-gather.23.cloned.1.call-start = ((), (), s32[]{:S(2)}) async-start(), calls=%async_computation.25 | async-start | bytes 1327104 | tf_op jit(solution)/shard_map/while/body/eval_jaxpr/all_gather | solution.py:137
  933.8 25.3 %reduce-scatter.19.cloned.1.call-start = ((), (), s32[]{:S(2)}) async-start(), calls=%async_computation.16 | async-start | bytes 983040 | tf_op jit(solution)/shard_map/reduce_scatter | solution.py:354
  934.4 123.6 %all-reduce.64.cloned.1.call-start = ((), (), s32[]{:S(2)}) async-start(), calls=%async_computation.22 | async-start | bytes 2359296
  974.6 111.0 %reduce-scatter.13.cloned.1.call-start = ((), (), s32[]{:S(2)}) async-start(), calls=%async_computation.12 | async-start | bytes 491520 | tf_op jit(solution)/shard_map/reduce_scatter | solution.py:277
  997.5 106.3 %reduce-scatter.29.cloned.1.call-start = ((), (), s32[]{:S(2)}) async-start(), calls=%async_computation.21 | async-start | bytes 737280 | tf_op jit(solution)/shard_map/reduce_scatter | solution.py:540
  999.6 125.6 %reduce-scatter.23.cloned.1.call-start = ((), (), s32[]{:S(2)}) async-start(), calls=%async_computation.18 | async-start | bytes 368640 | tf_op jit(solution)/shard_map/reduce_scatter | solution.py:531
  1002.0 153.1 %reduce-scatter.27.cloned.1.call-start = ((), (), s32[]{:S(2)}) async-start(), calls=%async_computation.20 | async-start | bytes 1474560 | tf_op jit(solution)/shard_map/reduce_scatter | solution.py:537
  1007.3 187.1 %reduce-scatter.25.cloned.1.call-start = ((), (), s32[]{:S(2)}) async-start(), calls=%async_computation.19 | async-start | bytes 2211840 | tf_op jit(solution)/shard_map/reduce_scatter | solution.py:534
  1012.7 208.3 %reduce-scatter.21.cloned.1.call-start = ((), (), s32[]{:S(2)}) async-start(), calls=%async_computation.17 | async-start | bytes 1105920 | tf_op jit(solution)/shard_map/reduce_scatter | solution.py:528
  1059.0 3.2 collective-permute-start.5
  1074.5 281.4 %all-reduce.66.cloned.1.call-start = ((), (), s32[]{:S(2)}) async-start(), calls=%async_computation.23 | async-start | bytes 204800 | tf_op jit(solution)/shard_map/psum | solution.py:544
  1082.9 378.5 %all-reduce.68.cloned.1.call-start = ((), (), s32[]{:S(2)}) async-start(), calls=%async_computation.24 | async-start | bytes 11796480 | tf_op jit(solution)/shard_map/psum | solution.py:559
  1355.9 117.7 %copy-start.227 = (f32[8,31]{1,0:T(8,128)S(1)}, f32[8,31]{1,0:T(8,128)}, u32[]{:S(2)}) copy-start(f32[8,31]{1,0:T(8,128)} %get-tuple-element.1171) | copy-start | bytes 2980
  1355.9 118.3 %copy-start.226 = (f32[768]{0:T(1024)S(1)}, f32[768]{0:T(1024)}, u32[]{:S(2)}) copy-start(f32[768]{0:T(1024)} %get-tuple-element.1174) | copy-start | bytes 9220
  (249 other events, 3393.2 us)
Sparse Core Ops, SparseCore 0:
  38.4 45.4 all-gather.20
  86.6 39.7 all-gather.18
  174.4 27.8 reduce-scatter.10
  206.3 24.6 reduce-scatter.14
  270.9 40.6 all-gather.24
  323.9 39.8 all-gather.24
  396.0 19.7 reduce-scatter.16
  425.3 39.3 all-gather.26
  479.9 78.9 all-reduce.69
  564.0 40.2 all-gather.26
  619.6 78.9 all-reduce.69
  841.0 40.5 all-gather.22
  889.6 39.8 all-gather.22
  937.2 21.8 reduce-scatter.18
  974.8 83.1 all-reduce.63
  1060.7 19.8 reduce-scatter.12
  1083.3 20.4 reduce-scatter.28
  1106.5 18.5 reduce-scatter.22
  1127.5 27.5 reduce-scatter.26
  1157.3 37.0 reduce-scatter.24
  1197.3 23.6 reduce-scatter.20
  1228.6 127.2 all-reduce.65
  1360.7 100.6 all-reduce.67
where the time goes:
time: 1500 us; the launch traced here: 1490 us
  waiting for transfers between devices  793 us (53%)
  local copies, waits for them, and re-layouts  278 us (19%)
  blocking collectives  210 us (14%)
  matrix products  85.4 us (6%)
  other arithmetic  80.8 us (5%)
  between operations  18.3 us (1%)
  starting transfers between devices  17.4 us (1%)
    all_gather x8, waiting for transfers between devices, gather_keys(): return lax.all_gather(block, ('seq', 'tensor'), axis=1, tiled=True)  296 us
    while x10, waiting for transfers between devices  155 us
    all_gather x6, blocking collectives, tensor_rows(): return lax.all_gather(values, 'tensor', axis=0, tiled=True)  112 us
    psum x1, waiting for transfers between devices, local(): lax.psum((grads_a[8], grads_a[9], grads_b[8], grads_b[9], shares[0], shar...  106 us
    psum x1, blocking collectives, local(): lax.psum((grads_a[8], grads_a[9], grads_b[8], grads_b[9], shares[0], shar...  98.1 us
    unnamed x16, waiting for transfers between devices  43.1 us
    reduce_scatter x1, waiting for transfers between devices, local(): lax.psum_scatter(grads_b[1].astype(jnp.bfloat16), 'tensor', scatter_dimen...  38.2 us
    psum x1, waiting for transfers between devices, local(): lax.psum((grads_a[0], grads_a[2], grads_a[3], grads_a[4], grads_a[7], gra...  36.8 us
  transfers between devices with their start and end apart: 29, of which 22 were waited for; matrix products, arithmetic and copies ran while one was open for 15% of the time, Pallas kernels for 0%

commit v1 on v0

v1 whole, which is shorter than its diff:
```python
import functools

import jax
import jax.numpy as jnp
import numpy as np
from jax import lax
from jax.experimental import pallas as pl
from jax.experimental.pallas import tpu as pltpu
from jax.sharding import Mesh
from jax.sharding import PartitionSpec as P

F32 = jnp.float32
BF16 = jnp.bfloat16
HIGHEST = lax.Precision.HIGHEST
EPSILON = 1e-06
MASKED = -1000000000.0
LOG_FOUR = 1.3862943611198906
SIZE = 96
LANES = 384
INTERPRET = False
PLANE = ("chip", "core", "seq")
EVERY = ("chip", "core", "seq", "tensor")


def log2(n):
    return n.bit_length() - 1


def mm(left, right):
    return jnp.dot(left, right, preferred_element_type=F32)


def mm_tl(left, right):
    return lax.dot_general(left, right, (((0,), (0,)), ((), ())), preferred_element_type=F32)


def mm_tr(left, right):
    return lax.dot_general(left, right, (((1,), (1,)), ((), ())), preferred_element_type=F32)


def norm(field):
    mean = jnp.mean(field, axis=-1, keepdims=True)
    centered = field - mean
    inverse = lax.rsqrt(jnp.mean(centered * centered, axis=-1, keepdims=True) + EPSILON)
    return centered * inverse, inverse


def norm_back(grad, gain, normed, inverse):
    scaled = grad * gain
    field = inverse * (
        scaled
        - jnp.mean(scaled, axis=-1, keepdims=True)
        - normed * jnp.mean(scaled * normed, axis=-1, keepdims=True)
    )
    return field, jnp.sum(grad * normed, axis=0, keepdims=True)


def gelu(values):
    return 0.5 * values * (1.0 + lax.erf(values * 0.7071067811865476))


def gelu_both(values):
    half = 0.5 * (1.0 + lax.erf(values * 0.7071067811865476))
    slope = half + values * jnp.exp(-0.5 * values * values) * 0.3989422804014327
    return values * half, slope


def blocks(values, count):
    rows = values.shape[0] // count
    return [values[i * rows : (i + 1) * rows] for i in range(count)]


def pool(values, weights):
    parts = blocks(values, 4)
    total = parts[0] * weights[0:1]
    for p in range(1, 4):
        total = total + parts[p] * weights[p : p + 1]
    return total


class Plan:
    def __init__(self, seq, tensor, shape):
        clips, frames, rows, cols, _ = shape
        self.seq, self.tensor = seq, tensor
        assert clips == tensor and frames % seq == 0 and rows % 2 == 0 and cols % 2 == 0
        self.all_frames = frames
        self.frames = frames // seq
        self.rows, self.cols = rows, cols
        self.group = seq * tensor
        self.cells = self.group * rows * cols // 4
        self.pooled = self.frames * self.cells
        self.tokens = 4 * self.pooled
        self.local_squeeze = self.frames % 4 == 0
        self.memory = frames // 4 * self.cells
        self.own = seq * self.pooled
        self.keys = self.own + 2 * self.memory
        for n in (self.cells, self.pooled, self.memory, self.own, self.frames, seq):
            assert n == 1 << log2(n)

    def arrange(self):
        take = np.arange(self.tokens).reshape(
            self.group, self.frames, self.rows // 2, 2, self.cols // 2, 2
        )
        per = self.frames * self.rows * self.cols
        half = per // 4 * 2
        step = per + half
        x_rows = take // per * step + take % per
        x_rows = x_rows.transpose(3, 5, 1, 0, 2, 4).reshape(-1)
        cot = np.arange(self.pooled).reshape(self.group, self.frames, -1)
        low = cot // (per // 4) * step + per + cot % (per // 4) * 2
        low = low.transpose(1, 0, 2).reshape(-1)
        order = np.concatenate([x_rows, low, low + 1])
        return (order[:, None] == np.arange(self.group * step)[None, :]).astype(np.float32)


def clip_scalars(plan, resets, videos):
    s = lax.axis_index("seq")
    chip = lax.axis_index("chip") * lax.axis_size("core") + lax.axis_index("core")
    g = chip * plan.tensor + lax.axis_index("tensor")
    before = jnp.maximum(g - 1, 0)
    earlier = jnp.maximum(g - 2, 0)
    first = (g >= 1) & (videos[g] == videos[before]) & (resets[g] == 0)
    second = first & (g >= 2) & (videos[before] == videos[earlier]) & (resets[before] == 0)
    return s, first.astype(jnp.int32), second.astype(jnp.int32)


def key_facts(plan, s, first, second):
    k = lax.broadcasted_iota(jnp.int32, (1, plan.keys), 1)
    own_time = ((s ^ (k >> log2(plan.pooled))) << log2(plan.frames)) + (
        (k & (plan.pooled - 1)) >> log2(plan.cells)
    )
    m = k - plan.own
    late = (m >> log2(plan.memory)) > 0
    g = (m & (plan.memory - 1)) >> log2(plan.cells)
    if plan.local_squeeze:
        each = log2(plan.frames // 4)
        squeezed = ((s ^ (g >> each)) << each) + (g & (plan.frames // 4 - 1))
    else:
        squeezed = (s >> log2(4 // plan.frames)) ^ g
    kind = jnp.where(m < 0, 0, jnp.where(late, 2, 1))
    time = jnp.where(m < 0, own_time, 4 * squeezed - plan.all_frames * kind)
    counts = jnp.where(kind == 0, 1, jnp.where(kind == 1, first, second))
    return time, counts


def offset_onehot(plan, s, time, frame):
    index = s * plan.frames + frame - time + plan.all_frames - 1
    rows = lax.broadcasted_iota(jnp.int32, (128, plan.keys), 0)
    return jnp.where(rows == index, 1.0, 0.0).astype(F32)


def head_mask(width, head):
    lane = lax.broadcasted_iota(jnp.int32, (1, width), 1)
    inside = (lane >= head * SIZE) & (lane < (head + 1) * SIZE)
    return jnp.where(inside, 1.0, 0.0).astype(F32)


def attend(plan, query, keys, values, table, heads, probs_ref, scalars):
    s, first, second = scalars
    rows, width = query.shape
    places = rows // plan.pooled
    time, counts = key_facts(plan, s, first, second)
    biases = []
    for f in range(plan.frames):
        onehot = offset_onehot(plan, s, time, f)
        bias = jnp.dot(table, onehot, precision=HIGHEST, preferred_element_type=F32)
        biases.append(jnp.where(counts > 0, bias, MASKED))
    total = query.astype(F32)
    for h in range(heads):
        mask = head_mask(width, h)
        scores = mm_tr(query * mask.astype(BF16), keys) * SIZE ** (-0.5)
        bias = jnp.concatenate(
            [jnp.broadcast_to(b[h : h + 1], (plan.cells, plan.keys)) for b in biases] * places, axis=0
        )
        scores = scores + bias
        scores = jnp.exp(scores - jnp.max(scores, axis=-1, keepdims=True))
        probs = scores * (1.0 / jnp.sum(scores, axis=-1, keepdims=True))
        probs = probs.astype(BF16)
        probs_ref[h * rows : (h + 1) * rows] = probs
        total = total + mm(probs, values) * mask
    return total


def attend_back(plan, grad, query, keys, values, probs_ref, heads, bias_ref, table_ref, scalars):
    s, first, second = scalars
    rows, width = query.shape
    places = rows // plan.pooled
    grad_r = grad.astype(BF16)
    grad_query = grad
    grad_keys = jnp.zeros((plan.keys, width), F32)
    grad_values = jnp.zeros((plan.keys, width), F32)
    bias_ref[...] = jnp.zeros(bias_ref.shape, F32)
    for h in range(heads):
        mask = head_mask(width, h)
        mask_r = mask.astype(BF16)
        grad_head = grad_r * mask_r
        query_head = query * mask_r
        probs_r = probs_ref[h * rows : (h + 1) * rows]
        probs = probs_r.astype(F32)
        grad_probs = mm_tr(grad_head, values)
        weighted = probs * grad_probs
        grad_scores = weighted - probs * jnp.sum(weighted, axis=-1, keepdims=True)
        for f in range(plan.frames):
            part = grad_scores[f * plan.cells : (f + 1) * plan.cells]
            for p in range(1, places):
                at = p * plan.pooled + f * plan.cells
                part = part + grad_scores[at : at + plan.cells]
            bias_ref[f, h : h + 1, :] = jnp.sum(part, axis=0, keepdims=True)
        grad_scores_r = grad_scores.astype(BF16)
        grad_query = grad_query + mm(grad_scores_r, keys) * (mask * SIZE ** (-0.5))
        grad_keys = grad_keys + mm_tl(grad_scores_r, query_head)
        grad_values = grad_values + mm_tl(probs_r, grad_head)
    time, _ = key_facts(plan, s, first, second)
    table = jnp.zeros((8, 128), F32)
    for f in range(plan.frames):
        onehot = offset_onehot(plan, s, time, f)
        table = table + lax.dot_general(
            bias_ref[f], onehot, (((1,), (1,)), ((), ())), precision=HIGHEST, preferred_element_type=F32
        )
    table_ref[...] = table
    return grad_query, grad_keys * SIZE ** (-0.5), grad_values


def load_pairs(refs, width):
    pairs = jnp.concatenate([ref[...] for ref in refs], axis=0)
    return pairs[:, :width], pairs[:, width:]


def pool_pair(plan, raw, pool_ref, squeeze_ref, pair_ref):
    width = raw.shape[1] // 2
    for i in range(2):
        pooled = pool(raw[:, i * width : (i + 1) * width], pool_ref[pool_ref.shape[0] - 2 + i])
        pair_ref[: plan.pooled, i * width : (i + 1) * width] = pooled.astype(BF16)
        if plan.local_squeeze:
            weights = squeeze_ref[i]
            for g in range(plan.frames // 4):
                total = None
                for k in range(4):
                    at = (4 * g + k) * plan.cells
                    part = pooled[at : at + plan.cells] * weights[k : k + 1]
                    total = part if total is None else total + part
                at = plan.pooled + g * plan.cells
                pair_ref[at : at + plan.cells, i * width : (i + 1) * width] = total.astype(BF16)


def store_rows(ref, z, start, values):
    each, at = ref.shape[2], 0
    while at < values.shape[0]:
        who, off = divmod(start + at, each)
        n = min(each - off, values.shape[0] - at)
        ref[who, z, off : off + n, :] = values[at : at + n].astype(BF16)
        at += n


def store_columns(ref, tensor, start, values):
    rows = values.shape[0] // tensor
    for z in range(tensor):
        for c in range(values.shape[1] // LANES):
            part = values[z * rows : (z + 1) * rows, c * LANES : (c + 1) * LANES]
            store_rows(ref, z, start + c * rows, part)
    return start + values.shape[1] // LANES * rows


def smooth_max(raw):
    parts = blocks(raw, 4)
    highest = jnp.maximum(jnp.maximum(parts[0], parts[1]), jnp.maximum(parts[2], parts[3]))
    total = jnp.exp(parts[0] - highest)
    for p in range(1, 4):
        total = total + jnp.exp(parts[p] - highest)
    return highest + jnp.log(total) - LOG_FOUR


def smooth_max_back(raw, grad):
    parts = blocks(raw, 4)
    highest = jnp.maximum(jnp.maximum(parts[0], parts[1]), jnp.maximum(parts[2], parts[3]))
    parts = [jnp.exp(part - highest) for part in parts]
    total = parts[0] + parts[1] + parts[2] + parts[3]
    scaled = grad / total
    return jnp.concatenate([part * scaled for part in parts], axis=0)


def call(name, body, outs, vmem, smem=(), scratch=()):
    return pl.pallas_call(
        body,
        out_shape=[jax.ShapeDtypeStruct(shape, dtype) for shape, dtype in outs],
        in_specs=[pl.BlockSpec(memory_space=pltpu.SMEM)] * len(smem)
        + [pl.BlockSpec(memory_space=pltpu.VMEM)] * len(vmem),
        out_specs=[pl.BlockSpec(memory_space=pltpu.VMEM)] * len(outs),
        scratch_shapes=[pltpu.VMEM(shape, dtype) for shape, dtype in scratch],
        name=name,
        interpret=INTERPRET,
        compiler_params=pltpu.CompilerParams(vmem_limit_bytes=56 << 20),
    )(*smem, *vmem)


def enter_body(plan, arrived, order, gain, project, pools, squeeze, x_ref, cot_ref, n_ref, q_ref, pair_ref):
    rows = mm(order[...], arrived[...])
    x = rows[: plan.tokens]
    x_ref[...] = x.astype(BF16)
    width = cot_ref.shape[1] // 2
    cot_ref[:, :width] = rows[plan.tokens : plan.tokens + plan.pooled].astype(BF16)
    cot_ref[:, width:] = rows[plan.tokens + plan.pooled :].astype(BF16)
    n = (norm(x)[0] * gain[...]).astype(BF16)
    n_ref[...] = n
    raw = mm(n, project[...])
    q_ref[...] = raw[:, : x.shape[1]].astype(BF16)
    pool_pair(plan, raw[:, x.shape[1] :], pools, squeeze, pair_ref)


def pick_hidden(core, mine, theirs, expand, reduce, up_ref, down_ref):
    up_ref[0] = expand[...]
    down_ref[0] = reduce[...]

    @pl.when(core == 0)
    def _():
        for k in range(len(mine)):
            up_ref[k + 1] = mine[k][...]
            down_ref[k + 1] = theirs[k][...]

    @pl.when(core != 0)
    def _():
        for k in range(len(mine)):
            up_ref[k + 1] = theirs[k][...]
            down_ref[k + 1] = mine[k][...]


def first_body(plan, heads, resets, videos, *refs):
    refs = list(refs)

    def take(n):
        taken = refs[:n]
        del refs[:n]
        return taken

    x, query = take(2)
    pairs = take(plan.seq)
    memories = take(2)
    table, output, gain, expand, reduce = take(5)
    mine, theirs = take(plan.tensor - 1), take(plan.tensor - 1)
    gain_b, project_b, pool_b, squeeze_b, shortcut_b = take(5)
    or_ref, m_ref, l_ref, y_ref, probs_ref, nb_ref, qb_ref, pairb_ref, base_ref, up_ref, down_ref = refs
    width = x.shape[1]
    scalars = clip_scalars(plan, resets, videos)
    pick_hidden(lax.axis_index("core"), mine, theirs, expand, reduce, up_ref, down_ref)
    keys, values = load_pairs([ref.at[: plan.pooled] for ref in pairs] + memories, width)
    mixed = attend(plan, query[...], keys, values, table[...], heads, probs_ref, scalars)
    mixed_r = mixed.astype(BF16)
    or_ref[...] = mixed_r
    middle = x[...].astype(F32) + mm(mixed_r, output[...])
    m_ref[...] = middle
    l = (norm(middle)[0] * gain[...]).astype(BF16)
    l_ref[...] = l
    y = middle
    for k in range(plan.tensor):
        hidden = gelu(mm(l, up_ref[k])).astype(BF16)
        y = y + mm(hidden, down_ref[k])
    y_ref[...] = y
    n = (norm(y)[0] * gain_b[...]).astype(BF16)
    nb_ref[...] = n
    wide = base_ref.shape[1]
    raw = mm(n, project_b[...])
    qb_ref[...] = pool(raw[:, :wide], pool_b[0]).astype(BF16)
    pool_pair(plan, raw[:, wide:], pool_b, squeeze_b, pairb_ref)
    base_ref[...] = smooth_max(mm(n, shortcut_b[...]))


def second_body(plan, heads, resets, videos, *refs):
    refs = list(refs)
    query = refs.pop(0)
    pairs, refs = refs[: plan.seq], refs[plan.seq :]
    memories, refs = refs[:2], refs[2:]
    table, output, gain, base, cot, or_ref, m_ref, send_ref, probs_ref = refs
    width = query.shape[1]
    scalars = clip_scalars(plan, resets, videos)
    keys, values = load_pairs([ref.at[: plan.pooled] for ref in pairs] + memories, width)
    mixed_r = attend(plan, query[...], keys, values, table[...], heads, probs_ref, scalars).astype(BF16)
    or_ref[...] = mixed_r
    middle = base[...] + mm(mixed_r, output[...])
    m_ref[...] = middle
    send_ref[:, :width] = (norm(middle)[0] * gain[...]).astype(BF16)
    send_ref[:, width:] = cot[...]


def hidden_body(rows, up, down, send_ref, grads_ref):
    width = up.shape[0]
    l = rows[:, :width]
    grad = rows[:, width:]
    gate, slope = gelu_both(mm(l, up[...]))
    hidden = gate.astype(BF16)
    send_ref[:, :width] = mm(hidden, down[...]).astype(BF16)
    grad_pre = (slope * mm_tr(grad, down[...])).astype(BF16)
    send_ref[:, width:] = mm_tr(grad_pre, up[...]).astype(BF16)
    grad_up = mm_tl(l, grad_pre)
    grad_down = mm_tl(hidden, grad)
    at = 0
    for whole in (grad_up, grad_down):
        for c in range(whole.shape[1] // LANES):
            part = whole[:, c * LANES : (c + 1) * LANES]
            grads_ref[at : at + part.shape[0], :] = part.astype(BF16)
            at += part.shape[0]


def second_back_body(plan, heads, resets, videos, *refs):
    refs = list(refs)
    sums, cot, middle, gain, mixed, output, query, probs = refs[:8]
    pairs, refs = refs[8 : 8 + plan.seq], refs[8 + plan.seq :]
    memories, refs = refs[:2], refs[2:]
    out_ref, dm_ref, dgain_ref, doutput_ref, dq_ref, dtable_ref, gown_ref = refs[:7]
    gother, refs = refs[7 : 6 + plan.seq], refs[6 + plan.seq :]
    gm1_ref, gm2_ref, bias_ref = refs
    width = query.shape[1]
    total = sums[0].astype(F32)
    for z in range(1, plan.tensor):
        total = total + sums[z].astype(F32)
    m = middle[...]
    out_ref[...] = (m + total[:, :width]).astype(BF16)
    normed, inverse = norm(m)
    grad, dgain = norm_back(total[:, width:], gain[...], normed, inverse)
    dgain_ref[...] = dgain
    grad = cot[...].astype(F32) + grad
    dm_ref[...] = grad
    store_back(plan, heads, resets, videos, grad, mixed, output, query, probs, pairs, memories,
               doutput_ref, dq_ref, dtable_ref, gown_ref, gother, gm1_ref, gm2_ref, bias_ref)


def store_back(plan, heads, resets, videos, grad, mixed, output, query, probs, pairs, memories,
               doutput_ref, dq_ref, dtable_ref, gown_ref, gother, gm1_ref, gm2_ref, bias_ref):
    width = query.shape[1]
    scalars = clip_scalars(plan, resets, videos)
    grad_r = grad.astype(BF16)
    doutput_ref[...] = mm_tl(mixed[...], grad_r).astype(BF16)
    keys, values = load_pairs([ref.at[: plan.pooled] for ref in pairs] + list(memories), width)
    dq, dk, dv = attend_back(
        plan, mm_tr(grad_r, output[...]), query[...], keys, values, probs, heads, bias_ref, dtable_ref, scalars
    )
    dq_ref[...] = dq
    for i, part in enumerate((dk, dv)):
        lanes = slice(i * width, (i + 1) * width)
        gown_ref[:, lanes] = part[: plan.pooled]
        for o, ref in enumerate(gother):
            at = (o + 1) * plan.pooled
            ref[:, lanes] = part[at : at + plan.pooled].astype(BF16)
        gm1_ref[:, lanes] = part[plan.own : plan.own + plan.memory].astype(BF16)
        gm2_ref[:, lanes] = part[plan.own + plan.memory :].astype(BF16)


def pair_grads(plan, refs):
    own, received = refs[0], refs[1 : plan.seq]
    grad = own[...]
    for ref in received:
        grad = grad + ref[...].astype(F32)
    if not plan.local_squeeze:
        return grad, None
    parts = refs[plan.seq :]
    memory = parts[0][...].astype(F32)
    for ref in parts[1:]:
        memory = memory + ref[...].astype(F32)
    return grad, memory


def unpool(plan, raw, grad, memory, pool_ref, squeeze_ref, dpool_ref, dsqueeze_ref, first):
    width = raw.shape[1] // 2
    result = []
    for i in range(2):
        weights = pool_ref[first + i]
        lanes = slice(i * width, (i + 1) * width)
        part = grad[:, lanes]
        source = raw[:, lanes]
        if plan.local_squeeze:
            pooled = pool(source, weights)
            ws = squeeze_ref[i]
            pieces = []
            sums = [None] * 4
            for g in range(plan.frames // 4):
                dm = memory[g * plan.cells : (g + 1) * plan.cells, lanes]
                for k in range(4):
                    at = (4 * g + k) * plan.cells
                    pieces.append(part[at : at + plan.cells] + dm * ws[k : k + 1])
                    total = jnp.sum(dm * pooled[at : at + plan.cells], axis=0, keepdims=True)
                    sums[k] = total if sums[k] is None else sums[k] + total
            part = jnp.concatenate(pieces, axis=0)
            for k in range(4):
                dsqueeze_ref[i, k : k + 1, :] = sums[k]
        result.append(unpool_one(source, part, weights, dpool_ref, first + i))
    return result


def unpool_one(source, part, weights, dpool_ref, place):
    pieces = []
    for p, piece in enumerate(blocks(source, 4)):
        dpool_ref[place, p : p + 1, :] = jnp.sum(part * piece, axis=0, keepdims=True)
        pieces.append((part * weights[p : p + 1]).astype(BF16))
    return jnp.concatenate(pieces, axis=0)


def middle_back_body(plan, heads, resets, videos, *refs):
    refs = list(refs)

    def take(n):
        taken = refs[:n]
        del refs[:n]
        return taken

    pieces = 2 * plan.seq if plan.local_squeeze else plan.seq
    grads = take(pieces)
    dq, dm, doutput_b, n_ref, y_ref, gain_b, project_b, pool_b, squeeze_b, shortcut_b = take(10)
    m_ref, l_ref, gain, mixed, output, query, probs, expand, reduce = take(9)
    mine, theirs = take(plan.tensor - 1), take(plan.tensor - 1)
    pairs, memories = take(plan.seq), take(2)
    big_ref, dpool_ref, dsqueeze_ref, dgainb_ref, dgain_ref, dm_out, doutput_ref, dq_ref, dtable_ref = take(9)
    gown_ref = take(1)[0]
    gother = take(plan.seq - 1)
    gm1_ref, gm2_ref, up_ref, down_ref, bias_ref = refs
    tensor = plan.tensor
    pick_hidden(lax.axis_index("core"), mine, theirs, expand, reduce, up_ref, down_ref)
    wide = dm.shape[1]
    n = n_ref[...]
    grad, memory = pair_grads(plan, grads)
    at = 0
    grad_n = None
    raw = mm(n, project_b[...])
    parts = [unpool_one(raw[:, :wide], dq[...], pool_b[0], dpool_ref, 0)]
    parts += unpool(plan, raw[:, wide:], grad, memory, pool_b, squeeze_b, dpool_ref, dsqueeze_ref, 1)
    for i, part in enumerate(parts):
        at = store_columns(big_ref, tensor, at, mm_tl(n, part))
        back = mm_tr(part, project_b[:, i * wide : (i + 1) * wide])
        grad_n = back if grad_n is None else grad_n + back
    grad_z = smooth_max_back(mm(n, shortcut_b[...]), dm[...]).astype(BF16)
    at = store_columns(big_ref, tensor, at, mm_tl(n, grad_z))
    at = store_columns(big_ref, tensor, at, doutput_b[...])
    grad_n = grad_n + mm_tr(grad_z, shortcut_b[...])
    normed, inverse = norm(y_ref[...])
    grad_y, dgain = norm_back(grad_n, gain_b[...], normed, inverse)
    dgainb_ref[...] = dgain
    grad_r = grad_y.astype(BF16)
    l = l_ref[...]
    t = lax.axis_index("tensor")
    grad_l = None
    for k in range(tensor):
        gate, slope = gelu_both(mm(l, up_ref[k]))
        hidden = gate.astype(BF16)
        grad_pre = (slope * mm_tr(grad_r, down_ref[k])).astype(BF16)
        z = t ^ k
        store_rows(big_ref, z, at, mm_tl(l, grad_pre))
        store_rows(big_ref, z, at + l.shape[1], mm_tl(hidden, grad_r))
        back = mm_tr(grad_pre, up_ref[k])
        grad_l = back if grad_l is None else grad_l + back
    normed, inverse = norm(m_ref[...])
    grad, dgain = norm_back(grad_l, gain[...], normed, inverse)
    dgain_ref[...] = dgain
    grad = grad_y + grad
    dm_out[...] = grad
    store_back(plan, heads, resets, videos, grad, mixed, output, query, probs, pairs, memories,
               doutput_ref, dq_ref, dtable_ref, gown_ref, gother, gm1_ref, gm2_ref, bias_ref)


def leave_body(plan, *refs):
    refs = list(refs)
    pieces = 2 * plan.seq if plan.local_squeeze else plan.seq
    grads, refs = refs[:pieces], refs[pieces:]
    (dq, dm, doutput, n_ref, x_ref, gain, project, pools, squeeze, order, out,
     dgain_mid, dtable, dgain_b, dpool_b, dsqueeze_b, dmid_b, dtable_b) = refs[:18]
    refs = refs[18:]
    given = refs.pop(0) if not plan.local_squeeze else None
    send_ref, tail_ref, small_ref, dpool_ref, dsqueeze_ref, sum_ref = refs
    width = x_ref.shape[1]
    n = n_ref[...]
    grad, memory = pair_grads(plan, grads)
    raw = mm(n, project[:, width:])
    parts = [dq[...].astype(BF16)]
    parts += unpool(plan, raw, grad, memory, pools, squeeze, dpool_ref, dsqueeze_ref, 0)
    at = 0
    grad_n = None
    for i, part in enumerate(parts):
        at = store_columns(tail_ref, plan.tensor, at, mm_tl(n, part))
        back = mm_tr(part, project[:, i * width : (i + 1) * width])
        grad_n = back if grad_n is None else grad_n + back
    store_columns(tail_ref, plan.tensor, at, doutput[...])
    normed, inverse = norm(x_ref[...].astype(F32))
    grad_x, dgain = norm_back(grad_n, gain[...], normed, inverse)
    grad_x = (grad_x + dm[...]).astype(BF16)
    leaving = jnp.concatenate([grad_x, out[:, :width], out[:, width:]], axis=0)
    send_ref[...] = mm_tl(order[...], leaving).astype(BF16)
    sum_ref[...] = jnp.zeros(sum_ref.shape, F32)
    squeeze_a = dsqueeze_ref if given is None else given
    sum_ref[0:1, :] = dgain
    sum_ref[1:2, :] = dgain_mid[...]
    sum_ref[2:3, :] = dgain_b[...]
    for i in range(2):
        half = slice(i * width, (i + 1) * width)
        sum_ref[3 + i : 4 + i, :] = dmid_b[:, half]
        sum_ref[8 + 4 * i : 12 + 4 * i, :] = dpool_ref[i]
        sum_ref[16 + 4 * i : 20 + 4 * i, :] = squeeze_a[i]
        for j in range(3):
            sum_ref[24 + 16 * i + 4 * j : 28 + 16 * i + 4 * j, :] = dpool_b[j, :, half]
        for j in range(2):
            sum_ref[56 + 8 * i + 4 * j : 60 + 8 * i + 4 * j, :] = dsqueeze_b[j, :, half]
    sum_ref[72:80, :128] = dtable[...]
    sum_ref[80:88, :128] = dtable_b[...]
    store_rows(small_ref, 0, 0, sum_ref[...])


def all_pairs(axis, by):
    n = lax.axis_size(axis)
    return [(i, i ^ by) for i in range(n)]


def shift(values, by):
    chips, cores = lax.axis_size("chip"), lax.axis_size("core")
    seq, tensor = lax.axis_size("seq"), lax.axis_size("tensor")
    clips = chips * cores * tensor
    pairs = []
    for g in range(clips):
        if 0 <= g + by < clips:
            for s in range(seq):
                source = (g // tensor * seq + s) * tensor + g % tensor
                target = ((g + by) // tensor * seq + s) * tensor + (g + by) % tensor
                pairs.append((source, target))
    return lax.ppermute(values, EVERY, pairs)


def relative_weights(plan, squeeze):
    s = lax.axis_index("seq")
    order = jnp.arange(plan.all_frames)
    frame = ((s ^ (order // plan.frames)) * plan.frames + order % plan.frames) % 4
    pair = jnp.concatenate([squeeze[0], squeeze[1]], axis=-1)
    return pair[frame], frame


def share_pairs(plan, pair, squeeze):
    pairs = [pair] + [lax.ppermute(pair, "seq", all_pairs("seq", o)) for o in range(1, plan.seq)]
    if plan.local_squeeze:
        memory = jnp.concatenate([each[plan.pooled :] for each in pairs], axis=0)
    else:
        memory = squeeze_all(plan, pairs, squeeze)
    return pairs, (shift(memory, 1), shift(memory, 2))


def by_frame(plan, pairs):
    together = jnp.concatenate(pairs, axis=0).astype(F32)
    return together.reshape(plan.all_frames // 4, 4, plan.cells, -1)


def squeeze_all(plan, pairs, squeeze):
    weights = relative_weights(plan, squeeze)[0].reshape(plan.all_frames // 4, 4, 1, -1)
    total = jnp.sum(by_frame(plan, pairs) * weights, axis=1)
    return total.reshape(plan.memory, -1).astype(BF16)


def return_pairs(plan, grads, pairs, squeeze):
    own, others, first, second = grads
    memory = shift(first, -1).astype(F32) + shift(second, -2).astype(F32)
    if plan.local_squeeze:
        received = [lax.ppermute(each, "seq", all_pairs("seq", o + 1)) for o, each in enumerate(others)]
        parts = jnp.split(memory, plan.seq, axis=0)
        moved = [
            lax.ppermute(each.astype(BF16), "seq", all_pairs("seq", o + 1)) for o, each in enumerate(parts[1:])
        ]
        return [own] + received + [parts[0]] + moved, None
    weights, frame = relative_weights(plan, squeeze)
    weights = weights.reshape(plan.all_frames // 4, 4, 1, -1)
    memory = memory.reshape(plan.all_frames // 4, 1, plan.cells, -1)
    both = by_frame(plan, [own] + [each.astype(F32) for each in others]) + memory * weights
    both = jnp.split(both.reshape(plan.own, -1), plan.seq, axis=0)
    sums = jnp.sum(by_frame(plan, pairs) * memory, axis=2).reshape(plan.all_frames, -1)
    onehot = (frame[None, :] == jnp.arange(4)[:, None]).astype(F32)
    sums = jnp.dot(onehot, sums, precision=HIGHEST)
    width = sums.shape[1] // 2
    received = [
        lax.ppermute(each.astype(BF16), "seq", all_pairs("seq", o + 1)) for o, each in enumerate(both[1:])
    ]
    return [both[0]] + received, jnp.stack([sums[:, :width], sums[:, width:]])


def sum_first(values):
    return jnp.sum(values.astype(F32), axis=0).astype(BF16)


def spread(values, axes):
    return lax.all_to_all(values, axes, 0, 0, tiled=True)


def gather_plane(values):
    plane = lax.axis_size(PLANE)
    return spread(jnp.broadcast_to(values[None], (plane,) + values.shape), PLANE)


def padded(rows, parts):
    return -(-rows // (16 * parts)) * 16


def local(
    clips_in, cotangent, resets, videos,
    attend_gain_a, project_a, pooling_a, squeeze_a, offsets_a, output_a, mixer_gain_a, expand_a, reduce_a,
    attend_gain_b, project_b, pooling_b, squeeze_b, offsets_b, output_b, shortcut_b, mixer_gain_b, expand_b, reduce_b,
):
    seq, tensor, plane = lax.axis_size("seq"), lax.axis_size("tensor"), lax.axis_size(PLANE)
    plan = Plan(seq, tensor, clips_in.shape)
    width, wide = clips_in.shape[-1], cotangent.shape[-1]
    heads_a, heads_b = offsets_a.shape[0], offsets_b.shape[0]
    core = lax.axis_index("core")
    tokens, pooled, keys, memory = plan.tokens, plan.pooled, plan.keys, plan.memory
    half = jnp.where(core == 0, expand_a, reduce_a)
    mine = [lax.ppermute(half, "tensor", all_pairs("tensor", k)) for k in range(1, tensor)]
    theirs = [lax.ppermute(each, "core", all_pairs("core", 1)) for each in mine]

    order = jnp.asarray(plan.arrange(), BF16)
    home = ("tensor", "seq")
    leaving = jnp.concatenate(
        [clips_in.reshape(plan.group, -1, width), cotangent.reshape(plan.group, -1, width)], axis=1
    )
    arrived = spread(leaving, home).reshape(-1, width)
    row = lambda gain: gain.reshape(1, -1)
    table = lambda offsets: jnp.pad(offsets, ((0, 8 - offsets.shape[0]), (0, 128 - offsets.shape[1])))
    table_a, table_b = table(offsets_a), table(offsets_b)
    pair_rows = pooled + (plan.frames // 4 * plan.cells if plan.local_squeeze else 0)
    x, cot, n_a, q_a, pair_a = call(
        "enter",
        functools.partial(enter_body, plan),
        [((tokens, width), BF16), ((pooled, wide), BF16), ((tokens, width), BF16), ((tokens, width), BF16),
         ((pair_rows, 2 * width), BF16)],
        [arrived, order, row(attend_gain_a), project_a, pooling_a, squeeze_a],
    )
    pairs_a, memories_a = share_pairs(plan, pair_a, squeeze_a)
    hidden = [((tensor, width, expand_a.shape[1]), BF16), ((tensor, reduce_a.shape[0], width), BF16)]
    or_a, m_a, l_a, y_a, probs_a, n_b, q_b, pair_b, base = call(
        "first",
        functools.partial(first_body, plan, heads_a),
        [((tokens, width), BF16), ((tokens, width), F32), ((tokens, width), BF16), ((tokens, width), F32),
         ((heads_a * tokens, keys), BF16), ((tokens, width), BF16), ((pooled, wide), BF16),
         ((pair_rows, 2 * wide), BF16), ((pooled, wide), F32)],
        [x, q_a, *pairs_a, *memories_a, table_a, output_a, row(mixer_gain_a), expand_a, reduce_a, *mine, *theirs,
         row(attend_gain_b), project_b, pooling_b, squeeze_b, shortcut_b],
        [resets, videos],
        hidden,
    )
    pairs_b, memories_b = share_pairs(plan, pair_b, squeeze_b)
    or_b, m_b, rows_b, probs_b = call(
        "second",
        functools.partial(second_body, plan, heads_b),
        [((pooled, wide), BF16), ((pooled, wide), F32), ((pooled, 2 * wide), BF16),
         ((heads_b * pooled, keys), BF16)],
        [q_b, *pairs_b, *memories_b, table_b, output_b, row(mixer_gain_b), base, cot],
        [resets, videos],
    )
    rows_all = lax.all_gather(rows_b, "tensor", axis=0, tiled=True)
    hidden_rows = (expand_b.shape[1] // LANES) * wide + (wide // LANES) * reduce_b.shape[0]
    shares, grads_0 = call(
        "hidden",
        hidden_body,
        [((tensor * pooled, 2 * wide), BF16), ((hidden_rows, LANES), BF16)],
        [rows_all, expand_b, reduce_b],
    )
    sums = spread(shares, "tensor").reshape(tensor, pooled, 2 * wide)
    bias = lambda: [((plan.frames, 8, keys), F32)]
    key_grads = lambda w: (
        [((pooled, 2 * w), F32)] + [((pooled, 2 * w), BF16)] * (seq - 1) + [((memory, 2 * w), BF16)] * 2
    )
    out, dm_b, dmid_b, doutput_b, dq_b, dtable_b, *back = call(
        "second_back",
        functools.partial(second_back_body, plan, heads_b),
        [((pooled, wide), BF16), ((pooled, wide), F32), ((1, wide), F32), ((wide, wide), BF16), ((pooled, wide), F32),
         ((8, 128), F32), *key_grads(wide)],
        [sums, cot, m_b, row(mixer_gain_b), or_b, output_b, q_b, probs_b, *pairs_b, *memories_b],
        [resets, videos],
        bias(),
    )
    pieces, dsqueeze_given = return_pairs(plan, (back[0], back[1:seq], back[-2], back[-1]), pairs_b, squeeze_b)
    big_rows = padded((3 + 1) * wide // LANES * (width // tensor) + wide // LANES * (wide // tensor) + 2 * width, plane)
    big, dpool_b, dsqueeze_b, dgain_b, dmid_a, dm_a, doutput_a, dq_a, dtable_a, *back = call(
        "middle_back",
        functools.partial(middle_back_body, plan, heads_a),
        [((plane, tensor, big_rows, LANES), BF16), ((3, 4, wide), F32), ((2, 4, wide), F32), ((1, width), F32),
         ((1, width), F32), ((tokens, width), F32), ((width, width), BF16), ((tokens, width), F32), ((8, 128), F32),
         *key_grads(width)],
        [*pieces, dq_b, dm_b, doutput_b, n_b, y_a, row(attend_gain_b), project_b, pooling_b, squeeze_b, shortcut_b,
         m_a, l_a, row(mixer_gain_a), or_a, output_a, q_a, probs_a, expand_a, reduce_a, *mine, *theirs,
         *pairs_a, *memories_a],
        [resets, videos],
        hidden + bias(),
    )
    if dsqueeze_given is not None:
        dsqueeze_b = dsqueeze_given
    pieces, dsqueeze_given = return_pairs(plan, (back[0], back[1:seq], back[-2], back[-1]), pairs_a, squeeze_a)
    tail_rows, small_rows = padded(4 * (width // tensor), plane), padded(128, plane)
    leaving, tail, small = call(
        "leave",
        functools.partial(leave_body, plan),
        [(arrived.shape, BF16), ((plane, tensor, tail_rows, LANES), BF16), ((plane, 1, small_rows, LANES), BF16)],
        [*pieces, dq_a, dm_a, doutput_a, n_a, x, row(attend_gain_a), project_a, pooling_a, squeeze_a, order, out,
         dmid_a, dtable_a, dgain_b, dpool_b, dsqueeze_b, dmid_b, dtable_b]
        + ([] if dsqueeze_given is None else [dsqueeze_given]),
        (),
        [((2, 4, width), F32), ((2, 4, width), F32), ((128, LANES), F32)],
    )
    returned = spread(leaving.reshape(plan.group, -1, width), home)
    x_rows = plan.frames * plan.rows * plan.cols
    grad_input = returned[:, :x_rows].reshape(clips_in.shape).astype(F32)
    result = returned[:, x_rows:].reshape(cotangent.shape).astype(F32)

    hidden_each = padded(hidden_rows, plane)
    assert hidden_each * plane == hidden_rows
    grads_0 = sum_first(spread(grads_0.reshape(plane, hidden_each, LANES), PLANE))
    big = sum_first(spread(sum_first(spread(big, PLANE)), "tensor"))
    tail = jnp.concatenate(
        [tail.reshape(plane, tensor * tail_rows, LANES), small.reshape(plane, small_rows, LANES)], axis=1
    )
    tail = sum_first(spread(tail, PLANE))
    small = jnp.broadcast_to(tail[None, tensor * tail_rows :], (tensor, small_rows, LANES))
    tail = jnp.concatenate([tail[: tensor * tail_rows].reshape(tensor, tail_rows, LANES), small], axis=1)
    tail = sum_first(spread(tail.reshape(tensor, -1, LANES), "tensor").reshape(tensor, -1, LANES))
    whole = gather_plane(jnp.concatenate([grads_0, big, tail], axis=0)).astype(F32)
    at = 0
    groups = []
    for rows in (hidden_each, big_rows, tail_rows, small_rows):
        groups.append(whole[:, at : at + rows].reshape(plane * rows, LANES))
        at += rows
    hidden_g, big_g, tail_g, small_g = groups

    def columns(group, start, rows, count):
        part = group[start : start + rows * count].reshape(count, rows, LANES)
        return part.transpose(1, 0, 2).reshape(rows, count * LANES), start + rows * count

    grad_expand_b, at = columns(hidden_g, 0, wide, expand_b.shape[1] // LANES)
    grad_reduce_b, at = columns(hidden_g, at, reduce_b.shape[0], wide // LANES)
    share = width // tensor
    grad_project_b, at = columns(big_g, 0, share, 3 * wide // LANES)
    grad_shortcut_b, at = columns(big_g, at, share, wide // LANES)
    grad_output_b, at = columns(big_g, at, wide // tensor, wide // LANES)
    grad_expand_a, at = columns(big_g, at, width, 1)
    grad_reduce_a, at = columns(big_g, at, width, 1)
    grad_project_a, at = columns(tail_g, 0, share, 3)
    grad_output_a, at = columns(tail_g, at, share, 1)
    halves = lambda a, b, n: jnp.concatenate([small_g[a : a + n], small_g[b : b + n]], axis=1)
    entries = offsets_a.shape[1]
    return (
        result,
        grad_input,
        small_g[0],
        grad_project_a,
        small_g[8:16].reshape(2, 4, width),
        small_g[16:24].reshape(2, 4, width),
        small_g[72 : 72 + heads_a, :entries],
        grad_output_a,
        small_g[1],
        grad_expand_a,
        grad_reduce_a,
        small_g[2],
        grad_project_b,
        halves(24, 40, 12).reshape(3, 4, wide),
        halves(56, 64, 8).reshape(2, 4, wide),
        small_g[80 : 80 + heads_b, :entries],
        grad_output_b,
        grad_shortcut_b,
        halves(3, 4, 1).reshape(wide),
        grad_expand_b,
        grad_reduce_b,
    )


def solution(mesh):
    clip, seq, tensor = mesh.devices.shape
    split = Mesh(mesh.devices.reshape(clip // 2, 2, seq, tensor), EVERY)
    clips = ("chip", "core")
    field = P(clips, None, "seq", "tensor", None)
    up, down = P(None, "tensor"), P("tensor", None)
    block = (P(), P(), P(), P(), P(), P(), P(), up, down)
    block_b = (P(), P(), P(), P(), P(), P(), P(), P(), up, down)
    grads = (P(), down, P(), P(), P(), down, P(), up, down)
    grads_b = (P(), down, P(), P(), P(), down, down, P(), up, down)
    return jax.shard_map(
        local,
        mesh=split,
        in_specs=(field, field, P(), P()) + block + block_b,
        out_specs=(field, field) + grads + grads_b,
        check_vma=False,
    )
```

time: 1500 us -> 447 us (0.30)
  waiting for transfers between devices: 793 us -> 185 us
  local copies, waits for them, and re-layouts: 278 us -> 44 us
  blocking collectives: 210 us -> 87.7 us
  matrix products: 85.4 us -> 0 us
  other arithmetic: 80.8 us -> 14.9 us
  Pallas kernels: 0 us -> 53.6 us
  starting transfers between devices: 17.4 us -> 58.8 us
  between operations: 18.3 us -> 1.13 us
    all_gather x8 -> x0, waiting for transfers between devices: 296 us -> none  [gather_keys(): return lax.all_gather(block, ('seq', 'tensor'), axis=1, tiled=True)]
    reduce_scatter x10 -> x0, waiting for transfers between devices: 156 us -> none  [the longest x1 38.2 us: local(): lax.psum_scatter(grads_b[1].astype(jnp.bfloat16), 'tensor', scatter_dimen...]
    while x10 -> x0, waiting for transfers between devices: 155 us -> none
    psum x2 -> x0, waiting for transfers between devices: 142 us -> none  [the longest x1 106 us: local(): lax.psum((grads_a[8], grads_a[9], grads_b[8], grads_b[9], shares[0], shar...]
    all_to_all x0 -> x6, waiting for transfers between devices: none -> 120 us  [spread(): return lax.all_to_all(values, axes, 0, 0, tiled=True)]
    psum x1 -> x0, blocking collectives: 98.1 us -> none  [local(): lax.psum((grads_a[8], grads_a[9], grads_b[8], grads_b[9], shares[0], shar...]
    all_gather x6 -> x1, blocking collectives: 112 us -> 20.7 us  [local(): rows_all = lax.all_gather(rows_b, 'tensor', axis=0, tiled=True)]
    dot_general x63 -> x0, matrix products: 85.4 us -> none  [the longest x9 18 us: inner_left(): lax.dot_general(left, right, (((0,), (0,)), ((), ())), preferred_element_...]
  transfers between devices with their start and end apart: 29 -> 26, of which waited for: 22 -> 16; matrix products, arithmetic and copies ran while one was open for 15% -> 5% of each run, Pallas kernels for 0% -> 7%
where the time goes in v1:
time: 447 us; the launch traced here: 445 us
  waiting for transfers between devices  185 us (41%)
  blocking collectives  87.7 us (20%)
  starting transfers between devices  58.8 us (13%)
  Pallas kernels  53.6 us (12%)
  local copies, waits for them, and re-layouts  44 us (10%)
  other arithmetic  14.9 us (3%)
    all_to_all x6, waiting for transfers between devices, spread(): return lax.all_to_all(values, axes, 0, 0, tiled=True)  120 us
    all_to_all x3, blocking collectives, spread(): return lax.all_to_all(values, axes, 0, 0, tiled=True)  67 us
    pallas_call x7, Pallas kernels, call(): pl.pallas_call(body, out_shape=[jax.ShapeDtypeStruct(shape, dtype) for sh...  53.6 us
    ppermute x3, waiting for transfers between devices, local(): lax.ppermute(half, 'tensor', all_pairs('tensor', k))  29.4 us
    all_to_all x6, starting transfers between devices, spread(): return lax.all_to_all(values, axes, 0, 0, tiled=True)  28 us
    all_gather x1, blocking collectives, local(): rows_all = lax.all_gather(rows_b, 'tensor', axis=0, tiled=True)  20.7 us
    ppermute x8, starting transfers between devices, shift(): return lax.ppermute(values, EVERY, pairs)  16.1 us
    ppermute x2, waiting for transfers between devices, return_pairs(): lax.ppermute(each.astype(BF16), 'seq', all_pairs('seq', o + 1))  13.8 us
  transfers between devices with their start and end apart: 26, of which 16 were waited for; matrix products, arithmetic and copies ran while one was open for 5% of the time, Pallas kernels for 7%

profile of v1, /device:TPU:0, one launch (start us, length us, event | category | flops | bytes accessed | tf_op | source)
XLA Modules:
  0.0 445.0 jit_solution(2555447375349258597)
XLA Ops:
  3.4 7.3 %all-to-all-start = ((bf16[8,48,384]{2,1,0:T(8,128)(2,1)}), bf16[8,48,384]{2,1,0:T(8,128)(2,1)S(1)}, u32[]{:S(2)}, u32[]{:S(2)}) async-start(bf16[8,48,384]{2,1,0:T(8,128)(2,1)} %pad_maximum_fusion.2), calls=%async_computation | async-start | bytes 589824 | tf_op jit(solution)/shard_map/all_to_all | solution.py:680
  11.7 3.9 collective-permute-start.5
  16.3 11.1 %collective-permute-done.5.refs_13_.refs_25_ = bf16[384,384]{1,0:T(8,128)(2,1)S(1)} collective-permute-done((bf16[384,384]{1,0:T(8,128)(2,1)S(1)}, bf16[384,384]{1,0:T(8,128)(2,1)S(1)}, u32[]{:S(2)}, u32[]{:S(2)}) %collective-permute-start.5) | collective-permute-done | bytes 294944 | tf_op jit(solution)/shard_map/ppermute | solution.py:704
  27.3 18.3 %collective-permute-done.4.refs_12_.refs_24_ = bf16[384,384]{1,0:T(8,128)(2,1)S(1)} collective-permute-done((bf16[384,384]{1,0:T(8,128)(2,1)S(1)}, bf16[384,384]{1,0:T(8,128)(2,1)S(1)}, u32[]{:S(2)}, u32[]{:S(2)}) %collective-permute-start.4) | collective-permute-done | bytes 294944 | tf_op jit(solution)/shard_map/ppermute | solution.py:704
  52.6 3.3 collective-permute-done.refs_3_.refs_30_
  57.4 4.1 collective-permute-start.1
  64.1 8.7 %first.1 = (bf16[256,384]{1,0:T(8,128)(2,1)}, f32[256,384]{1,0:T(8,128)}, bf16[256,384]{1,0:T(8,128)(2,1)}, f32[256,384]{1,0:T(8,128)}, bf16[1024,192]{1,0:T(8,1...) custom-call(s32[16]{0:T(128)} %resets.7, ...), custom_call_target="tpu_custom_call" | custom-call | tf_op jit(solution)/shard_map/first/pallas_call | solution.py:283
  75.5 6.2 %collective-permute-done.9.refs_2_.refs_9_ = bf16[80,1536]{1,0:T(8,128)(2,1)S(1)} collective-permute-done((bf16[80,1536]{1,0:T(8,128)(2,1)}, bf16[80,1536]{1,0:T(8,128)(2,1)S(1)}, u32[]{:S(2)}, u32[]{:S(2)}) %collective-permute-start.9) | collective-permute-done | bytes 245792 | tf_op jit(solution)/shard_map/ppermute | solution.py:631
  81.7 4.1 collective-permute-start.11
  90.9 7.3 %second.1 = (bf16[64,768]{1,0:T(8,128)(2,1)}, f32[64,768]{1,0:T(8,128)}, bf16[64,1536]{1,0:T(8,128)(2,1)}, bf16[512,192]{1,0:T(8,128)(2,1)}) custom-call(s32[16]{0:T(128)} %resets.7, s32[16]{0:T(128)} %videos.7, bf16[64,768]{1,0:T(8,128)(2,1)} %get-tuple-element.70.refs_0_.refs_6_, bf16[80,1536]{1,0:T(8,128)(2,1)} %get-tuple-element.71.refs_1_.refs_8_, ...), custom_call_target="tpu_custom_call" | custom-call | tf_op jit(solution)/shard_map/second/pallas_call | solution.py:283
  98.2 20.7 %all_gather.3.rows = bf16[256,1536]{1,0:T(8,128)(2,1)} all-gather(bf16[64,1536]{1,0:T(8,128)(2,1)} %get-tuple-element.74), channel_id=1, replica_groups=mesh['chip'=2,'core'=2,'seq'=2,'tensor'=4] {'tensor'}, dimensions={0}, use_global_device_ids=true | all-gather | bytes 983040 | tf_op jit(solution)/shard_map/all_gather | solution.py:746
  118.9 5.4 %hidden.1 = (bf16[256,1536]{1,0:T(8,128)(2,1)}, bf16[3072,384]{1,0:T(8,128)(2,1)}) custom-call(bf16[256,1536]{1,0:T(8,128)(2,1)} %all_gather.3.rows, bf16[768,768]{1,0:T(8,128)(2,1)} %up.1, bf16[768,768]{1,0:T(8,128)(2,1)} %down.1), custom_call_target="tpu_custom_call" | custom-call | tf_op jit(solution)/shard_map/hidden/pallas_call | solution.py:283
  124.4 24.1 %all_to_all.49.refs_0_ = bf16[4,64,1536]{2,1,0:T(8,128)(2,1)} all-to-all(bf16[4,64,1536]{2,1,0:T(8,128)(2,1)} %bitcast.54), channel_id=1, replica_groups=mesh['chip'=2,'core'=2,'seq'=2,'tensor'=4] {'tensor'}, dimensions={0} | all-to-all | bytes 1572864 | tf_op jit(solution)/shard_map/all_to_all | solution.py:680
  148.5 3.8 all-to-all-start.3
  152.3 9.2 %second_back.1 = (bf16[64,768]{1,0:T(8,128)(2,1)}, f32[64,768]{1,0:T(8,128)}, f32[1,768]{1,0:T(1,128)}, bf16[768,768]{1,0:T(8,128)(2,1)}, f32[64,768]{1,0:T(8,12...) custom-call(s32[16]{0:T(128)} %resets.7, ...), custom_call_target="tpu_custom_call" | custom-call | tf_op jit(solution)/shard_map/second_back/pallas_call | solution.py:283
  170.4 4.0 collective-permute-start.15
  175.1 10.6 %collective-permute-done.15.refs_3_ = bf16[16,1536]{1,0:T(8,128)(2,1)S(1)} collective-permute-done((bf16[16,1536]{1,0:T(8,128)(2,1)S(1)}, bf16[16,1536]{1,0:T(8,128)(2,1)S(1)}, u32[]{:S(2)}, u32[]{:S(2)}) %collective-permute-start.15) | collective-permute-done | bytes 49184 | tf_op jit(solution)/shard_map/ppermute | solution.py:657
  186.4 15.4 %middle_back.1 = (bf16[8,4,240,384]{3,2,1,0:T(8,128)(2,1)}, f32[3,4,768]{2,1,0:T(4,128)}, f32[2,4,768]{2,1,0:T(4,128)}, f32[1,384]{1,0:T(1,128)}, f32[1,384]{1,0...) custom-call(s32[16]{0:T(128)} %resets.7, ...), custom_call_target="tpu_custom_call" | custom-call | tf_op jit(solution)/shard_map/middle_back/pallas_call | solution.py:283
  211.5 3.2 collective-permute-done.19.refs_3_
  215.3 4.7 %leave.1 = (bf16[384,384]{1,0:T(8,128)(2,1)}, bf16[8,4,48,384]{3,2,1,0:T(8,128)(2,1)}, bf16[8,1,16,384]{3,2,1,0:T(8,128)(2,1)}) custom-call(f32[64,768]{1,0:T(8,128)} %get-tuple-element.92.refs_0_, bf16[64,768]{1,0:T(8,128)(2,1)} %copy-done.14, f32[16,768]{1,0:T(8,128)} %split.20.refs_2_, bf16[16,768]{1,0:T(8,128)(2,1)} %copy-done.16, ...), custom_call_target="tpu_custom_call" | custom-call | tf_op jit(solution)/shard_map/leave/pallas_call | solution.py:283
  222.5 21.7 %all_to_all.50 = bf16[8,208,384]{2,1,0:T(8,128)(2,1)} all-to-all(bf16[8,208,384]{2,1,0:T(8,128)(2,1)} %pad_maximum_fusion), channel_id=1, replica_groups=mesh['chip'=2,'core'=2,'seq'=2,'tensor'=4] {'chip','core','seq'}, dimensions={0} | all-to-all | bytes 2555904 | tf_op jit(solution)/shard_map/all_to_all | solution.py:680
  244.2 4.7 %all-to-all-start.4 = ((bf16[8,4,240,384]{3,2,1,0:T(8,128)(2,1)}), bf16[8,4,240,384]{3,2,1,0:T(8,128)(2,1)}, u32[]{:S(2)}, u32[]{:S(2)}) async-start(bf16[8,4,240,384]{3,2,1,0:T(8,128)(2,1)} %get-tuple-element.110), calls=%async_computation.4 | async-start | bytes 11796480 | tf_op jit(solution)/shard_map/all_to_all | solution.py:680
  251.2 64.2 %all-to-all-done.4 = bf16[8,4,240,384]{3,2,1,0:T(8,128)(2,1)} async-done(((bf16[8,4,240,384]{3,2,1,0:T(8,128)(2,1)}), bf16[8,4,240,384]{3,2,1,0:T(8,128)(2,1)}, u32[]{:S(2)}, u32[]{:S(2)}) %all-to-all-start.4) | async-done | bytes 5898272 | tf_op jit(solution)/shard_map/all_to_all | solution.py:680
  315.4 4.0 all-to-all-start.7
  319.4 4.5 %reduce_sum.61 = bf16[4,240,384]{2,1,0:T(8,128)(2,1)} reduce(bf16[8,4,240,384]{3,2,1,0:T(8,128)(2,1)} %all-to-all-done.4, bf16[]{:T(256)} %constant.18.clone.1), dimensions={0}, to_apply=%region_1.2 | reduce | flops 2580480 | bytes 6635522 | tf_op jit(solution)/shard_map/reduce_sum | solution.py:676
  324.0 3.4 all-to-all-done.7
  327.4 21.2 %all_to_all.51 = bf16[4,240,384]{2,1,0:T(8,128)(2,1)S(1)} all-to-all(bf16[4,240,384]{2,1,0:T(8,128)(2,1)} %reduce_sum.61), channel_id=1, replica_groups=mesh['chip'=2,'core'=2,'seq'=2,'tensor'=4] {'tensor'}, dimensions={0} | all-to-all | bytes 1474560 | tf_op jit(solution)/shard_map/all_to_all | solution.py:680
  348.6 3.6 all-to-all-start.2
  355.5 5.2 %all-to-all-done.2 = bf16[8,48,384]{2,1,0:T(8,128)(2,1)S(1)} async-done(((bf16[8,48,384]{2,1,0:T(8,128)(2,1)}), bf16[8,48,384]{2,1,0:T(8,128)(2,1)S(1)}, u32[]{:S(2)}, u32[]{:S(2)}) %all-to-all-start.2) | async-done | bytes 294944 | tf_op jit(solution)/shard_map/all_to_all | solution.py:680
  363.1 4.6 %all-to-all-start.8 = ((bf16[8,688,384]{2,1,0:T(8,128)(2,1)}), bf16[8,688,384]{2,1,0:T(8,128)(2,1)}, u32[]{:S(2)}, u32[]{:S(2)}) async-start(bf16[8,688,384]{2,1,0:T(8,128)(2,1)} %broadcast_in_dim.5), calls=%async_computation.8 | async-start | bytes 8454144 | tf_op jit(solution)/shard_map/all_to_all | solution.py:680
  369.3 46.9 %all-to-all-done.8 = bf16[8,688,384]{2,1,0:T(8,128)(2,1)} async-done(((bf16[8,688,384]{2,1,0:T(8,128)(2,1)}), bf16[8,688,384]{2,1,0:T(8,128)(2,1)}, u32[]{:S(2)}, u32[]{:S(2)}) %all-to-all-start.8) | async-done | bytes 4227104 | tf_op jit(solution)/shard_map/all_to_all | solution.py:680
  427.3 4.1 fusion
  (146 shorter events, 80.2 us)
Async XLA Ops:
  0.7 45.5 %copy-start.19 = (f32[384]{0:T(512)S(1)}, f32[384]{0:T(512)}, u32[]{:S(2)}) copy-start(f32[384]{0:T(512)} %param.28) | copy-start | bytes 4612
  0.7 60.8 %copy-start.20 = (f32[384]{0:T(512)S(1)}, f32[384]{0:T(512)}, u32[]{:S(2)}) copy-start(f32[384]{0:T(512)} %param.34) | copy-start | bytes 4612
  0.7 61.4 %copy-start.21 = (f32[384]{0:T(512)S(1)}, f32[384]{0:T(512)}, u32[]{:S(2)}) copy-start(f32[384]{0:T(512)} %param.37) | copy-start | bytes 4612
  0.7 61.9 %copy-start.22 = (f32[4,31]{1,0:T(4,128)S(1)}, f32[4,31]{1,0:T(4,128)}, u32[]{:S(2)}) copy-start(f32[4,31]{1,0:T(4,128)} %param.32) | copy-start | bytes 1492
  3.4 43.3 %all-to-all-start = ((bf16[8,48,384]{2,1,0:T(8,128)(2,1)}), bf16[8,48,384]{2,1,0:T(8,128)(2,1)S(1)}, u32[]{:S(2)}, u32[]{:S(2)}) async-start(bf16[8,48,384]{2,1,0:T(8,128)(2,1)} %pad_maximum_fusion.2), calls=%async_computation | async-start | bytes 589824 | tf_op jit(solution)/shard_map/all_to_all | solution.py:680
  11.7 15.6 %collective-permute-start.5 = (bf16[384,384]{1,0:T(8,128)(2,1)S(1)}, bf16[384,384]{1,0:T(8,128)(2,1)S(1)}, u32[]{:S(2)}, u32[]{:S(2)}) collective-permute-start(bf16[384,384]{1,0:T(8,128)(2,1)S(1)} %broadcast_select_fusion), channel_id=1, source_target_pairs={{0,3},{1,2},{2,1},{3,0},{4,7},{5,6},{6,5},{7,4},{8,11},{9,10},{10,... | collective-permute-start | bytes 884744 | tf_op jit(solution)/shard_map/ppermute | solution.py:704
  15.6 30.0 %collective-permute-start.4 = (bf16[384,384]{1,0:T(8,128)(2,1)S(1)}, bf16[384,384]{1,0:T(8,128)(2,1)S(1)}, u32[]{:S(2)}, u32[]{:S(2)}) collective-permute-start(bf16[384,384]{1,0:T(8,128)(2,1)S(1)} %broadcast_select_fusion), channel_id=1, source_target_pairs={{0,2},{1,3},{2,0},{3,1},{4,6},{5,7},{6,4},{7,5},{8,10},{9,11},{10,... | collective-permute-start | bytes 884744 | tf_op jit(solution)/shard_map/ppermute | solution.py:704
  15.6 30.0 %collective-permute-start.3 = (bf16[384,384]{1,0:T(8,128)(2,1)S(1)}, bf16[384,384]{1,0:T(8,128)(2,1)S(1)}, u32[]{:S(2)}, u32[]{:S(2)}) collective-permute-start(bf16[384,384]{1,0:T(8,128)(2,1)S(1)} %broadcast_select_fusion), channel_id=1, source_target_pairs={{0,1},{1,0},{2,3},{3,2},{4,5},{5,4},{6,7},{7,6},{8,9},{9,8},{10,11... | collective-permute-start | bytes 884744 | tf_op jit(solution)/shard_map/ppermute | solution.py:704
  27.3 35.9 %copy-start.1 = (bf16[384,384]{1,0:T(8,128)(2,1)}, bf16[384,384]{1,0:T(8,128)(2,1)S(1)}, u32[]{:S(2)}) copy-start(bf16[384,384]{1,0:T(8,128)(2,1)S(1)} %collective-permute-done.5.refs_13_.refs_25_) | copy-start | bytes 884740
  27.3 35.9 %collective-permute-start.8 = (bf16[384,384]{1,0:T(8,128)(2,1)S(1)}, bf16[384,384]{1,0:T(8,128)(2,1)S(1)}, u32[]{:S(2)}, u32[]{:S(2)}) collective-permute-start(bf16[384,384]{1,0:T(8,128)(2,1)S(1)} %collective-permute-done.5.refs_13_.refs_25_), channel_id=1, source_target_pairs={{0,8},{8,0},{1,9},{9,1},{2,10},{10,2},{3,11},{11,3},{4,12},{12,4},... | collective-permute-start | bytes 884744 | tf_op jit(solution)/shard_map/ppermute | solution.py:705
  45.6 17.6 %collective-permute-start.7 = (bf16[384,384]{1,0:T(8,128)(2,1)S(1)}, bf16[384,384]{1,0:T(8,128)(2,1)S(1)}, u32[]{:S(2)}, u32[]{:S(2)}) collective-permute-start(bf16[384,384]{1,0:T(8,128)(2,1)S(1)} %collective-permute-done.4.refs_12_.refs_24_), channel_id=1, source_target_pairs={{0,8},{8,0},{1,9},{9,1},{2,10},{10,2},{3,11},{11,3},{4,12},{12,4},... | collective-permute-start | bytes 884744 | tf_op jit(solution)/shard_map/ppermute | solution.py:705
  45.6 17.6 %collective-permute-start.6 = (bf16[384,384]{1,0:T(8,128)(2,1)S(1)}, bf16[384,384]{1,0:T(8,128)(2,1)S(1)}, u32[]{:S(2)}, u32[]{:S(2)}) collective-permute-start(bf16[384,384]{1,0:T(8,128)(2,1)S(1)} %collective-permute-done.3.refs_11_.refs_23_), channel_id=1, source_target_pairs={{0,8},{8,0},{1,9},{9,1},{2,10},{10,2},{3,11},{11,3},{4,12},{12,4},... | collective-permute-start | bytes 884744 | tf_op jit(solution)/shard_map/ppermute | solution.py:705
  50.4 5.5 %collective-permute-start = (bf16[80,768]{1,0:T(8,128)(2,1)}, bf16[80,768]{1,0:T(8,128)(2,1)S(1)}, u32[]{:S(2)}, u32[]{:S(2)}) collective-permute-start(bf16[80,768]{1,0:T(8,128)(2,1)} %get-tuple-element.69.refs_2_.refs_29_), channel_id=1, source_target_pairs={{0,4},{4,0},{1,5},{5,1},{2,6},{6,2},{3,7},{7,3},{8,12},{12,8},{9,1... | collective-permute-start | bytes 368648 | tf_op jit(solution)/shard_map/ppermute | solution.py:631
  55.9 7.3 %collective-permute-start.2 = (bf16[32,768]{1,0:T(8,128)(2,1)S(1)}, bf16[32,768]{1,0:T(8,128)(2,1)S(1)}, u32[]{:S(2)}, u32[]{:S(2)}) collective-permute-start(bf16[32,768]{1,0:T(8,128)(2,1)S(1)} %pad_maximum_fusion.5), channel_id=1, source_target_pairs={{0,2},{4,6},{1,3},{5,7},{2,8},{6,12},{3,9},{7,13},{8,10},{12,14},{... | collective-permute-start | bytes 147464 | tf_op jit(solution)/shard_map/ppermute | solution.py:619
  57.4 5.9 %collective-permute-start.1 = (bf16[32,768]{1,0:T(8,128)(2,1)S(1)}, bf16[32,768]{1,0:T(8,128)(2,1)S(1)}, u32[]{:S(2)}, u32[]{:S(2)}) collective-permute-start(bf16[32,768]{1,0:T(8,128)(2,1)S(1)} %pad_maximum_fusion.5), channel_id=1, source_target_pairs={{0,1},{4,5},{1,2},{5,6},{2,3},{6,7},{3,8},{7,12},{8,9},{12,13},{9,... | collective-permute-start | bytes 147464 | tf_op jit(solution)/shard_map/ppermute | solution.py:619
  64.1 23.6 %copy-start.18 = (f32[8,31]{1,0:T(8,128)S(1)}, f32[8,31]{1,0:T(8,128)}, u32[]{:S(2)}) copy-start(f32[8,31]{1,0:T(8,128)} %param.41) | copy-start | bytes 2980
  72.9 8.8 %collective-permute-start.9 = (bf16[80,1536]{1,0:T(8,128)(2,1)}, bf16[80,1536]{1,0:T(8,128)(2,1)S(1)}, u32[]{:S(2)}, u32[]{:S(2)}) collective-permute-start(bf16[80,1536]{1,0:T(8,128)(2,1)} %get-tuple-element.71.refs_1_.refs_8_), channel_id=1, source_target_pairs={{0,4},{4,0},{1,5},{5,1},{2,6},{6,2},{3,7},{7,3},{8,12},{12,8},{9,1... | collective-permute-start | bytes 737288 | tf_op jit(solution)/shard_map/ppermute | solution.py:631
  81.7 6.7 %collective-permute-start.11 = (bf16[32,1536]{1,0:T(8,128)(2,1)S(1)}, bf16[32,1536]{1,0:T(8,128)(2,1)S(1)}, u32[]{:S(2)}, u32[]{:S(2)}) collective-permute-start(bf16[32,1536]{1,0:T(8,128)(2,1)S(1)} %pad_maximum_fusion.4), channel_id=1, source_target_pairs={{0,2},{4,6},{1,3},{5,7},{2,8},{6,12},{3,9},{7,13},{8,10},{12,14},{... | collective-permute-start | bytes 294920 | tf_op jit(solution)/shard_map/ppermute | solution.py:619
  85.8 4.5 %collective-permute-start.10 = (bf16[32,1536]{1,0:T(8,128)(2,1)S(1)}, bf16[32,1536]{1,0:T(8,128)(2,1)S(1)}, u32[]{:S(2)}, u32[]{:S(2)}) collective-permute-start(bf16[32,1536]{1,0:T(8,128)(2,1)S(1)} %pad_maximum_fusion.4), channel_id=1, source_target_pairs={{0,1},{4,5},{1,2},{5,6},{2,3},{6,7},{3,8},{7,12},{8,9},{12,13},{9,... | collective-permute-start | bytes 294920 | tf_op jit(solution)/shard_map/ppermute | solution.py:619
  148.5 74.1 %all-to-all-start.3 = ((bf16[8,384,384]{2,1,0:T(8,128)(2,1)}), bf16[8,384,384]{2,1,0:T(8,128)(2,1)S(1)}, u32[]{:S(2)}, u32[]{:S(2)}) async-start(bf16[8,384,384]{2,1,0:T(8,128)(2,1)} %bitcast.45), calls=%async_computation.3 | async-start | bytes 4718592 | tf_op jit(solution)/shard_map/all_to_all | solution.py:680
  161.5 7.0 %collective-permute-start.13 = (bf16[32,1536]{1,0:T(8,128)(2,1)}, bf16[32,1536]{1,0:T(8,128)(2,1)S(1)}, u32[]{:S(2)}, u32[]{:S(2)}) collective-permute-start(bf16[32,1536]{1,0:T(8,128)(2,1)} %get-tuple-element.81), channel_id=1, source_target_pairs={{1,0},{5,4},{2,1},{6,5},{3,2},{7,6},{8,3},{12,7},{9,8},{13,12},{10... | collective-permute-start | bytes 294920 | tf_op jit(solution)/shard_map/ppermute | solution.py:619
  162.8 7.6 %collective-permute-start.14 = (bf16[32,1536]{1,0:T(8,128)(2,1)}, bf16[32,1536]{1,0:T(8,128)(2,1)S(1)}, u32[]{:S(2)}, u32[]{:S(2)}) collective-permute-start(bf16[32,1536]{1,0:T(8,128)(2,1)} %get-tuple-element.82), channel_id=1, source_target_pairs={{2,0},{6,4},{3,1},{7,5},{8,2},{12,6},{9,3},{13,7},{10,8},{14,12},{... | collective-permute-start | bytes 294920 | tf_op jit(solution)/shard_map/ppermute | solution.py:619
  164.1 21.7 %collective-permute-start.12 = (bf16[64,1536]{1,0:T(8,128)(2,1)}, bf16[64,1536]{1,0:T(8,128)(2,1)S(1)}, u32[]{:S(2)}, u32[]{:S(2)}) collective-permute-start(bf16[64,1536]{1,0:T(8,128)(2,1)} %get-tuple-element.80), channel_id=1, source_target_pairs={{0,4},{4,0},{1,5},{5,1},{2,6},{6,2},{3,7},{7,3},{8,12},{12,8},{9,1... | collective-permute-start | bytes 589832 | tf_op jit(solution)/shard_map/ppermute | solution.py:654
  170.4 15.3 %collective-permute-start.15 = (bf16[16,1536]{1,0:T(8,128)(2,1)S(1)}, bf16[16,1536]{1,0:T(8,128)(2,1)S(1)}, u32[]{:S(2)}, u32[]{:S(2)}) collective-permute-start(bf16[16,1536]{1,0:T(8,128)(2,1)S(1)} %split.24), channel_id=1, source_target_pairs={{0,4},{4,0},{1,5},{5,1},{2,6},{6,2},{3,7},{7,3},{8,12},{12,8},{9,1... | collective-permute-start | bytes 147464 | tf_op jit(solution)/shard_map/ppermute | solution.py:657
  201.8 6.2 %collective-permute-start.17 = (bf16[32,768]{1,0:T(8,128)(2,1)}, bf16[32,768]{1,0:T(8,128)(2,1)S(1)}, u32[]{:S(2)}, u32[]{:S(2)}) collective-permute-start(bf16[32,768]{1,0:T(8,128)(2,1)} %get-tuple-element.94), channel_id=1, source_target_pairs={{1,0},{5,4},{2,1},{6,5},{3,2},{7,6},{8,3},{12,7},{9,8},{13,12},{10... | collective-permute-start | bytes 147464 | tf_op jit(solution)/shard_map/ppermute | solution.py:619
  203.1 7.6 %collective-permute-start.18 = (bf16[32,768]{1,0:T(8,128)(2,1)}, bf16[32,768]{1,0:T(8,128)(2,1)S(1)}, u32[]{:S(2)}, u32[]{:S(2)}) collective-permute-start(bf16[32,768]{1,0:T(8,128)(2,1)} %get-tuple-element.95), channel_id=1, source_target_pairs={{2,0},{6,4},{3,1},{7,5},{8,2},{12,6},{9,3},{13,7},{10,8},{14,12},{... | collective-permute-start | bytes 147464 | tf_op jit(solution)/shard_map/ppermute | solution.py:619
  204.4 10.2 %collective-permute-start.16 = (bf16[64,768]{1,0:T(8,128)(2,1)}, bf16[64,768]{1,0:T(8,128)(2,1)S(1)}, u32[]{:S(2)}, u32[]{:S(2)}) collective-permute-start(bf16[64,768]{1,0:T(8,128)(2,1)} %get-tuple-element.93), channel_id=1, source_target_pairs={{0,4},{4,0},{1,5},{5,1},{2,6},{6,2},{3,7},{7,3},{8,12},{12,8},{9,1... | collective-permute-start | bytes 294920 | tf_op jit(solution)/shard_map/ppermute | solution.py:654
  210.8 3.9 collective-permute-start.19
  244.2 71.2 %all-to-all-start.4 = ((bf16[8,4,240,384]{3,2,1,0:T(8,128)(2,1)}), bf16[8,4,240,384]{3,2,1,0:T(8,128)(2,1)}, u32[]{:S(2)}, u32[]{:S(2)}) async-start(bf16[8,4,240,384]{3,2,1,0:T(8,128)(2,1)} %get-tuple-element.110), calls=%async_computation.4 | async-start | bytes 11796480 | tf_op jit(solution)/shard_map/all_to_all | solution.py:680
  315.4 12.0 %all-to-all-start.7 = ((bf16[4,64,384]{2,1,0:T(8,128)(2,1)}), bf16[4,64,384]{2,1,0:T(8,128)(2,1)}, u32[]{:S(2)}, u32[]{:S(2)}) async-start(bf16[4,64,384]{2,1,0:T(8,128)(2,1)} %pad_maximum_fusion.3), calls=%async_computation.7 | async-start | bytes 393216 | tf_op jit(solution)/shard_map/all_to_all | solution.py:680
  348.6 12.0 %all-to-all-start.2 = ((bf16[8,48,384]{2,1,0:T(8,128)(2,1)}), bf16[8,48,384]{2,1,0:T(8,128)(2,1)S(1)}, u32[]{:S(2)}, u32[]{:S(2)}) async-start(bf16[8,48,384]{2,1,0:T(8,128)(2,1)} %bitcast.63), calls=%async_computation.2 | async-start | bytes 589824 | tf_op jit(solution)/shard_map/all_to_all | solution.py:680
  363.1 53.1 %all-to-all-start.8 = ((bf16[8,688,384]{2,1,0:T(8,128)(2,1)}), bf16[8,688,384]{2,1,0:T(8,128)(2,1)}, u32[]{:S(2)}, u32[]{:S(2)}) async-start(bf16[8,688,384]{2,1,0:T(8,128)(2,1)} %broadcast_in_dim.5), calls=%async_computation.8 | async-start | bytes 8454144 | tf_op jit(solution)/shard_map/all_to_all | solution.py:680
  (17 other events, 84.3 us)

commit v2 on v1

v2 whole, which is shorter than its diff:
```python
import functools

import jax
import jax.numpy as jnp
import numpy as np
from jax import lax
from jax.experimental import pallas as pl
from jax.experimental.pallas import tpu as pltpu
from jax.sharding import Mesh
from jax.sharding import PartitionSpec as P

F32 = jnp.float32
BF16 = jnp.bfloat16
HIGHEST = lax.Precision.HIGHEST
EPSILON = 1e-06
MASKED = -1000000000.0
LOG_FOUR = 1.3862943611198906
SIZE = 96
LANES = 384
INTERPRET = False
PLANE = ("chip", "core", "far", "near")
EVERY = PLANE + ("tensor",)
ACROSS = ("chip", "far", "near")
FRAMES = ("far", "core")


def wide_row(gain):
    return gain[...].reshape(1, gain.shape[0])


def log2(n):
    return n.bit_length() - 1


def mm(left, right):
    return jnp.dot(left, right, preferred_element_type=F32)


def mm_tl(left, right):
    return lax.dot_general(left, right, (((0,), (0,)), ((), ())), preferred_element_type=F32)


def mm_tr(left, right):
    return lax.dot_general(left, right, (((1,), (1,)), ((), ())), preferred_element_type=F32)


def norm(field):
    mean = jnp.mean(field, axis=-1, keepdims=True)
    centered = field - mean
    inverse = lax.rsqrt(jnp.mean(centered * centered, axis=-1, keepdims=True) + EPSILON)
    return centered * inverse, inverse


def norm_back(grad, gain, normed, inverse):
    scaled = grad * gain
    field = inverse * (
        scaled
        - jnp.mean(scaled, axis=-1, keepdims=True)
        - normed * jnp.mean(scaled * normed, axis=-1, keepdims=True)
    )
    return field, jnp.sum(grad * normed, axis=0, keepdims=True)


def gelu(values):
    return 0.5 * values * (1.0 + lax.erf(values * 0.7071067811865476))


def gelu_both(values):
    half = 0.5 * (1.0 + lax.erf(values * 0.7071067811865476))
    slope = half + values * jnp.exp(-0.5 * values * values) * 0.3989422804014327
    return values * half, slope


def blocks(values, count):
    rows = values.shape[0] // count
    return [values[i * rows : (i + 1) * rows] for i in range(count)]


def pool(values, weights):
    parts = blocks(values, 4)
    total = parts[0] * weights[0:1]
    for p in range(1, 4):
        total = total + parts[p] * weights[p : p + 1]
    return total


class Plan:
    def __init__(self, seq, tensor, shape):
        clips, frames, rows, cols, _ = shape
        self.seq, self.tensor = seq, tensor
        assert clips == tensor and frames % seq == 0 and rows % 2 == 0 and cols % 2 == 0
        self.all_frames = frames
        self.frames = frames // seq
        self.rows, self.cols = rows, cols
        self.group = seq * tensor
        self.cells = self.group * rows * cols // 4
        self.pooled = self.frames * self.cells
        self.tokens = 4 * self.pooled
        self.local_squeeze = self.frames % 4 == 0
        self.memory = frames // 4 * self.cells
        self.own = seq * self.pooled
        self.sources = seq + 2 * (seq if self.local_squeeze else 1)
        self.returned = seq + (2 * seq if self.local_squeeze else 0)
        self.keys = self.own + 2 * self.memory
        for n in (self.cells, self.pooled, self.memory, self.own, self.frames, seq):
            assert n == 1 << log2(n)

    def arrange(self):
        take = np.arange(self.tokens).reshape(
            self.group, self.frames, self.rows // 2, 2, self.cols // 2, 2
        )
        per = self.frames * self.rows * self.cols
        half = per // 4 * 2
        step = per + half
        x_rows = take // per * step + take % per
        x_rows = x_rows.transpose(3, 5, 1, 0, 2, 4).reshape(-1)
        cot = np.arange(self.pooled).reshape(self.group, self.frames, -1)
        low = cot // (per // 4) * step + per + cot % (per // 4) * 2
        low = low.transpose(1, 0, 2).reshape(-1)
        order = np.concatenate([x_rows, low, low + 1])
        return (order[:, None] == np.arange(self.group * step)[None, :]).astype(np.float32)


def clip_scalars(plan, resets, videos):
    s = lax.axis_index("far") * lax.axis_size("core") + lax.axis_index("core")
    chip = lax.axis_index("chip") * lax.axis_size("near") + lax.axis_index("near")
    g = chip * plan.tensor + lax.axis_index("tensor")
    before = jnp.maximum(g - 1, 0)
    earlier = jnp.maximum(g - 2, 0)
    first = (g >= 1) & (videos[g] == videos[before]) & (resets[g] == 0)
    second = first & (g >= 2) & (videos[before] == videos[earlier]) & (resets[before] == 0)
    return s, first.astype(jnp.int32), second.astype(jnp.int32)


def key_facts(plan, s, first, second):
    k = lax.broadcasted_iota(jnp.int32, (1, plan.keys), 1)
    own_time = ((s ^ (k >> log2(plan.pooled))) << log2(plan.frames)) + (
        (k & (plan.pooled - 1)) >> log2(plan.cells)
    )
    m = k - plan.own
    late = (m >> log2(plan.memory)) > 0
    g = (m & (plan.memory - 1)) >> log2(plan.cells)
    if plan.local_squeeze:
        each = log2(plan.frames // 4)
        squeezed = ((s ^ (g >> each)) << each) + (g & (plan.frames // 4 - 1))
    else:
        squeezed = (s >> log2(4 // plan.frames)) ^ g
    kind = jnp.where(m < 0, 0, jnp.where(late, 2, 1))
    time = jnp.where(m < 0, own_time, 4 * squeezed - plan.all_frames * kind)
    counts = jnp.where(kind == 0, 1, jnp.where(kind == 1, first, second))
    return time, counts


def offset_onehot(plan, s, time, frame):
    index = s * plan.frames + frame - time + plan.all_frames - 1
    rows = lax.broadcasted_iota(jnp.int32, (128, plan.keys), 0)
    return jnp.where(rows == index, 1.0, 0.0).astype(F32)


def head_mask(width, head):
    lane = lax.broadcasted_iota(jnp.int32, (1, width), 1)
    inside = (lane >= head * SIZE) & (lane < (head + 1) * SIZE)
    return jnp.where(inside, 1.0, 0.0).astype(F32)


def attend(plan, query, keys, values, offsets, heads, probs_ref, table_ref, scalars):
    s, first, second = scalars
    rows, width = query.shape
    places = rows // plan.pooled
    time, counts = key_facts(plan, s, first, second)
    biases = []
    table_ref[...] = jnp.zeros(table_ref.shape, F32)
    table_ref[:heads, : offsets.shape[1]] = offsets[...]
    table = table_ref[...]
    for f in range(plan.frames):
        onehot = offset_onehot(plan, s, time, f)
        bias = jnp.dot(table, onehot, precision=HIGHEST, preferred_element_type=F32)
        biases.append(jnp.where(counts > 0, bias, MASKED))
    total = query.astype(F32)
    for h in range(heads):
        mask = head_mask(width, h)
        scores = mm_tr(query * mask.astype(BF16), keys) * SIZE ** (-0.5)
        bias = jnp.concatenate(
            [jnp.broadcast_to(b[h : h + 1], (plan.cells, plan.keys)) for b in biases] * places, axis=0
        )
        scores = scores + bias
        scores = jnp.exp(scores - jnp.max(scores, axis=-1, keepdims=True))
        probs = scores * (1.0 / jnp.sum(scores, axis=-1, keepdims=True))
        probs = probs.astype(BF16)
        probs_ref[h * rows : (h + 1) * rows] = probs
        total = total + mm(probs, values) * mask
    return total


def attend_back(plan, grad, query, keys, values, probs_ref, heads, bias_ref, table_ref, scalars):
    s, first, second = scalars
    rows, width = query.shape
    places = rows // plan.pooled
    grad_r = grad.astype(BF16)
    grad_query = grad
    grad_keys = jnp.zeros((plan.keys, width), F32)
    grad_values = jnp.zeros((plan.keys, width), F32)
    bias_ref[...] = jnp.zeros(bias_ref.shape, F32)
    for h in range(heads):
        mask = head_mask(width, h)
        mask_r = mask.astype(BF16)
        grad_head = grad_r * mask_r
        query_head = query * mask_r
        probs_r = probs_ref[h * rows : (h + 1) * rows]
        probs = probs_r.astype(F32)
        grad_probs = mm_tr(grad_head, values)
        weighted = probs * grad_probs
        grad_scores = weighted - probs * jnp.sum(weighted, axis=-1, keepdims=True)
        for f in range(plan.frames):
            part = grad_scores[f * plan.cells : (f + 1) * plan.cells]
            for p in range(1, places):
                at = p * plan.pooled + f * plan.cells
                part = part + grad_scores[at : at + plan.cells]
            bias_ref[f, h : h + 1, :] = jnp.sum(part, axis=0, keepdims=True)
        grad_scores_r = grad_scores.astype(BF16)
        grad_query = grad_query + mm(grad_scores_r, keys) * (mask * SIZE ** (-0.5))
        grad_keys = grad_keys + mm_tl(grad_scores_r, query_head)
        grad_values = grad_values + mm_tl(probs_r, grad_head)
    time, _ = key_facts(plan, s, first, second)
    table = jnp.zeros((8, 128), F32)
    for f in range(plan.frames):
        onehot = offset_onehot(plan, s, time, f)
        table = table + lax.dot_general(
            bias_ref[f], onehot, (((1,), (1,)), ((), ())), precision=HIGHEST, preferred_element_type=F32
        )
    table_ref[...] = table
    return grad_query, grad_keys * SIZE ** (-0.5), grad_values


def load_pairs(refs, width):
    pairs = jnp.concatenate([ref[...] for ref in refs], axis=0)
    return pairs[:, :width], pairs[:, width:]


def pool_pair(plan, raw, pool_ref, squeeze_ref, pair_ref, memory_ref=None):
    width = raw.shape[1] // 2
    for i in range(2):
        pooled = pool(raw[:, i * width : (i + 1) * width], pool_ref[pool_ref.shape[0] - 2 + i])
        pair_ref[:, i * width : (i + 1) * width] = pooled.astype(BF16)
        if memory_ref is not None:
            weights = squeeze_ref[i]
            for g in range(plan.frames // 4):
                total = None
                for k in range(4):
                    at = (4 * g + k) * plan.cells
                    part = pooled[at : at + plan.cells] * weights[k : k + 1]
                    total = part if total is None else total + part
                at = g * plan.cells
                memory_ref[at : at + plan.cells, i * width : (i + 1) * width] = total.astype(BF16)


def store_rows(stage, each, z, start, values, base=0):
    core = lax.axis_index("core")
    half, at = stage.shape[1], 0
    while at < values.shape[0]:
        who, off = divmod(start + at, each)
        n = min(each - off, values.shape[0] - at)
        part = values[at : at + n].astype(BF16)
        stage[(who // half) ^ core, who % half, z, base + off : base + off + n, :] = part
        at += n


def store_columns(stage, each, tensor, start, values):
    rows = values.shape[0] // tensor
    for z in range(tensor):
        for c in range(values.shape[1] // LANES):
            part = values[z * rows : (z + 1) * rows, c * LANES : (c + 1) * LANES]
            store_rows(stage, each, z, start + c * rows, part)
    return start + values.shape[1] // LANES * rows


def send_stage(stage, keep, give, sems):
    copies = [pltpu.make_async_copy(stage.at[i], (keep, give)[i], sems.at[i]) for i in range(2)]
    for copy in copies:
        copy.start()
    for copy in copies:
        copy.wait()


def smooth_max(raw):
    parts = blocks(raw, 4)
    highest = jnp.maximum(jnp.maximum(parts[0], parts[1]), jnp.maximum(parts[2], parts[3]))
    total = jnp.exp(parts[0] - highest)
    for p in range(1, 4):
        total = total + jnp.exp(parts[p] - highest)
    return highest + jnp.log(total) - LOG_FOUR


def smooth_max_back(raw, grad):
    parts = blocks(raw, 4)
    highest = jnp.maximum(jnp.maximum(parts[0], parts[1]), jnp.maximum(parts[2], parts[3]))
    parts = [jnp.exp(part - highest) for part in parts]
    total = parts[0] + parts[1] + parts[2] + parts[3]
    scaled = grad / total
    return jnp.concatenate([part * scaled for part in parts], axis=0)


def call(name, body, outs, vmem, smem=(), scratch=(), stage=None):
    scratch = [pltpu.VMEM(shape, dtype) for shape, dtype in scratch]
    spaces = [pltpu.VMEM] * len(outs)
    if stage is not None:
        outs = outs + [(stage[1:], BF16)] * 2
        spaces += [pl.ANY] * 2
        scratch += [pltpu.VMEM(stage, BF16), pltpu.SemaphoreType.DMA((2,))]
    return pl.pallas_call(
        body,
        out_shape=[jax.ShapeDtypeStruct(shape, dtype) for shape, dtype in outs],
        in_specs=[pl.BlockSpec(memory_space=pltpu.SMEM)] * len(smem)
        + [pl.BlockSpec(memory_space=pltpu.VMEM)] * len(vmem),
        out_specs=[pl.BlockSpec(memory_space=space) for space in spaces],
        scratch_shapes=scratch,
        name=name,
        interpret=INTERPRET,
        compiler_params=pltpu.CompilerParams(vmem_limit_bytes=56 << 20),
    )(*smem, *vmem)


def enter_body(plan, arrived, order, gain, project, pools, squeeze, x_ref, cot_ref, n_ref, q_ref, *pair):
    rows = mm(order[...], arrived[...])
    x = rows[: plan.tokens]
    x_ref[...] = x.astype(BF16)
    width = cot_ref.shape[1] // 2
    cot_ref[:, :width] = rows[plan.tokens : plan.tokens + plan.pooled].astype(BF16)
    cot_ref[:, width:] = rows[plan.tokens + plan.pooled :].astype(BF16)
    n = (norm(x)[0] * wide_row(gain)).astype(BF16)
    n_ref[...] = n
    raw = mm(n, project[...])
    q_ref[...] = raw[:, : x.shape[1]].astype(BF16)
    pool_pair(plan, raw[:, x.shape[1] :], pools, squeeze, *pair)


def pick_hidden(pieces, expand, reduce, up_ref, down_ref):
    up_ref[0] = expand[...]
    down_ref[0] = reduce[...]
    core, near = lax.axis_index("core"), lax.axis_index("near")
    rows = pieces[0].shape[0]

    def put(first, second):
        for i, piece in enumerate(pieces):
            k, n, c = i // 4 + 1, i // 2 % 2, i % 2
            at = pl.multiple_of((n ^ near) * rows, 16)
            (second if c else first)[k, pl.ds(at, rows), :] = piece[...]

    @pl.when(core == 0)
    def _():
        put(up_ref, down_ref)

    @pl.when(core != 0)
    def _():
        put(down_ref, up_ref)


def first_body(plan, heads, resets, videos, *refs):
    x, query = refs[:2]
    pairs, refs = refs[2 : 2 + plan.sources], refs[2 + plan.sources :]
    table, output, gain, or_ref, m_ref, l_ref, probs_ref, table_ref = refs
    scalars = clip_scalars(plan, resets, videos)
    keys, values = load_pairs(pairs, x.shape[1])
    mixed_r = attend(plan, query[...], keys, values, table, heads, probs_ref, table_ref, scalars).astype(BF16)
    or_ref[...] = mixed_r
    middle = x[...].astype(F32) + mm(mixed_r, output[...])
    m_ref[...] = middle
    l_ref[...] = (norm(middle)[0] * wide_row(gain)).astype(BF16)


def between_body(plan, m_ref, l_ref, expand, reduce, *refs):
    weights, refs = refs[: 4 * plan.tensor - 4], refs[4 * plan.tensor - 4 :]
    gain_b, project_b, pool_b, squeeze_b, shortcut_b, y_ref, nb_ref, qb_ref, base_ref = refs[:9]
    pair, up_ref, down_ref = refs[9:-2], refs[-2], refs[-1]
    pick_hidden(weights, expand, reduce, up_ref, down_ref)
    l = l_ref[...]
    y = m_ref[...]
    for k in range(plan.tensor):
        hidden = gelu(mm(l, up_ref[k])).astype(BF16)
        y = y + mm(hidden, down_ref[k])
    y_ref[...] = y
    n = (norm(y)[0] * wide_row(gain_b)).astype(BF16)
    nb_ref[...] = n
    wide = base_ref.shape[1]
    raw = mm(n, project_b[...])
    qb_ref[...] = pool(raw[:, :wide], pool_b[0]).astype(BF16)
    pool_pair(plan, raw[:, wide:], pool_b, squeeze_b, *pair)
    base_ref[...] = smooth_max(mm(n, shortcut_b[...]))


def second_body(plan, heads, resets, videos, *refs):
    query, pairs, refs = refs[0], refs[1 : 1 + plan.sources], refs[1 + plan.sources :]
    table, output, gain, base, cot, or_ref, m_ref, send_ref, probs_ref, table_ref = refs
    width = query.shape[1]
    scalars = clip_scalars(plan, resets, videos)
    keys, values = load_pairs(pairs, width)
    mixed_r = attend(plan, query[...], keys, values, table, heads, probs_ref, table_ref, scalars).astype(BF16)
    or_ref[...] = mixed_r
    middle = base[...] + mm(mixed_r, output[...])
    m_ref[...] = middle
    send_ref[:, :width] = (norm(middle)[0] * wide_row(gain)).astype(BF16)
    send_ref[:, width:] = cot[...]


def hidden_body(each, rows, up, down, send_ref, keep, give, stage, sems):
    width = up.shape[0]
    l = rows[:, :width]
    grad = rows[:, width:]
    gate, slope = gelu_both(mm(l, up[...]))
    hidden = gate.astype(BF16)
    send_ref[:, :width] = mm(hidden, down[...]).astype(BF16)
    grad_pre = (slope * mm_tr(grad, down[...])).astype(BF16)
    send_ref[:, width:] = mm_tr(grad_pre, up[...]).astype(BF16)
    grad_up = mm_tl(l, grad_pre)
    grad_down = mm_tl(hidden, grad)
    at = 0
    for whole in (grad_up, grad_down):
        for c in range(whole.shape[1] // LANES):
            part = whole[:, c * LANES : (c + 1) * LANES]
            store_rows(stage, each, 0, at, part)
            at += part.shape[0]
    send_stage(stage, keep, give, sems)


def second_back_body(plan, heads, resets, videos, *refs):
    refs = list(refs)
    sums, cot, middle, gain, mixed, output, query, probs = refs[:8]
    pairs, refs = refs[8 : 8 + plan.sources], refs[8 + plan.sources :]
    out_ref, dm_ref, dgain_ref = refs[:3]
    refs = refs[3:]
    width = query.shape[1]
    total = sums[0].astype(F32)
    for z in range(1, plan.tensor):
        total = total + sums[z].astype(F32)
    m = middle[...]
    out_ref[...] = (m + total[:, :width]).astype(BF16)
    normed, inverse = norm(m)
    grad, dgain = norm_back(total[:, width:], wide_row(gain), normed, inverse)
    dgain_ref[...] = dgain
    grad = cot[...].astype(F32) + grad
    dm_ref[...] = grad
    store_back(plan, heads, resets, videos, grad, mixed, output, query, probs, pairs, *refs)


def store_back(plan, heads, resets, videos, grad, mixed, output, query, probs, pairs, doutput_ref, dq_ref, dtable_ref,
               *refs):
    width = query.shape[1]
    scalars = clip_scalars(plan, resets, videos)
    grad_r = grad.astype(BF16)
    doutput_ref[...] = mm_tl(mixed[...], grad_r).astype(BF16)
    grads, bias_ref = refs[:-1], refs[-1]
    keys, values = load_pairs(pairs, width)
    dq, dk, dv = attend_back(
        plan, mm_tr(grad_r, output[...]), query[...], keys, values, probs, heads, bias_ref, dtable_ref, scalars
    )
    dq_ref[...] = dq
    for i, part in enumerate((dk, dv)):
        lanes = slice(i * width, (i + 1) * width)
        at = 0
        for ref in grads:
            ref[:, lanes] = part[at : at + ref.shape[0]].astype(ref.dtype)
            at += ref.shape[0]


def pair_grads(plan, refs):
    own, received = refs[0], refs[1 : plan.seq]
    grad = own[...]
    for ref in received:
        grad = grad + ref[...].astype(F32)
    if not plan.local_squeeze:
        return grad, None
    memory = None
    size = plan.memory // plan.seq
    for i, ref in enumerate(refs[plan.seq :]):
        o = i % plan.seq
        part = ref[o * size : (o + 1) * size, :].astype(F32)
        memory = part if memory is None else memory + part
    return grad, memory


def unpool(plan, raw, grad, memory, pool_ref, squeeze_ref, dpool_ref, dsqueeze_ref, first):
    width = raw.shape[1] // 2
    result = []
    for i in range(2):
        weights = pool_ref[first + i]
        lanes = slice(i * width, (i + 1) * width)
        part = grad[:, lanes]
        source = raw[:, lanes]
        if plan.local_squeeze:
            pooled = pool(source, weights)
            ws = squeeze_ref[i]
            pieces = []
            sums = [None] * 4
            for g in range(plan.frames // 4):
                dm = memory[g * plan.cells : (g + 1) * plan.cells, lanes]
                for k in range(4):
                    at = (4 * g + k) * plan.cells
                    pieces.append(part[at : at + plan.cells] + dm * ws[k : k + 1])
                    total = jnp.sum(dm * pooled[at : at + plan.cells], axis=0, keepdims=True)
                    sums[k] = total if sums[k] is None else sums[k] + total
            part = jnp.concatenate(pieces, axis=0)
            for k in range(4):
                dsqueeze_ref[i, k : k + 1, :] = sums[k]
        result.append(unpool_one(source, part, weights, dpool_ref, first + i))
    return result


def unpool_one(source, part, weights, dpool_ref, place):
    pieces = []
    for p, piece in enumerate(blocks(source, 4)):
        dpool_ref[place, p : p + 1, :] = jnp.sum(part * piece, axis=0, keepdims=True)
        pieces.append((part * weights[p : p + 1]).astype(BF16))
    return jnp.concatenate(pieces, axis=0)


def cross_body(plan, each, *refs):
    pieces = plan.returned
    grads = refs[:pieces]
    (dq, dm, doutput_b, n_ref, y_ref, gain_b, project_b, pool_b, squeeze_b, shortcut_b,
     dy_ref, dpool_ref, dsqueeze_ref, dgain_ref, keep, give, stage, sems) = refs[pieces:]
    tensor = plan.tensor
    wide = dm.shape[1]
    n = n_ref[...]
    grad, memory = pair_grads(plan, grads)
    raw = mm(n, project_b[...])
    parts = [unpool_one(raw[:, :wide], dq[...], pool_b[0], dpool_ref, 0)]
    parts += unpool(plan, raw[:, wide:], grad, memory, pool_b, squeeze_b, dpool_ref, dsqueeze_ref, 1)
    at = 0
    grad_n = None
    for i, part in enumerate(parts):
        at = store_columns(stage, each, tensor, at, mm_tl(n, part))
        back = mm_tr(part, project_b[:, i * wide : (i + 1) * wide])
        grad_n = back if grad_n is None else grad_n + back
    grad_z = smooth_max_back(mm(n, shortcut_b[...]), dm[...]).astype(BF16)
    at = store_columns(stage, each, tensor, at, mm_tl(n, grad_z))
    store_columns(stage, each, tensor, at, doutput_b[...])
    grad_n = grad_n + mm_tr(grad_z, shortcut_b[...])
    normed, inverse = norm(y_ref[...])
    grad_y, dgain = norm_back(grad_n, wide_row(gain_b), normed, inverse)
    dgain_ref[...] = dgain
    dy_ref[...] = grad_y
    send_stage(stage, keep, give, sems)


def first_back_body(plan, each, heads, resets, videos, *refs):
    refs = list(refs)

    def take(n):
        taken = refs[:n]
        del refs[:n]
        return taken

    dy_ref, m_ref, l_ref, gain, mixed, output, query, probs, expand, reduce = take(10)
    weights = take(4 * plan.tensor - 4)
    pairs = take(plan.sources)
    dgain_ref, dm_out = take(2)
    refs, (keep, give, up_ref, down_ref, bias_ref, stage, sems) = refs[:-7], refs[-7:]
    tensor = plan.tensor
    pick_hidden(weights, expand, reduce, up_ref, down_ref)
    grad_y = dy_ref[...]
    grad_r = grad_y.astype(BF16)
    l = l_ref[...]
    t = lax.axis_index("tensor")
    grad_l = None
    for k in range(tensor):
        gate, slope = gelu_both(mm(l, up_ref[k]))
        hidden = gate.astype(BF16)
        grad_pre = (slope * mm_tr(grad_r, down_ref[k])).astype(BF16)
        z = t ^ k
        store_rows(stage, each, z, 0, mm_tl(l, grad_pre))
        store_rows(stage, each, z, l.shape[1], mm_tl(hidden, grad_r))
        back = mm_tr(grad_pre, up_ref[k])
        grad_l = back if grad_l is None else grad_l + back
    normed, inverse = norm(m_ref[...])
    grad, dgain = norm_back(grad_l, wide_row(gain), normed, inverse)
    dgain_ref[...] = dgain
    grad = grad_y + grad
    dm_out[...] = grad
    store_back(plan, heads, resets, videos, grad, mixed, output, query, probs, pairs, *refs, bias_ref)
    send_stage(stage, keep, give, sems)


def store_tail(stage, each, tensor, start, values):
    rows = values.shape[0] // tensor
    for z in range(tensor):
        for c in range(values.shape[1] // LANES):
            part = values[z * rows : (z + 1) * rows, c * LANES : (c + 1) * LANES]
            store_rows(stage, each, 0, start + c * rows, part, z * each)
    return start + values.shape[1] // LANES * rows


def load_rows(whole, each, start, count, base=0):
    half = whole.shape[1]
    parts, at = [], 0
    while at < count:
        who, off = divmod(start + at, each)
        n = min(each - off, count - at)
        parts.append(whole[who // half, who % half, base + off : base + off + n, :].astype(F32))
        at += n
    return parts


def across_index():
    index = 0
    for axis in ACROSS:
        index = index * lax.axis_size(axis) + lax.axis_index(axis)
    return index


def unpack_columns(whole, each, base, start, out):
    rows = out.shape[0]
    for c in range(out.shape[1] // LANES):
        at = 0
        for part in load_rows(whole, each, start + c * rows, rows, base):
            out[at : at + part.shape[0], c * LANES : (c + 1) * LANES] = part
            at += part.shape[0]
    return start + out.shape[1] // LANES * rows


def unpack_body(groups, *refs):
    core, across = lax.axis_index("core"), across_index()
    half = refs[-1].shape[1]
    pieces, refs = refs[: 2 * half], refs[2 * half :]
    count = sum(n for _, n in groups)
    outs, small, whole = refs[:count], refs[count:-1], refs[-1]
    sums, small = (small[-1], small[:-1]) if small else (None, small)
    for i, ref in enumerate(pieces):
        whole[(i // half) ^ core, (i % half) ^ across] = ref[...]
    base, first = 0, 0
    for each, n in groups:
        at = 0
        for out in outs[first : first + n]:
            at = unpack_columns(whole, each, base, at, out)
        base, first = base + each, first + n
    if sums is None:
        return
    at = 0
    for part in load_rows(whole, whole.shape[2] - base, 0, sums.shape[0], base):
        sums[at : at + part.shape[0]] = part
        at += part.shape[0]
    gain_a, pool_a, squeeze_a, table_a, mid_a, gain_b, pool_b, squeeze_b, table_b, mid_b = small
    for i, ref in enumerate((gain_a, mid_a, gain_b)):
        ref[...] = sums[i]
    for i in range(2):
        half = slice(i * LANES, (i + 1) * LANES)
        mid_b[half] = sums[3 + i]
        pool_a[i] = sums[8 + 4 * i : 12 + 4 * i, :]
        squeeze_a[i] = sums[16 + 4 * i : 20 + 4 * i, :]
        for j in range(3):
            pool_b[j, :, half] = sums[24 + 16 * i + 4 * j : 28 + 16 * i + 4 * j, :]
        for j in range(2):
            squeeze_b[j, :, half] = sums[56 + 8 * i + 4 * j : 60 + 8 * i + 4 * j, :]
    for ref, at in ((table_a, 72), (table_b, 80)):
        ref[...] = sums[at : at + ref.shape[0], : ref.shape[1]]


def leave_body(plan, each, small_each, *refs):
    refs = list(refs)
    pieces = plan.returned
    grads, refs = refs[:pieces], refs[pieces:]
    (dq, dm, doutput, n_ref, x_ref, gain, project, pools, squeeze, order, out,
     dgain_mid, dtable, dgain_b, dpool_b, dsqueeze_b, dmid_b, dtable_b) = refs[:18]
    refs = refs[18:]
    given = refs.pop(0) if not plan.local_squeeze else None
    send_ref, keep, give, dpool_ref, dsqueeze_ref, sum_ref, stage, sems = refs
    tensor = plan.tensor
    width = x_ref.shape[1]
    n = n_ref[...]
    grad, memory = pair_grads(plan, grads)
    raw = mm(n, project[:, width:])
    parts = [dq[...].astype(BF16)]
    parts += unpool(plan, raw, grad, memory, pools, squeeze, dpool_ref, dsqueeze_ref, 0)
    at = 0
    grad_n = None
    for i, part in enumerate(parts):
        at = store_tail(stage, each, tensor, at, mm_tl(n, part))
        back = mm_tr(part, project[:, i * width : (i + 1) * width])
        grad_n = back if grad_n is None else grad_n + back
    store_tail(stage, each, tensor, at, doutput[...])
    normed, inverse = norm(x_ref[...].astype(F32))
    grad_x, dgain = norm_back(grad_n, wide_row(gain), normed, inverse)
    grad_x = (grad_x + dm[...]).astype(BF16)
    leaving = jnp.concatenate([grad_x, out[:, :width], out[:, width:]], axis=0)
    send_ref[...] = mm_tl(order[...], leaving).astype(BF16)
    sum_ref[...] = jnp.zeros(sum_ref.shape, F32)
    squeeze_a = dsqueeze_ref if given is None else given
    sum_ref[0:1, :] = dgain
    sum_ref[1:2, :] = dgain_mid[...]
    sum_ref[2:3, :] = dgain_b[...]
    for i in range(2):
        half = slice(i * width, (i + 1) * width)
        sum_ref[3 + i : 4 + i, :] = dmid_b[:, half]
        sum_ref[8 + 4 * i : 12 + 4 * i, :] = dpool_ref[i]
        sum_ref[16 + 4 * i : 20 + 4 * i, :] = squeeze_a[i]
        for j in range(3):
            sum_ref[24 + 16 * i + 4 * j : 28 + 16 * i + 4 * j, :] = dpool_b[j, :, half]
        for j in range(2):
            sum_ref[56 + 8 * i + 4 * j : 60 + 8 * i + 4 * j, :] = dsqueeze_b[j, :, half]
    sum_ref[72:80, :128] = dtable[...]
    sum_ref[80:88, :128] = dtable_b[...]
    store_rows(stage, small_each, 0, 0, sum_ref[...], tensor * each)
    send_stage(stage, keep, give, sems)


def exchange(values, axes, by):
    axes = (axes,) if isinstance(axes, str) else axes
    order = [axis for axis in EVERY if axis in axes]
    sizes = [lax.axis_size(axis) for axis in axes]
    into = [axes.index(axis) for axis in order]
    place = np.arange(np.prod(sizes)).reshape(sizes).transpose(into).reshape(-1)
    where = np.argsort(place)
    return lax.ppermute(values, tuple(order), [(i, int(where[p ^ by])) for i, p in enumerate(place)])


def to_core(values):
    return exchange(values, "core", 1)


def swap(values):
    cores, near = lax.axis_size("core"), lax.axis_size("near")
    assert cores == near
    pairs = [(i * near + j, j * near + i) for i in range(cores) for j in range(near)]
    return lax.ppermute(values, ("core", "near"), pairs)


def shift(values, by):
    chips, cores, far, near, tensor = (lax.axis_size(axis) for axis in EVERY)
    clips = chips * near * tensor

    def place(g, core, f):
        chip, n = divmod(g // tensor, near)
        return (((chip * cores + core) * far + f) * near + n) * tensor + g % tensor

    pairs = [
        (place(g, core, f), place(g + by, core, f))
        for g in range(clips)
        for core in range(cores)
        for f in range(far)
        if 0 <= g + by < clips
    ]
    return lax.ppermute(values, EVERY, pairs)


def relative_weights(plan, squeeze):
    s = lax.axis_index(FRAMES)
    order = jnp.arange(plan.all_frames)
    frame = ((s ^ (order // plan.frames)) * plan.frames + order % plan.frames) % 4
    pair = jnp.concatenate([squeeze[0], squeeze[1]], axis=-1)
    return pair[frame], frame


def share_pairs(plan, pair, squeeze):
    pairs = [pair[0]] + [exchange(pair[0], FRAMES, o) for o in range(1, plan.seq)]
    if plan.local_squeeze:
        memories = [shift(pair[1], by) for by in (1, 2)]
        return pairs + [exchange(each, FRAMES, o) if o else each for each in memories for o in range(plan.seq)]
    memory = squeeze_all(plan, pairs, squeeze)
    return pairs + [shift(memory, 1), shift(memory, 2)]


def by_frame(plan, pairs):
    together = jnp.concatenate([each.astype(F32) for each in pairs], axis=0)
    return together.reshape(plan.all_frames // 4, 4, plan.cells, -1)


def squeeze_all(plan, pairs, squeeze):
    weights = relative_weights(plan, squeeze)[0].reshape(plan.all_frames // 4, 4, 1, -1)
    total = jnp.sum(by_frame(plan, pairs) * weights, axis=1)
    return total.reshape(plan.memory, -1).astype(BF16)


def return_pairs(plan, grads, pairs, squeeze):
    own, others, memories = grads[0], grads[1 : plan.seq], grads[plan.seq :]
    memories = [shift(memories[0], -1), shift(memories[1], -2)]
    if plan.local_squeeze:
        received = [exchange(each, FRAMES, o + 1) for o, each in enumerate(others)]
        memories = [exchange(each, FRAMES, o) if o else each for each in memories for o in range(plan.seq)]
        return [own] + received + memories, None
    memory = memories[0].astype(F32) + memories[1].astype(F32)
    weights, frame = relative_weights(plan, squeeze)
    weights = weights.reshape(plan.all_frames // 4, 4, 1, -1)
    memory = memory.reshape(plan.all_frames // 4, 1, plan.cells, -1)
    both = by_frame(plan, [own, *others]) + memory * weights
    both = jnp.split(both.reshape(plan.own, -1), plan.seq, axis=0)
    sums = jnp.sum(by_frame(plan, pairs[: plan.seq]) * memory, axis=2).reshape(plan.all_frames, -1)
    onehot = (frame[None, :] == jnp.arange(4)[:, None]).astype(F32)
    sums = jnp.dot(onehot, sums, precision=HIGHEST)
    width = sums.shape[1] // 2
    received = [
        exchange(each.astype(BF16), FRAMES, o + 1) for o, each in enumerate(both[1:])
    ]
    return [both[0]] + received, jnp.stack([sums[:, :width], sums[:, width:]])


def sum_first(values):
    return jnp.sum(values.astype(F32), axis=0).astype(BF16)


def spread(values, axes):
    return lax.all_to_all(values, axes, 0, 0, tiled=True)


def after(value, *others):
    return lax.optimization_barrier((value, others))[0]


def sum_cores(keep, give):
    return (keep.astype(F32) + to_core(give).astype(F32)).astype(BF16)


def gather_plane(values):
    mine = [exchange(values, ACROSS, k) if k else values for k in range(lax.axis_size(ACROSS))]
    return mine + [to_core(each) for each in mine]


def padded(rows, parts):
    return -(-rows // (16 * parts)) * 16


def local(
    clips_in, cotangent, resets, videos,
    attend_gain_a, project_a, pooling_a, squeeze_a, offsets_a, output_a, mixer_gain_a, expand_a, reduce_a,
    attend_gain_b, project_b, pooling_b, squeeze_b, offsets_b, output_b, shortcut_b, mixer_gain_b, expand_b, reduce_b,
):
    seq, tensor, plane = lax.axis_size(FRAMES), lax.axis_size("tensor"), lax.axis_size(PLANE)
    plan = Plan(seq, tensor, clips_in.shape)
    width, wide = clips_in.shape[-1], cotangent.shape[-1]
    heads_a, heads_b = offsets_a.shape[0], offsets_b.shape[0]
    core = lax.axis_index("core")
    tokens, pooled, keys, memory = plan.tokens, plan.pooled, plan.keys, plan.memory
    order = jnp.asarray(plan.arrange(), BF16)
    home = ("tensor",) + FRAMES
    leaving = jnp.concatenate(
        [clips_in.reshape(plan.group, -1, width), cotangent.reshape(plan.group, -1, width)], axis=1
    )
    arrived = spread(swap(leaving), home)
    half = jnp.where(core == 0, expand_a, reduce_a)
    half, arrived = lax.optimization_barrier((half, arrived))
    arrived = arrived.reshape(-1, width)
    quarter = half.reshape(2, -1, half.shape[1])[lax.axis_index("near")]
    mine = [exchange(quarter, "tensor", k) for k in range(1, tensor)]
    pair = lambda w: [((pooled, 2 * w), BF16)] + [((memory // seq, 2 * w), BF16)] * plan.local_squeeze
    x, cot, n_a, q_a, *pair_a = call(
        "enter",
        functools.partial(enter_body, plan),
        [((tokens, width), BF16), ((pooled, wide), BF16), ((tokens, width), BF16), ((tokens, width), BF16),
         *pair(width)],
        [arrived, order, attend_gain_a, project_a, pooling_a, squeeze_a],
    )
    pairs_a = share_pairs(plan, pair_a, squeeze_a)
    hidden = [((tensor, width, expand_a.shape[1]), BF16), ((tensor, reduce_a.shape[0], width), BF16)]
    or_a, m_a, l_a, probs_a = call(
        "first",
        functools.partial(first_body, plan, heads_a),
        [((tokens, width), BF16), ((tokens, width), F32), ((tokens, width), BF16), ((heads_a * tokens, keys), BF16)],
        [x, q_a, *pairs_a, offsets_a, output_a, mixer_gain_a],
        [resets, videos],
        [((8, 128), F32)],
    )
    mine, pairs_a = lax.optimization_barrier((mine, pairs_a))
    weights = []
    for each in mine:
        other = exchange(each, "near", 1)
        weights += [each, to_core(each), other, to_core(other)]
    y_a, n_b, q_b, base, *pair_b = call(
        "between",
        functools.partial(between_body, plan),
        [((tokens, width), F32), ((tokens, width), BF16), ((pooled, wide), BF16), ((pooled, wide), F32), *pair(wide)],
        [m_a, l_a, expand_a, reduce_a, *weights, attend_gain_b, project_b, pooling_b, squeeze_b, shortcut_b],
        (),
        hidden,
    )
    pairs_b = share_pairs(plan, pair_b, squeeze_b)
    or_b, m_b, rows_b, probs_b = call(
        "second",
        functools.partial(second_body, plan, heads_b),
        [((pooled, wide), BF16), ((pooled, wide), F32), ((pooled, 2 * wide), BF16),
         ((heads_b * pooled, keys), BF16)],
        [q_b, *pairs_b, offsets_b, output_b, mixer_gain_b, base, cot],
        [resets, videos],
        [((8, 128), F32)],
    )
    rows_all = lax.all_gather(rows_b, "tensor", axis=0, tiled=True)
    hidden_rows = (expand_b.shape[1] // LANES) * wide + (wide // LANES) * reduce_b.shape[0]
    half_plane = plane // 2
    hidden_each = padded(hidden_rows, plane)
    shares, keep, give = call(
        "hidden",
        functools.partial(hidden_body, hidden_each),
        [((tensor * pooled, 2 * wide), BF16)],
        [rows_all, expand_b, reduce_b],
        stage=(2, half_plane, 1, hidden_each, LANES),
    )
    sums = spread(shares, "tensor")
    early = spread(after(sum_cores(keep, give), sums), ACROSS)
    sums = sums.reshape(tensor, pooled, 2 * wide)
    bias = lambda: [((plan.frames, 8, keys), F32)]
    key_grads = lambda w: (
        [((pooled, 2 * w), F32)] + [((pooled, 2 * w), BF16)] * (seq - 1) + [((memory, 2 * w), BF16)] * 2
    )
    out, dm_b, dmid_b, doutput_b, dq_b, dtable_b, *back = call(
        "second_back",
        functools.partial(second_back_body, plan, heads_b),
        [((pooled, wide), BF16), ((pooled, wide), F32), ((1, wide), F32), ((wide, wide), BF16), ((pooled, wide), F32),
         ((8, 128), F32), *key_grads(wide)],
        [sums, cot, m_b, mixer_gain_b, or_b, output_b, q_b, probs_b, *pairs_b],
        [resets, videos],
        bias(),
    )
    pieces, dsqueeze_given = return_pairs(plan, back, pairs_b, squeeze_b)
    dq_b = after(dq_b, early)
    early = gather_plane(sum_first(early)[0])
    share = width // tensor
    cross_each = padded((3 + 1) * wide // LANES * share + wide // LANES * (wide // tensor), plane)
    dy_a, dpool_b, dsqueeze_b, dgain_b, keep, give = call(
        "cross",
        functools.partial(cross_body, plan, cross_each),
        [((tokens, width), F32), ((3, 4, wide), F32), ((2, 4, wide), F32), ((1, width), F32)],
        [*pieces, dq_b, dm_b, doutput_b, n_b, y_a, attend_gain_b, project_b, pooling_b, squeeze_b, shortcut_b],
        stage=(2, half_plane, tensor, cross_each, LANES),
    )
    cross = spread(sum_cores(keep, give), ACROSS)
    first_each = padded(2 * width, plane)
    dmid_a, dm_a, doutput_a, dq_a, dtable_a, *back, keep, give = call(
        "first_back",
        functools.partial(first_back_body, plan, first_each, heads_a),
        [((1, width), F32), ((tokens, width), F32), ((width, width), BF16), ((tokens, width), F32), ((8, 128), F32),
         *key_grads(width)],
        [dy_a, m_a, l_a, mixer_gain_a, or_a, output_a, q_a, probs_a, expand_a, reduce_a, *weights,
         *pairs_a],
        [resets, videos],
        hidden + bias(),
        stage=(2, half_plane, tensor, first_each, LANES),
    )
    first = spread(after(sum_cores(keep, give), cross), ACROSS)
    grad_expand_b, grad_reduce_b = call(
        "unpack_early",
        functools.partial(unpack_body, [(hidden_each, 2)]),
        [(expand_b.shape, F32), (reduce_b.shape, F32)],
        early,
        (),
        [((2, half_plane, hidden_each, LANES), BF16)],
    )
    if dsqueeze_given is not None:
        dsqueeze_b = dsqueeze_given
    pieces, dsqueeze_given = return_pairs(plan, back, pairs_a, squeeze_a)
    tail_each, small_each = padded(4 * share, plane), padded(128, plane)
    leaving, keep, give = call(
        "leave",
        functools.partial(leave_body, plan, tail_each, small_each),
        [(arrived.shape, BF16)],
        [*pieces, dq_a, dm_a, doutput_a, n_a, x, attend_gain_a, project_a, pooling_a, squeeze_a, order, out,
         dmid_a, dtable_a, dgain_b, dpool_b, dsqueeze_b, dmid_b, dtable_b]
        + ([] if dsqueeze_given is None else [dsqueeze_given]),
        (),
        [((2, 4, width), F32), ((2, 4, width), F32), ((128, LANES), F32)],
        stage=(2, half_plane, 1, tensor * tail_each + small_each, LANES),
    )
    last = spread(after(sum_cores(keep, give), first), ACROSS)
    cross, first = sum_first(cross), sum_first(first)
    last = sum_first(last)[0]
    small = jnp.broadcast_to(last[None, tensor * tail_each :], (tensor, small_each, LANES))
    last = last[: tensor * tail_each].reshape(tensor, tail_each, LANES)
    last = spread(jnp.concatenate([cross, first, last, small], axis=1), "tensor")
    leaving = after(leaving, last)
    late = gather_plane(sum_first(last))
    returned = swap(spread(leaving.reshape(plan.group, -1, width), home))
    x_rows = plan.frames * plan.rows * plan.cols
    grad_input = returned[:, :x_rows].reshape(clips_in.shape).astype(F32)
    result = returned[:, x_rows:].reshape(cotangent.shape).astype(F32)
    column = lambda rows, columns: ((rows, columns), F32)
    (
        grad_project_b, grad_shortcut_b, grad_output_b, grad_expand_a, grad_reduce_a, grad_project_a, grad_output_a,
        *small,
    ) = call(
        "unpack",
        functools.partial(unpack_body, [(cross_each, 3), (first_each, 2), (tail_each, 2)]),
        [
            column(share, 3 * wide), column(share, wide), column(wide // tensor, wide), (expand_a.shape, F32),
            (reduce_a.shape, F32), column(share, 3 * width), column(share, width),
            ((width,), F32), (pooling_a.shape, F32), (squeeze_a.shape, F32), (offsets_a.shape, F32), ((width,), F32),
            ((width,), F32), (pooling_b.shape, F32), (squeeze_b.shape, F32), (offsets_b.shape, F32), ((wide,), F32),
        ],
        late,
        (),
        [((128, LANES), F32), ((2, half_plane, cross_each + first_each + tail_each + small_each, LANES), BF16)],
    )
    return (
        result,
        grad_input,
        small[0],
        grad_project_a,
        small[1],
        small[2],
        small[3],
        grad_output_a,
        small[4],
        grad_expand_a,
        grad_reduce_a,
        small[5],
        grad_project_b,
        small[6],
        small[7],
        small[8],
        grad_output_b,
        grad_shortcut_b,
        small[9],
        grad_expand_b,
        grad_reduce_b,
    )


def solution(mesh):
    clip, seq, tensor = mesh.devices.shape
    split = Mesh(mesh.devices.reshape(clip // 2, 2, seq // 2, 2, tensor), EVERY)
    field = P(("chip", "core"), None, ("far", "near"), "tensor", None)
    up, down = P(None, "tensor"), P("tensor", None)
    block = (P(), P(), P(), P(), P(), P(), P(), up, down)
    block_b = (P(), P(), P(), P(), P(), P(), P(), P(), up, down)
    grads = (P(), down, P(), P(), P(), down, P(), up, down)
    grads_b = (P(), down, P(), P(), P(), down, down, P(), up, down)
    return jax.shard_map(
        local,
        mesh=split,
        in_specs=(field, field, P(), P()) + block + block_b,
        out_specs=(field, field) + grads + grads_b,
        check_vma=False,
    )
```

time: 447 us -> 322 us (0.72)
  waiting for transfers between devices: 185 us -> 116 us
  blocking collectives: 87.7 us -> 24.8 us
  local copies, waits for them, and re-layouts: 44 us -> 7.99 us
  starting transfers between devices: 58.8 us -> 90.5 us
  Pallas kernels: 53.6 us -> 67.3 us
    all_to_all x3 -> x0, blocking collectives: 67 us -> none  [spread(): return lax.all_to_all(values, axes, 0, 0, tiled=True)]
    all_to_all x6 -> x8, waiting for transfers between devices: 120 us -> 79.5 us  [spread(): return lax.all_to_all(values, axes, 0, 0, tiled=True)]
    ppermute x12 -> x44, waiting for transfers between devices: 52.7 us -> 16.5 us  [the longest x42 16.5 us: exchange(): lax.ppermute(values, tuple(order), [(i, int(where[p ^ by])) for i, p in e...]
    all_to_all x6 -> x8, starting transfers between devices: 28 us -> 44.4 us  [spread(): return lax.all_to_all(values, axes, 0, 0, tiled=True)]
    slice x19 -> x1, local copies, waits for them, and re-layouts: 13.9 us -> 0.02 us  [local(): last = last[:tensor * tail_each].reshape(tensor, tail_each, LANES)]
    pallas_call x7 -> x11, Pallas kernels: 53.6 us -> 67.3 us  [call(): pl.pallas_call(body, out_shape=[jax.ShapeDtypeStruct(shape, dtype) for sh...]
    ppermute x12 -> x44, starting transfers between devices: 14.7 us -> 26.5 us  [the longest x42 23.5 us: exchange(): lax.ppermute(values, tuple(order), [(i, int(where[p ^ by])) for i, p in e...]
    convert_element_type x0 -> x4, other arithmetic: none -> 7.78 us  [sum_cores(): return (keep.astype(F32) + to_core(give).astype(F32)).astype(BF16)]
  transfers between devices with their start and end apart: 26 -> 60, of which waited for: 16 -> 23; matrix products, arithmetic and copies ran while one was open for 5% -> 3% of each run, Pallas kernels for 7% -> 12%
where the time goes in v2:
time: 322 us; the launch traced here: 320 us
  waiting for transfers between devices  116 us (36%)
  starting transfers between devices  90.5 us (28%)
  Pallas kernels  67.3 us (21%)
  blocking collectives  24.8 us (8%)
  other arithmetic  12.6 us (4%)
  local copies, waits for them, and re-layouts  7.99 us (2%)
    all_to_all x8, waiting for transfers between devices, spread(): return lax.all_to_all(values, axes, 0, 0, tiled=True)  79.5 us
    pallas_call x11, Pallas kernels, call(): pl.pallas_call(body, out_shape=[jax.ShapeDtypeStruct(shape, dtype) for sh...  67.3 us
    all_to_all x8, starting transfers between devices, spread(): return lax.all_to_all(values, axes, 0, 0, tiled=True)  44.4 us
    all_gather x1, blocking collectives, local(): rows_all = lax.all_gather(rows_b, 'tensor', axis=0, tiled=True)  24.8 us
    ppermute x42, starting transfers between devices, exchange(): lax.ppermute(values, tuple(order), [(i, int(where[p ^ by])) for i, p in e...  23.5 us
    ppermute x8, waiting for transfers between devices, shift(): return lax.ppermute(values, EVERY, pairs)  19.8 us
    ppermute x8, starting transfers between devices, shift(): return lax.ppermute(values, EVERY, pairs)  19.6 us
    ppermute x42, waiting for transfers between devices, exchange(): lax.ppermute(values, tuple(order), [(i, int(where[p ^ by])) for i, p in e...  16.5 us
  transfers between devices with their start and end apart: 60, of which 23 were waited for; matrix products, arithmetic and copies ran while one was open for 3% of the time, Pallas kernels for 12%

profile of v2, /device:TPU:0, one launch (start us, length us, event | category | flops | bytes accessed | tf_op | source)
XLA Modules:
  0.0 320.4 jit_solution(1027877542376214157)
XLA Ops:
  4.1 12.6 %all-to-all-start = ((bf16[8,48,384]{2,1,0:T(8,128)(2,1)}), bf16[8,48,384]{2,1,0:T(8,128)(2,1)S(1)}, u32[]{:S(2)}, u32[]{:S(2)}) async-start(bf16[8,48,384]{2,1,0:T(8,128)(2,1)} %collective-permute-done), calls=%async_computation | async-start | bytes 589824 | tf_op jit(solution)/shard_map/all_to_all | solution.py:800
  16.8 10.4 %all-to-all-done = bf16[8,48,384]{2,1,0:T(8,128)(2,1)S(1)} async-done(((bf16[8,48,384]{2,1,0:T(8,128)(2,1)}), bf16[8,48,384]{2,1,0:T(8,128)(2,1)S(1)}, u32[]{:S(2)}, u32[]{:S(2)}) %all-to-all-start) | async-done | bytes 294944 | tf_op jit(solution)/shard_map/all_to_all | solution.py:800
  37.6 8.8 %collective-permute-start.4 = (bf16[16,768]{1,0:T(8,128)(2,1)}, bf16[16,768]{1,0:T(8,128)(2,1)S(1)}, u32[]{:S(2)}, u32[]{:S(2)}) collective-permute-start(bf16[16,768]{1,0:T(8,128)(2,1)} %get-tuple-element.112), channel_id=1, source_target_pairs={{0,2},{8,10},{1,3},{9,11},{2,4},{10,12},{3,5},{11,13},{4,6},{12,14... | collective-permute-start | bytes 73736 | tf_op jit(solution)/shard_map/ppermute | solution.py:741
  50.8 4.8 %collective-permute-start.10 = (bf16[192,384]{1,0:T(8,128)(2,1)S(1)}, bf16[192,384]{1,0:T(8,128)(2,1)S(1)}, u32[]{:S(2)}, u32[]{:S(2)}) collective-permute-start(bf16[192,384]{1,0:T(8,128)(2,1)S(1)} %collective-permute-done.6.refs_0_.refs_10_), channel_id=1, source_target_pairs={{0,4},{4,0},{1,5},{5,1},{2,6},{6,2},{3,7},{7,3},{8,12},{12,8},{9,1... | collective-permute-start | bytes 442376 | tf_op jit(solution)/shard_map/ppermute | solution.py:712
  60.3 3.2 collective-permute-done.13.refs_6_.refs_16_
  66.3 4.1 %first.1 = (bf16[256,384]{1,0:T(8,128)(2,1)}, f32[256,384]{1,0:T(8,128)}, bf16[256,384]{1,0:T(8,128)(2,1)}, bf16[1024,192]{1,0:T(8,128)(2,1)}) custom-call(s32[16]{0:T(128)} %resets.7, s32[16]{0:T(128)} %videos.7, bf16[256,384]{1,0:T(8,128)(2,1)} %get-tuple-element.109.refs_0_.refs_10_, bf16[256,384]{1,0:T(8,128)(2,1)} %get-tuple-element.110.refs_1_.refs_6_, ...), custom_call_target="tpu_custom_call" | custom-call | tf_op jit(solution)/shard_map/first/pallas_call | solution.py:310
  71.3 6.3 %between.1 = (f32[256,384]{1,0:T(8,128)}, bf16[256,384]{1,0:T(8,128)(2,1)}, bf16[64,768]{1,0:T(8,128)(2,1)}, f32[64,768]{1,0:T(8,128)}, bf16[64,1536]{1,0:T(8,128)(2,1)}, /*index=5*/bf16[16,1536]{1,0:T(8,128)(2,1)}) custom-call(f32[256,384]{1,0:T(8,128)} %get-tuple-element.113.m_ref.refs_1_, bf16[256,384]{1,0:T(8,128)(2,1)} %get-tuple-element.114.l_ref.refs_2_, ...), custom_call_target="tpu_custom_call" | custom-call | tf_op jit(solution)/shard_map/between/pallas_call | solution.py:310
  86.3 7.2 %second.1 = (bf16[64,768]{1,0:T(8,128)(2,1)}, f32[64,768]{1,0:T(8,128)}, bf16[64,1536]{1,0:T(8,128)(2,1)}, bf16[512,192]{1,0:T(8,128)(2,1)}) custom-call(s32[16]{0:T(128)} %resets.7, s32[16]{0:T(128)} %videos.7, bf16[64,768]{1,0:T(8,128)(2,1)} %get-tuple-element.119.refs_0_.refs_6_, bf16[64,1536]{1,0:T(8,128)(2,1)} %get-tuple-element.120.refs_1_.refs_8_, ...), custom_call_target="tpu_custom_call" | custom-call | tf_op jit(solution)/shard_map/second/pallas_call | solution.py:310
  93.6 24.8 %all_gather.3.rows = bf16[256,1536]{1,0:T(8,128)(2,1)} all-gather(bf16[64,1536]{1,0:T(8,128)(2,1)} %get-tuple-element.124), channel_id=1, replica_groups=mesh['chip'=2,'core'=2,'far'=1,'near'=2,'tensor'=4] {'tensor'}, dimensions={0}, use_global_device_ids=true | all-gather | bytes 983040 | tf_op jit(solution)/shard_map/all_gather | solution.py:883
  118.3 6.3 %hidden.1 = (bf16[256,1536]{1,0:T(8,128)(2,1)}, bf16[4,1,384,384]{3,2,1,0:T(8,128)(2,1)}, bf16[4,1,384,384]{3,2,1,0:T(8,128)(2,1)}) custom-call(bf16[256,1536]{1,0:T(8,128)(2,1)} %all_gather.3.rows, bf16[768,768]{1,0:T(8,128)(2,1)} %up.1, bf16[768,768]{1,0:T(8,128)(2,1)} %down.1), custom_call_target="tpu_custom_call" | custom-call | tf_op jit(solution)/shard_map/hidden/pallas_call | solution.py:310
  124.8 3.6 %all-to-all-start.1 = ((bf16[4,64,1536]{2,1,0:T(8,128)(2,1)}), bf16[4,64,1536]{2,1,0:T(8,128)(2,1)S(1)}, u32[]{:S(2)}, u32[]{:S(2)}) async-start(bf16[4,64,1536]{2,1,0:T(8,128)(2,1)} %bitcast.11), calls=%async_computation.1 | async-start | bytes 1572864 | tf_op jit(solution)/shard_map/all_to_all | solution.py:800
  129.7 19.5 %all-to-all-done.1.refs_0_ = bf16[4,64,1536]{2,1,0:T(8,128)(2,1)S(1)} async-done(((bf16[4,64,1536]{2,1,0:T(8,128)(2,1)}), bf16[4,64,1536]{2,1,0:T(8,128)(2,1)S(1)}, u32[]{:S(2)}, u32[]{:S(2)}) %all-to-all-start.1) | async-done | bytes 786464 | tf_op jit(solution)/shard_map/all_to_all | solution.py:800
  149.3 4.3 %all-to-all-start.2 = ((bf16[4,1,384,384]{3,2,1,0:T(8,128)(2,1)}), bf16[4,1,384,384]{3,2,1,0:T(8,128)(2,1)S(1)}, u32[]{:S(2)}, u32[]{:S(2)}) async-start(bf16[4,1,384,384]{3,2,1,0:T(8,128)(2,1)} %add_convert_fusion.2), calls=%async_computation.2 | async-start | bytes 2359296 | tf_op jit(solution)/shard_map/all_to_all | solution.py:800
  153.6 9.1 %second_back.1 = (bf16[64,768]{1,0:T(8,128)(2,1)}, f32[64,768]{1,0:T(8,128)}, f32[1,768]{1,0:T(1,128)}, bf16[768,768]{1,0:T(8,128)(2,1)}, f32[64,768]{1,0:T(8,12...) custom-call(s32[16]{0:T(128)} %resets.7, ...), custom_call_target="tpu_custom_call" | custom-call | tf_op jit(solution)/shard_map/second_back/pallas_call | solution.py:310
  165.3 4.7 %collective-permute-done.24.refs_2_ = bf16[32,1536]{1,0:T(8,128)(2,1)S(1)} collective-permute-done((bf16[32,1536]{1,0:T(8,128)(2,1)}, bf16[32,1536]{1,0:T(8,128)(2,1)S(1)}, u32[]{:S(2)}, u32[]{:S(2)}) %collective-permute-start.24) | collective-permute-done | bytes 98336 | tf_op jit(solution)/shard_map/ppermute | solution.py:741
  170.0 4.3 %collective-permute-done.26.refs_4_ = bf16[32,1536]{1,0:T(8,128)(2,1)S(1)} collective-permute-done((bf16[32,1536]{1,0:T(8,128)(2,1)}, bf16[32,1536]{1,0:T(8,128)(2,1)S(1)}, u32[]{:S(2)}, u32[]{:S(2)}) %collective-permute-start.26) | collective-permute-done | bytes 98336 | tf_op jit(solution)/shard_map/ppermute | solution.py:741
  176.3 8.1 %cross.1 = (f32[256,384]{1,0:T(8,128)}, f32[3,4,768]{2,1,0:T(4,128)}, f32[2,4,768]{2,1,0:T(4,128)}, f32[1,384]{1,0:T(1,128)}, bf16[4,4,144,384]{3,2,1,0:T(8,128)(2,1)}, /*index=5*/bf16[4,4,144,384]{3,2,1,0:T(8,128)(2,1)}) custom-call(f32[64,1536]{1,0:T(8,128)} %get-tuple-element.129.refs_0_, bf16[64,1536]{1,0:T(8,128)(2,1)} %copy-done.36, ...), custom_call_target="tpu_custom_call" | custom-call | tf_op jit(solution)/shard_map/cross/pallas_call | solution.py:310
  184.7 10.4 %first_back.1 = (f32[1,384]{1,0:T(1,128)}, f32[256,384]{1,0:T(8,128)}, bf16[384,384]{1,0:T(8,128)(2,1)}, f32[256,384]{1,0:T(8,128)}, f32[8,128]{1,0:T(8,128)}, /...) custom-call(s32[16]{0:T(128)} %resets.7, ...), custom_call_target="tpu_custom_call" | custom-call | tf_op jit(solution)/shard_map/first_back/pallas_call | solution.py:310
  197.2 6.1 %all-to-all-start.3 = ((bf16[4,4,144,384]{3,2,1,0:T(8,128)(2,1)}), bf16[4,4,144,384]{3,2,1,0:T(8,128)(2,1)S(1)}, u32[]{:S(2)}, u32[]{:S(2)}) async-start(bf16[4,4,144,384]{3,2,1,0:T(8,128)(2,1)} %add_convert_fusion), calls=%async_computation.3 | async-start | bytes 3538944 | tf_op jit(solution)/shard_map/all_to_all | solution.py:800
  206.1 3.3 %collective-permute-done.30.refs_2_ = bf16[32,768]{1,0:T(8,128)(2,1)S(1)} collective-permute-done((bf16[32,768]{1,0:T(8,128)(2,1)S(1)}, bf16[32,768]{1,0:T(8,128)(2,1)S(1)}, u32[]{:S(2)}, u32[]{:S(2)}) %collective-permute-start.30) | collective-permute-done | bytes 49184 | tf_op jit(solution)/shard_map/ppermute | solution.py:741
  213.5 5.0 %leave.1 = (bf16[384,384]{1,0:T(8,128)(2,1)}, bf16[4,1,208,384]{3,2,1,0:T(8,128)(2,1)}, bf16[4,1,208,384]{3,2,1,0:T(8,128)(2,1)}) custom-call(f32[64,768]{1,0:T(8,128)} %get-tuple-element.150.refs_0_, bf16[64,768]{1,0:T(8,128)(2,1)} %copy-done.41, bf16[32,768]{1,0:T(8,128)(2,1)} %copy-done.50, bf16[32,768]{1,0:T(8,128)(2,1)} %copy-done.52, ...), custom_call_target="tpu_custom_call" | custom-call | tf_op jit(solution)/shard_map/leave/pallas_call | solution.py:310
  221.3 3.8 %all-to-all-done.3 = bf16[4,4,144,384]{3,2,1,0:T(8,128)(2,1)S(1)} async-done(((bf16[4,4,144,384]{3,2,1,0:T(8,128)(2,1)}), bf16[4,4,144,384]{3,2,1,0:T(8,128)(2,1)S(1)}, u32[]{:S(2)}, u32[]{:S(2)}) %all-to-all-start.3) | async-done | bytes 1769504 | tf_op jit(solution)/shard_map/all_to_all | solution.py:800
  225.2 4.3 %all-to-all-start.4 = ((bf16[4,4,96,384]{3,2,1,0:T(8,128)(2,1)}), bf16[4,4,96,384]{3,2,1,0:T(8,128)(2,1)}, u32[]{:S(2)}, u32[]{:S(2)}) async-start(bf16[4,4,96,384]{3,2,1,0:T(8,128)(2,1)} %add_convert_fusion.1), calls=%async_computation.4 | async-start | bytes 2359296 | tf_op jit(solution)/shard_map/all_to_all | solution.py:800
  231.7 14.3 %all-to-all-done.4 = bf16[4,4,96,384]{3,2,1,0:T(8,128)(2,1)} async-done(((bf16[4,4,96,384]{3,2,1,0:T(8,128)(2,1)}), bf16[4,4,96,384]{3,2,1,0:T(8,128)(2,1)}, u32[]{:S(2)}, u32[]{:S(2)}) %all-to-all-start.4) | async-done | bytes 1179680 | tf_op jit(solution)/shard_map/all_to_all | solution.py:800
  246.0 4.2 %all-to-all-start.5 = ((bf16[4,1,208,384]{3,2,1,0:T(8,128)(2,1)}), bf16[4,1,208,384]{3,2,1,0:T(8,128)(2,1)}, u32[]{:S(2)}, u32[]{:S(2)}) async-start(bf16[4,1,208,384]{3,2,1,0:T(8,128)(2,1)} %add_convert_fusion.3), calls=%async_computation.5 | async-start | bytes 1277952 | tf_op jit(solution)/shard_map/all_to_all | solution.py:800
  252.2 7.6 %all-to-all-done.5 = bf16[4,1,208,384]{3,2,1,0:T(8,128)(2,1)} async-done(((bf16[4,1,208,384]{3,2,1,0:T(8,128)(2,1)}), bf16[4,1,208,384]{3,2,1,0:T(8,128)(2,1)}, u32[]{:S(2)}, u32[]{:S(2)}) %all-to-all-start.5) | async-done | bytes 639008 | tf_op jit(solution)/shard_map/all_to_all | solution.py:800
  262.0 5.2 %all-to-all-start.6 = ((bf16[4,304,384]{2,1,0:T(8,128)(2,1)}), bf16[4,304,384]{2,1,0:T(8,128)(2,1)S(1)}, u32[]{:S(2)}, u32[]{:S(2)}) async-start(bf16[4,304,384]{2,1,0:T(8,128)(2,1)} %pad_maximum_fusion), calls=%async_computation.6 | async-start | bytes 1867776 | tf_op jit(solution)/shard_map/all_to_all | solution.py:800
  271.0 18.5 %all-to-all-done.6 = bf16[4,304,384]{2,1,0:T(8,128)(2,1)S(1)} async-done(((bf16[4,304,384]{2,1,0:T(8,128)(2,1)}), bf16[4,304,384]{2,1,0:T(8,128)(2,1)S(1)}, u32[]{:S(2)}, u32[]{:S(2)}) %all-to-all-start.6) | async-done | bytes 933920 | tf_op jit(solution)/shard_map/all_to_all | solution.py:800
  289.5 4.1 %all-to-all-start.7 = ((bf16[8,48,384]{2,1,0:T(8,128)(2,1)}), bf16[8,48,384]{2,1,0:T(8,128)(2,1)}, u32[]{:S(2)}, u32[]{:S(2)}) async-start(bf16[8,48,384]{2,1,0:T(8,128)(2,1)} %bitcast.7), calls=%async_computation.7 | async-start | bytes 589824 | tf_op jit(solution)/shard_map/all_to_all | solution.py:800
  298.5 5.5 %all-to-all-done.7 = bf16[8,48,384]{2,1,0:T(8,128)(2,1)} async-done(((bf16[8,48,384]{2,1,0:T(8,128)(2,1)}), bf16[8,48,384]{2,1,0:T(8,128)(2,1)}, u32[]{:S(2)}, u32[]{:S(2)}) %all-to-all-start.7) | async-done | bytes 294944 | tf_op jit(solution)/shard_map/all_to_all | solution.py:800
  309.4 4.2 %unpack_early.1 = (f32[768,768]{1,0:T(8,128)}, f32[768,768]{1,0:T(8,128)}) custom-call(bf16[384,384]{1,0:T(8,128)(2,1)} %copy-done.6, bf16[384,384]{1,0:T(8,128)(2,1)} %copy-done.23, bf16[384,384]{1,0:T(8,128)(2,1)} %copy-done.24, bf16[384,384]{1,0:T(8,128)(2,1)} %copy-done.25, bf16[384,384]{1,0:T(8,128)(2,1)} %copy-done.26, bf16[384,384]{1,0:T(8,128)(2,1)} %copy-done.27, ...), custom_call_target="tpu_custom_call" | custom-call | tf_op jit(solution)/shard_map/unpack_early/pallas_call | solution.py:310
  315.1 3.6 %unpack.1 = (f32[96,2304]{1,0:T(8,128)}, f32[96,768]{1,0:T(8,128)}, f32[192,768]{1,0:T(8,128)}, f32[384,384]{1,0:T(8,128)}, f32[384,384]{1,0:T(8,128)}, /*index=...) custom-call(bf16[304,384]{1,0:T(8,128)(2,1)} %copy-done.8, ...), custom_call_target="tpu_custom_call" | custom-call | tf_op jit(solution)/shard_map/unpack/pallas_call | solution.py:310
  (236 shorter events, 76.8 us)
Async XLA Ops:
  4.1 23.0 %all-to-all-start = ((bf16[8,48,384]{2,1,0:T(8,128)(2,1)}), bf16[8,48,384]{2,1,0:T(8,128)(2,1)S(1)}, u32[]{:S(2)}, u32[]{:S(2)}) async-start(bf16[8,48,384]{2,1,0:T(8,128)(2,1)} %collective-permute-done), calls=%async_computation | async-start | bytes 589824 | tf_op jit(solution)/shard_map/all_to_all | solution.py:800
  27.2 23.3 %collective-permute-start.6 = (bf16[192,384]{1,0:T(8,128)(2,1)S(1)}, bf16[192,384]{1,0:T(8,128)(2,1)S(1)}, u32[]{:S(2)}, u32[]{:S(2)}) collective-permute-start(bf16[192,384]{1,0:T(8,128)(2,1)S(1)} %dynamic-slice_bitcast_fusion), channel_id=1, source_target_pairs={{0,1},{1,0},{2,3},{3,2},{4,5},{5,4},{6,7},{7,6},{8,9},{9,8},{10,11... | collective-permute-start | bytes 442376 | tf_op jit(solution)/shard_map/ppermute | solution.py:712
  27.2 23.3 %collective-permute-start.7 = (bf16[192,384]{1,0:T(8,128)(2,1)S(1)}, bf16[192,384]{1,0:T(8,128)(2,1)S(1)}, u32[]{:S(2)}, u32[]{:S(2)}) collective-permute-start(bf16[192,384]{1,0:T(8,128)(2,1)S(1)} %dynamic-slice_bitcast_fusion), channel_id=1, source_target_pairs={{0,2},{1,3},{2,0},{3,1},{4,6},{5,7},{6,4},{7,5},{8,10},{9,11},{10,... | collective-permute-start | bytes 442376 | tf_op jit(solution)/shard_map/ppermute | solution.py:712
  29.1 21.4 %collective-permute-start.8 = (bf16[192,384]{1,0:T(8,128)(2,1)S(1)}, bf16[192,384]{1,0:T(8,128)(2,1)S(1)}, u32[]{:S(2)}, u32[]{:S(2)}) collective-permute-start(bf16[192,384]{1,0:T(8,128)(2,1)S(1)} %dynamic-slice_bitcast_fusion), channel_id=1, source_target_pairs={{0,3},{1,2},{2,1},{3,0},{4,7},{5,6},{6,5},{7,4},{8,11},{9,10},{10,... | collective-permute-start | bytes 442376 | tf_op jit(solution)/shard_map/ppermute | solution.py:712
  35.8 14.6 %collective-permute-start.1 = (bf16[64,768]{1,0:T(8,128)(2,1)}, bf16[64,768]{1,0:T(8,128)(2,1)S(1)}, u32[]{:S(2)}, u32[]{:S(2)}) collective-permute-start(bf16[64,768]{1,0:T(8,128)(2,1)} %get-tuple-element.144.refs_2_.refs_22_), channel_id=1, source_target_pairs={{0,8},{8,0},{1,9},{9,1},{2,10},{10,2},{3,11},{11,3},{4,12},{12,4},... | collective-permute-start | bytes 294920 | tf_op jit(solution)/shard_map/ppermute | solution.py:712
  37.6 10.5 %collective-permute-start.4 = (bf16[16,768]{1,0:T(8,128)(2,1)}, bf16[16,768]{1,0:T(8,128)(2,1)S(1)}, u32[]{:S(2)}, u32[]{:S(2)}) collective-permute-start(bf16[16,768]{1,0:T(8,128)(2,1)} %get-tuple-element.112), channel_id=1, source_target_pairs={{0,2},{8,10},{1,3},{9,11},{2,4},{10,12},{3,5},{11,13},{4,6},{12,14... | collective-permute-start | bytes 73736 | tf_op jit(solution)/shard_map/ppermute | solution.py:741
  50.8 9.5 %collective-permute-start.10 = (bf16[192,384]{1,0:T(8,128)(2,1)S(1)}, bf16[192,384]{1,0:T(8,128)(2,1)S(1)}, u32[]{:S(2)}, u32[]{:S(2)}) collective-permute-start(bf16[192,384]{1,0:T(8,128)(2,1)S(1)} %collective-permute-done.6.refs_0_.refs_10_), channel_id=1, source_target_pairs={{0,4},{4,0},{1,5},{5,1},{2,6},{6,2},{3,7},{7,3},{8,12},{12,8},{9,1... | collective-permute-start | bytes 442376 | tf_op jit(solution)/shard_map/ppermute | solution.py:712
  55.6 10.7 %collective-permute-start.16 = (bf16[192,384]{1,0:T(8,128)(2,1)S(1)}, bf16[192,384]{1,0:T(8,128)(2,1)S(1)}, u32[]{:S(2)}, u32[]{:S(2)}) collective-permute-start(bf16[192,384]{1,0:T(8,128)(2,1)S(1)} %collective-permute-done.8.refs_8_.refs_18_), channel_id=1, source_target_pairs={{0,4},{4,0},{1,5},{5,1},{2,6},{6,2},{3,7},{7,3},{8,12},{12,8},{9,1... | collective-permute-start | bytes 442376 | tf_op jit(solution)/shard_map/ppermute | solution.py:712
  57.6 12.8 %collective-permute-start.12 = (bf16[192,384]{1,0:T(8,128)(2,1)S(1)}, bf16[192,384]{1,0:T(8,128)(2,1)S(1)}, u32[]{:S(2)}, u32[]{:S(2)}) collective-permute-start(bf16[192,384]{1,0:T(8,128)(2,1)S(1)} %collective-permute-done.7.refs_4_.refs_14_), channel_id=1, source_target_pairs={{0,8},{8,0},{1,9},{9,1},{2,10},{10,2},{3,11},{11,3},{4,12},{12,4},... | collective-permute-start | bytes 442376 | tf_op jit(solution)/shard_map/ppermute | solution.py:712
  57.6 12.8 %collective-permute-start.15 = (bf16[192,384]{1,0:T(8,128)(2,1)S(1)}, bf16[192,384]{1,0:T(8,128)(2,1)S(1)}, u32[]{:S(2)}, u32[]{:S(2)}) collective-permute-start(bf16[192,384]{1,0:T(8,128)(2,1)S(1)} %collective-permute-done.8.refs_8_.refs_18_), channel_id=1, source_target_pairs={{0,8},{8,0},{1,9},{9,1},{2,10},{10,2},{3,11},{11,3},{4,12},{12,4},... | collective-permute-start | bytes 442376 | tf_op jit(solution)/shard_map/ppermute | solution.py:712
  60.3 10.2 %collective-permute-start.11 = (bf16[192,384]{1,0:T(8,128)(2,1)S(1)}, bf16[192,384]{1,0:T(8,128)(2,1)S(1)}, u32[]{:S(2)}, u32[]{:S(2)}) collective-permute-start(bf16[192,384]{1,0:T(8,128)(2,1)S(1)} %collective-permute-done.10.refs_2_.refs_12_), channel_id=1, source_target_pairs={{0,8},{8,0},{1,9},{9,1},{2,10},{10,2},{3,11},{11,3},{4,12},{12,4},... | collective-permute-start | bytes 442376 | tf_op jit(solution)/shard_map/ppermute | solution.py:712
  77.6 8.1 %collective-permute-start.18 = (bf16[64,1536]{1,0:T(8,128)(2,1)}, bf16[64,1536]{1,0:T(8,128)(2,1)S(1)}, u32[]{:S(2)}, u32[]{:S(2)}) collective-permute-start(bf16[64,1536]{1,0:T(8,128)(2,1)} %get-tuple-element.120.refs_1_.refs_8_), channel_id=1, source_target_pairs={{0,8},{8,0},{1,9},{9,1},{2,10},{10,2},{3,11},{11,3},{4,12},{12,4},... | collective-permute-start | bytes 589832 | tf_op jit(solution)/shard_map/ppermute | solution.py:712
  124.8 24.5 %all-to-all-start.1 = ((bf16[4,64,1536]{2,1,0:T(8,128)(2,1)}), bf16[4,64,1536]{2,1,0:T(8,128)(2,1)S(1)}, u32[]{:S(2)}, u32[]{:S(2)}) async-start(bf16[4,64,1536]{2,1,0:T(8,128)(2,1)} %bitcast.11), calls=%async_computation.1 | async-start | bytes 1572864 | tf_op jit(solution)/shard_map/all_to_all | solution.py:800
  149.3 25.1 %all-to-all-start.2 = ((bf16[4,1,384,384]{3,2,1,0:T(8,128)(2,1)}), bf16[4,1,384,384]{3,2,1,0:T(8,128)(2,1)S(1)}, u32[]{:S(2)}, u32[]{:S(2)}) async-start(bf16[4,1,384,384]{3,2,1,0:T(8,128)(2,1)} %add_convert_fusion.2), calls=%async_computation.2 | async-start | bytes 2359296 | tf_op jit(solution)/shard_map/all_to_all | solution.py:800
  162.7 11.7 %collective-permute-start.23 = (bf16[64,1536]{1,0:T(8,128)(2,1)}, bf16[64,1536]{1,0:T(8,128)(2,1)S(1)}, u32[]{:S(2)}, u32[]{:S(2)}) collective-permute-start(bf16[64,1536]{1,0:T(8,128)(2,1)} %get-tuple-element.130), channel_id=1, source_target_pairs={{0,8},{8,0},{1,9},{9,1},{2,10},{10,2},{3,11},{11,3},{4,12},{12,4},... | collective-permute-start | bytes 589832 | tf_op jit(solution)/shard_map/ppermute | solution.py:712
  164.0 10.3 %collective-permute-start.26 = (bf16[32,1536]{1,0:T(8,128)(2,1)}, bf16[32,1536]{1,0:T(8,128)(2,1)S(1)}, u32[]{:S(2)}, u32[]{:S(2)}) collective-permute-start(bf16[32,1536]{1,0:T(8,128)(2,1)} %get-tuple-element.132), channel_id=1, source_target_pairs={{2,0},{10,8},{3,1},{11,9},{4,2},{12,10},{5,3},{13,11},{6,4},{14,12... | collective-permute-start | bytes 294920 | tf_op jit(solution)/shard_map/ppermute | solution.py:741
  184.4 11.1 %collective-permute-start.34 = (bf16[4,4,144,384]{3,2,1,0:T(8,128)(2,1)}, bf16[4,4,144,384]{3,2,1,0:T(8,128)(2,1)S(1)}, u32[]{:S(2)}, u32[]{:S(2)}) collective-permute-start(bf16[4,4,144,384]{3,2,1,0:T(8,128)(2,1)} %get-tuple-element.168), channel_id=1, source_target_pairs={{0,8},{8,0},{1,9},{9,1},{2,10},{10,2},{3,11},{11,3},{4,12},{12,4},... | collective-permute-start | bytes 5308424 | tf_op jit(solution)/shard_map/ppermute | solution.py:712
  195.1 23.7 %collective-permute-start.35 = (bf16[4,4,96,384]{3,2,1,0:T(8,128)(2,1)}, bf16[4,4,96,384]{3,2,1,0:T(8,128)(2,1)}, u32[]{:S(2)}, u32[]{:S(2)}) collective-permute-start(bf16[4,4,96,384]{3,2,1,0:T(8,128)(2,1)} %get-tuple-element.170), channel_id=1, source_target_pairs={{0,8},{8,0},{1,9},{9,1},{2,10},{10,2},{3,11},{11,3},{4,12},{12,4},... | collective-permute-start | bytes 3538952 | tf_op jit(solution)/shard_map/ppermute | solution.py:712
  197.2 28.0 %all-to-all-start.3 = ((bf16[4,4,144,384]{3,2,1,0:T(8,128)(2,1)}), bf16[4,4,144,384]{3,2,1,0:T(8,128)(2,1)S(1)}, u32[]{:S(2)}, u32[]{:S(2)}) async-start(bf16[4,4,144,384]{3,2,1,0:T(8,128)(2,1)} %add_convert_fusion), calls=%async_computation.3 | async-start | bytes 3538944 | tf_op jit(solution)/shard_map/all_to_all | solution.py:800
  218.5 10.9 %collective-permute-start.36 = (bf16[4,1,208,384]{3,2,1,0:T(8,128)(2,1)}, bf16[4,1,208,384]{3,2,1,0:T(8,128)(2,1)}, u32[]{:S(2)}, u32[]{:S(2)}) collective-permute-start(bf16[4,1,208,384]{3,2,1,0:T(8,128)(2,1)} %get-tuple-element.173), channel_id=1, source_target_pairs={{0,8},{8,0},{1,9},{9,1},{2,10},{10,2},{3,11},{11,3},{4,12},{12,4},... | collective-permute-start | bytes 1916936 | tf_op jit(solution)/shard_map/ppermute | solution.py:712
  225.2 20.9 %all-to-all-start.4 = ((bf16[4,4,96,384]{3,2,1,0:T(8,128)(2,1)}), bf16[4,4,96,384]{3,2,1,0:T(8,128)(2,1)}, u32[]{:S(2)}, u32[]{:S(2)}) async-start(bf16[4,4,96,384]{3,2,1,0:T(8,128)(2,1)} %add_convert_fusion.1), calls=%async_computation.4 | async-start | bytes 2359296 | tf_op jit(solution)/shard_map/all_to_all | solution.py:800
  246.0 13.7 %all-to-all-start.5 = ((bf16[4,1,208,384]{3,2,1,0:T(8,128)(2,1)}), bf16[4,1,208,384]{3,2,1,0:T(8,128)(2,1)}, u32[]{:S(2)}, u32[]{:S(2)}) async-start(bf16[4,1,208,384]{3,2,1,0:T(8,128)(2,1)} %add_convert_fusion.3), calls=%async_computation.5 | async-start | bytes 1277952 | tf_op jit(solution)/shard_map/all_to_all | solution.py:800
  262.0 27.5 %all-to-all-start.6 = ((bf16[4,304,384]{2,1,0:T(8,128)(2,1)}), bf16[4,304,384]{2,1,0:T(8,128)(2,1)S(1)}, u32[]{:S(2)}, u32[]{:S(2)}) async-start(bf16[4,304,384]{2,1,0:T(8,128)(2,1)} %pad_maximum_fusion), calls=%async_computation.6 | async-start | bytes 1867776 | tf_op jit(solution)/shard_map/all_to_all | solution.py:800
  267.5 26.5 %collective-permute-start.45 = (bf16[384,384]{1,0:T(8,128)(2,1)S(1)}, bf16[384,384]{1,0:T(8,128)(2,1)S(1)}, u32[]{:S(2)}, u32[]{:S(2)}) collective-permute-start(bf16[384,384]{1,0:T(8,128)(2,1)S(1)} %reduce_sum.67.refs_0_), channel_id=1, source_target_pairs={{0,4},{4,0},{16,20},{20,16},{1,5},{5,1},{17,21},{21,17},{2,6},{6,2... | collective-permute-start | bytes 884744 | tf_op jit(solution)/shard_map/ppermute | solution.py:712
  268.4 25.7 %collective-permute-start.46 = (bf16[384,384]{1,0:T(8,128)(2,1)S(1)}, bf16[384,384]{1,0:T(8,128)(2,1)S(1)}, u32[]{:S(2)}, u32[]{:S(2)}) collective-permute-start(bf16[384,384]{1,0:T(8,128)(2,1)S(1)} %reduce_sum.67.refs_0_), channel_id=1, source_target_pairs={{0,16},{4,20},{16,0},{20,4},{1,17},{5,21},{17,1},{21,5},{2,18},{6,... | collective-permute-start | bytes 884744 | tf_op jit(solution)/shard_map/ppermute | solution.py:712
  269.0 25.5 %collective-permute-start.47 = (bf16[384,384]{1,0:T(8,128)(2,1)S(1)}, bf16[384,384]{1,0:T(8,128)(2,1)S(1)}, u32[]{:S(2)}, u32[]{:S(2)}) collective-permute-start(bf16[384,384]{1,0:T(8,128)(2,1)S(1)} %reduce_sum.67.refs_0_), channel_id=1, source_target_pairs={{0,20},{4,16},{16,4},{20,0},{1,21},{5,17},{17,5},{21,1},{2,22},{6,... | collective-permute-start | bytes 884744 | tf_op jit(solution)/shard_map/ppermute | solution.py:712
  289.5 14.5 %all-to-all-start.7 = ((bf16[8,48,384]{2,1,0:T(8,128)(2,1)}), bf16[8,48,384]{2,1,0:T(8,128)(2,1)}, u32[]{:S(2)}, u32[]{:S(2)}) async-start(bf16[8,48,384]{2,1,0:T(8,128)(2,1)} %bitcast.7), calls=%async_computation.7 | async-start | bytes 589824 | tf_op jit(solution)/shard_map/all_to_all | solution.py:800
  294.5 11.1 %collective-permute-start.51 = (bf16[384,384]{1,0:T(8,128)(2,1)S(1)}, bf16[384,384]{1,0:T(8,128)(2,1)}, u32[]{:S(2)}, u32[]{:S(2)}) collective-permute-start(bf16[384,384]{1,0:T(8,128)(2,1)S(1)} %collective-permute-done.47.refs_3_), channel_id=1, source_target_pairs={{0,8},{8,0},{1,9},{9,1},{2,10},{10,2},{3,11},{11,3},{4,12},{12,4},... | collective-permute-start | bytes 884744 | tf_op jit(solution)/shard_map/ppermute | solution.py:712
  294.9 11.5 %collective-permute-start.38 = (bf16[304,384]{1,0:T(8,128)(2,1)S(1)}, bf16[304,384]{1,0:T(8,128)(2,1)S(1)}, u32[]{:S(2)}, u32[]{:S(2)}) collective-permute-start(bf16[304,384]{1,0:T(8,128)(2,1)S(1)} %reduce_sum.66.refs_0_), channel_id=1, source_target_pairs={{0,4},{4,0},{16,20},{20,16},{1,5},{5,1},{17,21},{21,17},{2,6},{6,2... | collective-permute-start | bytes 700424 | tf_op jit(solution)/shard_map/ppermute | solution.py:712
  295.3 11.2 %collective-permute-start.39 = (bf16[304,384]{1,0:T(8,128)(2,1)S(1)}, bf16[304,384]{1,0:T(8,128)(2,1)S(1)}, u32[]{:S(2)}, u32[]{:S(2)}) collective-permute-start(bf16[304,384]{1,0:T(8,128)(2,1)S(1)} %reduce_sum.66.refs_0_), channel_id=1, source_target_pairs={{0,16},{4,20},{16,0},{20,4},{1,17},{5,21},{17,1},{21,5},{2,18},{6,... | collective-permute-start | bytes 700424 | tf_op jit(solution)/shard_map/ppermute | solution.py:712
  297.2 12.1 %collective-permute-start.40 = (bf16[304,384]{1,0:T(8,128)(2,1)S(1)}, bf16[304,384]{1,0:T(8,128)(2,1)S(1)}, u32[]{:S(2)}, u32[]{:S(2)}) collective-permute-start(bf16[304,384]{1,0:T(8,128)(2,1)S(1)} %reduce_sum.66.refs_0_), channel_id=1, source_target_pairs={{0,20},{4,16},{16,4},{20,0},{1,21},{5,17},{17,5},{21,1},{2,22},{6,... | collective-permute-start | bytes 700424 | tf_op jit(solution)/shard_map/ppermute | solution.py:712
  304.0 14.8 %collective-permute-start.37 = (bf16[8,48,384]{2,1,0:T(8,128)(2,1)}, bf16[8,48,384]{2,1,0:T(8,128)(2,1)S(1)}, u32[]{:S(2)}, u32[]{:S(2)}) collective-permute-start(bf16[8,48,384]{2,1,0:T(8,128)(2,1)} %all-to-all-done.7), channel_id=1, source_target_pairs={{0,0},{4,8},{8,4},{12,12},{1,1},{5,9},{9,5},{13,13},{2,2},{6,10},{... | collective-permute-start | bytes 884744 | tf_op jit(solution)/shard_map/ppermute | solution.py:723
  (85 other events, 598.3 us)

commit v3 on v2

--- a/solution.py
+++ b/solution.py
@@ -22,6 +22,11 @@
 EVERY = PLANE + ("tensor",)
 ACROSS = ("chip", "far", "near")
 FRAMES = ("far", "core")
+FEW = 8
+COSTS = {
+    "enter": 3, "first": 4, "between": 6, "second": 7, "hidden": 4, "hidden_rest": 5, "second_back": 9, "cross": 8,
+    "first_back": 10, "leave": 5, "exit": 2,
+}
 
 
 def wide_row(gain):
@@ -261,16 +266,18 @@
         who, off = divmod(start + at, each)
         n = min(each - off, values.shape[0] - at)
         part = values[at : at + n].astype(BF16)
-        stage[(who // half) ^ core, who % half, z, base + off : base + off + n, :] = part
+        rows = pl.ds(base + off if isinstance(base, int) else pl.multiple_of(base + off, 16), n)
+        stage[(who // half) ^ core, who % half, z, rows, :] = part
         at += n
 
 
 def store_columns(stage, each, tensor, start, values):
     rows = values.shape[0] // tensor
+    t = lax.axis_index("tensor")
     for z in range(tensor):
         for c in range(values.shape[1] // LANES):
             part = values[z * rows : (z + 1) * rows, c * LANES : (c + 1) * LANES]
-            store_rows(stage, each, z, start + c * rows, part)
+            store_rows(stage, each, z ^ t, start + c * rows, part)
     return start + values.shape[1] // LANES * rows
 
 
@@ -301,6 +308,7 @@
 
 
 def call(name, body, outs, vmem, smem=(), scratch=(), stage=None):
+    moved = COSTS.get(name, 4) * 3_000_000
     scratch = [pltpu.VMEM(shape, dtype) for shape, dtype in scratch]
     spaces = [pltpu.VMEM] * len(outs)
     if stage is not None:
@@ -316,6 +324,7 @@
         scratch_shapes=scratch,
         name=name,
         interpret=INTERPRET,
+        cost_estimate=pl.CostEstimate(flops=0, bytes_accessed=moved, transcendentals=0),
         compiler_params=pltpu.CompilerParams(vmem_limit_bytes=56 << 20),
     )(*smem, *vmem)
 
@@ -334,17 +343,18 @@
     pool_pair(plan, raw[:, x.shape[1] :], pools, squeeze, *pair)
 
 
-def pick_hidden(pieces, expand, reduce, up_ref, down_ref):
+def pick_hidden(tensor, expand, reduce, weights, up_ref, down_ref):
     up_ref[0] = expand[...]
     down_ref[0] = reduce[...]
     core, near = lax.axis_index("core"), lax.axis_index("near")
-    rows = pieces[0].shape[0]
+    rows = weights[0].shape[0] // (tensor - 1)
 
     def put(first, second):
-        for i, piece in enumerate(pieces):
-            k, n, c = i // 4 + 1, i // 2 % 2, i % 2
-            at = pl.multiple_of((n ^ near) * rows, 16)
-            (second if c else first)[k, pl.ds(at, rows), :] = piece[...]
+        for i, piece in enumerate(weights):
+            at = pl.multiple_of(((i % 2) ^ near) * rows, 16)
+            for k in range(1, tensor):
+                part = piece[(k - 1) * rows : k * rows, :]
+                (second if i // 2 else first)[k, pl.ds(at, rows), :] = part
 
     @pl.when(core == 0)
     def _():
@@ -369,10 +379,10 @@
 
 
 def between_body(plan, m_ref, l_ref, expand, reduce, *refs):
-    weights, refs = refs[: 4 * plan.tensor - 4], refs[4 * plan.tensor - 4 :]
+    weights, refs = refs[:4], refs[4:]
     gain_b, project_b, pool_b, squeeze_b, shortcut_b, y_ref, nb_ref, qb_ref, base_ref = refs[:9]
     pair, up_ref, down_ref = refs[9:-2], refs[-2], refs[-1]
-    pick_hidden(weights, expand, reduce, up_ref, down_ref)
+    pick_hidden(plan.tensor, expand, reduce, weights, up_ref, down_ref)
     l = l_ref[...]
     y = m_ref[...]
     for k in range(plan.tensor):
@@ -390,7 +400,7 @@
 
 def second_body(plan, heads, resets, videos, *refs):
     query, pairs, refs = refs[0], refs[1 : 1 + plan.sources], refs[1 + plan.sources :]
-    table, output, gain, base, cot, or_ref, m_ref, send_ref, probs_ref, table_ref = refs
+    table, output, gain, base, or_ref, m_ref, l_ref, probs_ref, table_ref = refs
     width = query.shape[1]
     scalars = clip_scalars(plan, resets, videos)
     keys, values = load_pairs(pairs, width)
@@ -398,44 +408,55 @@
     or_ref[...] = mixed_r
     middle = base[...] + mm(mixed_r, output[...])
     m_ref[...] = middle
-    send_ref[:, :width] = (norm(middle)[0] * wide_row(gain)).astype(BF16)
-    send_ref[:, width:] = cot[...]
-
-
-def hidden_body(each, rows, up, down, send_ref, keep, give, stage, sems):
-    width = up.shape[0]
-    l = rows[:, :width]
-    grad = rows[:, width:]
+    l_ref[...] = (norm(middle)[0] * wide_row(gain)).astype(BF16)
+
+
+def hidden_body(tensor, up, down, *refs):
+    rows, grads, refs = refs[:tensor], refs[tensor : 2 * tensor], refs[2 * tensor :]
+    sends, (hidden_ref, grad_pre_ref) = refs[:tensor], refs[tensor:]
+    l = jnp.concatenate([ref[...] for ref in rows], axis=0)
+    grad = jnp.concatenate([ref[...] for ref in grads], axis=0)
     gate, slope = gelu_both(mm(l, up[...]))
-    hidden = gate.astype(BF16)
-    send_ref[:, :width] = mm(hidden, down[...]).astype(BF16)
+    hidden_ref[...] = gate.astype(BF16)
     grad_pre = (slope * mm_tr(grad, down[...])).astype(BF16)
-    send_ref[:, width:] = mm_tr(grad_pre, up[...]).astype(BF16)
-    grad_up = mm_tl(l, grad_pre)
-    grad_down = mm_tl(hidden, grad)
+    grad_pre_ref[...] = grad_pre
+    for ref, part in zip(sends, blocks(mm_tr(grad_pre, up[...]), tensor)):
+        ref[...] = part.astype(BF16)
+
+
+def hidden_rest_body(tensor, each, down, hidden_ref, grad_pre_ref, *refs):
+    rows, grads, refs = refs[:tensor], refs[tensor : 2 * tensor], refs[2 * tensor :]
+    sends, (keep, give, stage, sems) = refs[:tensor], refs[tensor:]
+    hidden, grad_pre = hidden_ref[...], grad_pre_ref[...]
+    l = jnp.concatenate([ref[...] for ref in rows], axis=0)
+    grad = jnp.concatenate([ref[...] for ref in grads], axis=0)
     at = 0
-    for whole in (grad_up, grad_down):
+    for whole in (mm_tl(l, grad_pre), mm_tl(hidden, grad)):
         for c in range(whole.shape[1] // LANES):
             part = whole[:, c * LANES : (c + 1) * LANES]
             store_rows(stage, each, 0, at, part)
             at += part.shape[0]
+    for ref, part in zip(sends, blocks(mm(hidden, down[...]), tensor)):
+        ref[...] = part.astype(BF16)
     send_stage(stage, keep, give, sems)
+
+
+def sum_refs(refs):
+    total = refs[0][...].astype(F32)
+    for ref in refs[1:]:
+        total = total + ref[...].astype(F32)
+    return total
 
 
 def second_back_body(plan, heads, resets, videos, *refs):
     refs = list(refs)
-    sums, cot, middle, gain, mixed, output, query, probs = refs[:8]
-    pairs, refs = refs[8 : 8 + plan.sources], refs[8 + plan.sources :]
-    out_ref, dm_ref, dgain_ref = refs[:3]
-    refs = refs[3:]
-    width = query.shape[1]
-    total = sums[0].astype(F32)
-    for z in range(1, plan.tensor):
-        total = total + sums[z].astype(F32)
-    m = middle[...]
-    out_ref[...] = (m + total[:, :width]).astype(BF16)
-    normed, inverse = norm(m)
-    grad, dgain = norm_back(total[:, width:], wide_row(gain), normed, inverse)
+    sums, refs = refs[: plan.tensor], refs[plan.tensor :]
+    cot, middle, gain, mixed, output, query, probs = refs[:7]
+    pairs, refs = refs[7 : 7 + plan.sources], refs[7 + plan.sources :]
+    dm_ref, dgain_ref = refs[:2]
+    refs = refs[2:]
+    normed, inverse = norm(middle[...])
+    grad, dgain = norm_back(sum_refs(sums), wide_row(gain), normed, inverse)
     dgain_ref[...] = dgain
     grad = cot[...].astype(F32) + grad
     dm_ref[...] = grad
@@ -551,24 +572,22 @@
         return taken
 
     dy_ref, m_ref, l_ref, gain, mixed, output, query, probs, expand, reduce = take(10)
-    weights = take(4 * plan.tensor - 4)
+    weights = take(4)
     pairs = take(plan.sources)
     dgain_ref, dm_out = take(2)
     refs, (keep, give, up_ref, down_ref, bias_ref, stage, sems) = refs[:-7], refs[-7:]
     tensor = plan.tensor
-    pick_hidden(weights, expand, reduce, up_ref, down_ref)
+    pick_hidden(tensor, expand, reduce, weights, up_ref, down_ref)
     grad_y = dy_ref[...]
     grad_r = grad_y.astype(BF16)
     l = l_ref[...]
-    t = lax.axis_index("tensor")
     grad_l = None
     for k in range(tensor):
         gate, slope = gelu_both(mm(l, up_ref[k]))
         hidden = gate.astype(BF16)
         grad_pre = (slope * mm_tr(grad_r, down_ref[k])).astype(BF16)
-        z = t ^ k
-        store_rows(stage, each, z, 0, mm_tl(l, grad_pre))
-        store_rows(stage, each, z, l.shape[1], mm_tl(hidden, grad_r))
+        store_rows(stage, each, k, 0, mm_tl(l, grad_pre))
+        store_rows(stage, each, k, l.shape[1], mm_tl(hidden, grad_r))
         back = mm_tr(grad_pre, up_ref[k])
         grad_l = back if grad_l is None else grad_l + back
     normed, inverse = norm(m_ref[...])
@@ -582,10 +601,11 @@
 
 def store_tail(stage, each, tensor, start, values):
     rows = values.shape[0] // tensor
+    t = lax.axis_index("tensor")
     for z in range(tensor):
         for c in range(values.shape[1] // LANES):
             part = values[z * rows : (z + 1) * rows, c * LANES : (c + 1) * LANES]
-            store_rows(stage, each, 0, start + c * rows, part, z * each)
+            store_rows(stage, each, 0, start + c * rows, part, (z ^ t) * each)
     return start + values.shape[1] // LANES * rows
 
 
@@ -619,13 +639,13 @@
 
 def unpack_body(groups, *refs):
     core, across = lax.axis_index("core"), across_index()
-    half = refs[-1].shape[1]
-    pieces, refs = refs[: 2 * half], refs[2 * half :]
+    pieces, refs = refs[:2], refs[2:]
     count = sum(n for _, n in groups)
     outs, small, whole = refs[:count], refs[count:-1], refs[-1]
     sums, small = (small[-1], small[:-1]) if small else (None, small)
     for i, ref in enumerate(pieces):
-        whole[(i // half) ^ core, (i % half) ^ across] = ref[...]
+        for k in range(ref.shape[0]):
+            whole[i ^ core, k ^ across] = ref[k]
     base, first = 0, 0
     for each, n in groups:
         at = 0
@@ -658,11 +678,11 @@
     refs = list(refs)
     pieces = plan.returned
     grads, refs = refs[:pieces], refs[pieces:]
-    (dq, dm, doutput, n_ref, x_ref, gain, project, pools, squeeze, order, out,
-     dgain_mid, dtable, dgain_b, dpool_b, dsqueeze_b, dmid_b, dtable_b) = refs[:18]
-    refs = refs[18:]
+    (dq, dm, doutput, n_ref, x_ref, gain, project, pools, squeeze,
+     dgain_mid, dtable, dgain_b, dpool_b, dsqueeze_b, dmid_b, dtable_b) = refs[:16]
+    refs = refs[16:]
     given = refs.pop(0) if not plan.local_squeeze else None
-    send_ref, keep, give, dpool_ref, dsqueeze_ref, sum_ref, stage, sems = refs
+    grad_ref, keep, give, dpool_ref, dsqueeze_ref, sum_ref, stage, sems = refs
     tensor = plan.tensor
     width = x_ref.shape[1]
     n = n_ref[...]
@@ -679,9 +699,7 @@
     store_tail(stage, each, tensor, at, doutput[...])
     normed, inverse = norm(x_ref[...].astype(F32))
     grad_x, dgain = norm_back(grad_n, wide_row(gain), normed, inverse)
-    grad_x = (grad_x + dm[...]).astype(BF16)
-    leaving = jnp.concatenate([grad_x, out[:, :width], out[:, width:]], axis=0)
-    send_ref[...] = mm_tl(order[...], leaving).astype(BF16)
+    grad_ref[...] = (grad_x + dm[...]).astype(BF16)
     sum_ref[...] = jnp.zeros(sum_ref.shape, F32)
     squeeze_a = dsqueeze_ref if given is None else given
     sum_ref[0:1, :] = dgain
@@ -700,6 +718,14 @@
     sum_ref[80:88, :128] = dtable_b[...]
     store_rows(stage, small_each, 0, 0, sum_ref[...], tensor * each)
     send_stage(stage, keep, give, sems)
+
+
+def exit_body(order, grad_x, middle_b, *refs):
+    outs, send_ref = refs[:-1], refs[-1]
+    width = grad_x.shape[1]
+    out = (middle_b[...] + sum_refs(outs)).astype(BF16)
+    leaving = jnp.concatenate([grad_x[...], out[:, :width], out[:, width:]], axis=0)
+    send_ref[...] = mm_tl(order[...], leaving).astype(BF16)
 
 
 def exchange(values, axes, by):
@@ -792,8 +818,19 @@
     return [both[0]] + received, jnp.stack([sums[:, :width], sums[:, width:]])
 
 
+def add_all(parts):
+    total = parts[0].astype(F32)
+    for part in parts[1:]:
+        total = total + part.astype(F32)
+    return total.astype(BF16)
+
+
 def sum_first(values):
-    return jnp.sum(values.astype(F32), axis=0).astype(BF16)
+    return add_all([values[k] for k in range(values.shape[0])])
+
+
+def everyone(values, axis):
+    return [values[0]] + [exchange(values[k], axis, k) for k in range(1, lax.axis_size(axis))]
 
 
 def spread(values, axes):
@@ -804,13 +841,41 @@
     return lax.optimization_barrier((value, others))[0]
 
 
+def sum_pair(keep, other):
+    return (keep.astype(F32) + other.astype(F32)).astype(BF16)
+
+
 def sum_cores(keep, give):
-    return (keep.astype(F32) + to_core(give).astype(F32)).astype(BF16)
+    return sum_pair(keep, to_core(give))
+
+
+def scatter(values):
+    count = lax.axis_size(ACROSS)
+    if count > FEW:
+        values = spread(values, ACROSS)
+        return [values[k] for k in range(count)]
+    parts = [lax.dynamic_index_in_dim(values, across_index() ^ k, keepdims=False) for k in range(count)]
+    return [exchange(part, ACROSS, k) if k else part for k, part in enumerate(parts)]
+
+
+def gather_across(values):
+    return jnp.stack([exchange(values, ACROSS, k) if k else values for k in range(lax.axis_size(ACROSS))])
 
 
 def gather_plane(values):
-    mine = [exchange(values, ACROSS, k) if k else values for k in range(lax.axis_size(ACROSS))]
-    return mine + [to_core(each) for each in mine]
+    values = gather_across(values)
+    return [values, to_core(values)]
+
+
+def halve(values, axis):
+    for bit in range(log2(lax.axis_size(axis))):
+        values = values.reshape(-1, 2, *values.shape[1:])
+        values = sum_pair(values[:, 0], exchange(values[:, 1], axis, 1 << bit))
+    return values[0]
+
+
+def both_cores(values):
+    return [values, to_core(values)]
 
 
 def padded(rows, parts):
@@ -835,10 +900,10 @@
     )
     arrived = spread(swap(leaving), home)
     half = jnp.where(core == 0, expand_a, reduce_a)
-    half, arrived = lax.optimization_barrier((half, arrived))
+    quarter = half.reshape(2, -1, half.shape[1])[lax.axis_index("near")]
+    quarter, arrived = lax.optimization_barrier((quarter, arrived))
+    mine = [exchange(quarter, "tensor", k) for k in range(1, tensor)]
     arrived = arrived.reshape(-1, width)
-    quarter = half.reshape(2, -1, half.shape[1])[lax.axis_index("near")]
-    mine = [exchange(quarter, "tensor", k) for k in range(1, tensor)]
     pair = lambda w: [((pooled, 2 * w), BF16)] + [((memory // seq, 2 * w), BF16)] * plan.local_squeeze
     x, cot, n_a, q_a, *pair_a = call(
         "enter",
@@ -849,6 +914,12 @@
     )
     pairs_a = share_pairs(plan, pair_a, squeeze_a)
     hidden = [((tensor, width, expand_a.shape[1]), BF16), ((tensor, reduce_a.shape[0], width), BF16)]
+    mine, pairs_a[1] = lax.optimization_barrier((mine, pairs_a[1]))
+    mine = jnp.concatenate(mine, axis=0)
+    weights = [mine, exchange(mine, "near", 1)]
+    weights, cots, pairs_a = lax.optimization_barrier((weights, cot, pairs_a))
+    weights = weights + [to_core(each) for each in weights]
+    cots = [cot] + [exchange(cots, "tensor", k) for k in range(1, tensor)]
     or_a, m_a, l_a, probs_a = call(
         "first",
         functools.partial(first_body, plan, heads_a),
@@ -857,11 +928,7 @@
         [resets, videos],
         [((8, 128), F32)],
     )
-    mine, pairs_a = lax.optimization_barrier((mine, pairs_a))
-    weights = []
-    for each in mine:
-        other = exchange(each, "near", 1)
-        weights += [each, to_core(each), other, to_core(other)]
+    m_a, cots = lax.optimization_barrier((m_a, cots))
     y_a, n_b, q_b, base, *pair_b = call(
         "between",
         functools.partial(between_body, plan),
@@ -871,45 +938,40 @@
         hidden,
     )
     pairs_b = share_pairs(plan, pair_b, squeeze_b)
-    or_b, m_b, rows_b, probs_b = call(
+    or_b, m_b, l_b, probs_b = call(
         "second",
         functools.partial(second_body, plan, heads_b),
-        [((pooled, wide), BF16), ((pooled, wide), F32), ((pooled, 2 * wide), BF16),
-         ((heads_b * pooled, keys), BF16)],
-        [q_b, *pairs_b, offsets_b, output_b, mixer_gain_b, base, cot],
+        [((pooled, wide), BF16), ((pooled, wide), F32), ((pooled, wide), BF16), ((heads_b * pooled, keys), BF16)],
+        [q_b, *pairs_b, offsets_b, output_b, mixer_gain_b, base],
         [resets, videos],
         [((8, 128), F32)],
     )
-    rows_all = lax.all_gather(rows_b, "tensor", axis=0, tiled=True)
+    rows_b = [exchange(l_b, "tensor", k) if k else l_b for k in range(tensor)]
     hidden_rows = (expand_b.shape[1] // LANES) * wide + (wide // LANES) * reduce_b.shape[0]
     half_plane = plane // 2
     hidden_each = padded(hidden_rows, plane)
-    shares, keep, give = call(
+    units = ((tensor * pooled, expand_b.shape[1]), BF16)
+    *shares, hidden_b, grad_pre_b = call(
         "hidden",
-        functools.partial(hidden_body, hidden_each),
-        [((tensor * pooled, 2 * wide), BF16)],
-        [rows_all, expand_b, reduce_b],
-        stage=(2, half_plane, 1, hidden_each, LANES),
-    )
-    sums = spread(shares, "tensor")
-    early = spread(after(sum_cores(keep, give), sums), ACROSS)
-    sums = sums.reshape(tensor, pooled, 2 * wide)
+        functools.partial(hidden_body, tensor),
+        [((pooled, wide), BF16)] * tensor + [units, units],
+        [expand_b, reduce_b, *rows_b, *cots],
+    )
+    sums = everyone(shares, "tensor")
     bias = lambda: [((plan.frames, 8, keys), F32)]
     key_grads = lambda w: (
         [((pooled, 2 * w), F32)] + [((pooled, 2 * w), BF16)] * (seq - 1) + [((memory, 2 * w), BF16)] * 2
     )
-    out, dm_b, dmid_b, doutput_b, dq_b, dtable_b, *back = call(
+    dm_b, dmid_b, doutput_b, dq_b, dtable_b, *back = call(
         "second_back",
         functools.partial(second_back_body, plan, heads_b),
-        [((pooled, wide), BF16), ((pooled, wide), F32), ((1, wide), F32), ((wide, wide), BF16), ((pooled, wide), F32),
+        [((pooled, wide), F32), ((1, wide), F32), ((wide, wide), BF16), ((pooled, wide), F32),
          ((8, 128), F32), *key_grads(wide)],
-        [sums, cot, m_b, mixer_gain_b, or_b, output_b, q_b, probs_b, *pairs_b],
+        [*sums, cot, m_b, mixer_gain_b, or_b, output_b, q_b, probs_b, *pairs_b],
         [resets, videos],
         bias(),
     )
     pieces, dsqueeze_given = return_pairs(plan, back, pairs_b, squeeze_b)
-    dq_b = after(dq_b, early)
-    early = gather_plane(sum_first(early)[0])
     share = width // tensor
     cross_each = padded((3 + 1) * wide // LANES * share + wide // LANES * (wide // tensor), plane)
     dy_a, dpool_b, dsqueeze_b, dgain_b, keep, give = call(
@@ -919,7 +981,20 @@
         [*pieces, dq_b, dm_b, doutput_b, n_b, y_a, attend_gain_b, project_b, pooling_b, squeeze_b, shortcut_b],
         stage=(2, half_plane, tensor, cross_each, LANES),
     )
-    cross = spread(sum_cores(keep, give), ACROSS)
+    cross = (keep, give)
+    hidden_b = after(hidden_b, dgain_b)
+    *out_shares, keep, give = call(
+        "hidden_rest",
+        functools.partial(hidden_rest_body, tensor, hidden_each),
+        [((pooled, wide), BF16)] * tensor,
+        [reduce_b, hidden_b, grad_pre_b, *rows_b, *cots],
+        stage=(2, half_plane, 1, hidden_each, LANES),
+    )
+    early = (keep, give)
+    early, cross = sum_cores(*early), sum_cores(*cross)
+    early = [part.reshape(half_plane, -1, LANES) for part in (early, cross)]
+    early, dy_a = lax.optimization_barrier((jnp.concatenate(early, axis=1), dy_a))
+    early = spread(early, ACROSS)
     first_each = padded(2 * width, plane)
     dmid_a, dm_a, doutput_a, dq_a, dtable_a, *back, keep, give = call(
         "first_back",
@@ -932,58 +1007,69 @@
         hidden + bias(),
         stage=(2, half_plane, tensor, first_each, LANES),
     )
-    first = spread(after(sum_cores(keep, give), cross), ACROSS)
-    grad_expand_b, grad_reduce_b = call(
-        "unpack_early",
-        functools.partial(unpack_body, [(hidden_each, 2)]),
-        [(expand_b.shape, F32), (reduce_b.shape, F32)],
-        early,
-        (),
-        [((2, half_plane, hidden_each, LANES), BF16)],
-    )
     if dsqueeze_given is not None:
         dsqueeze_b = dsqueeze_given
     pieces, dsqueeze_given = return_pairs(plan, back, pairs_a, squeeze_a)
+    out_sums = everyone(out_shares, "tensor")
+    early, dq_a, out_sums = lax.optimization_barrier((early, dq_a, out_sums))
+    first = sum_cores(keep, give)
     tail_each, small_each = padded(4 * share, plane), padded(128, plane)
-    leaving, keep, give = call(
+    grad_x, keep, give = call(
         "leave",
         functools.partial(leave_body, plan, tail_each, small_each),
-        [(arrived.shape, BF16)],
-        [*pieces, dq_a, dm_a, doutput_a, n_a, x, attend_gain_a, project_a, pooling_a, squeeze_a, order, out,
-         dmid_a, dtable_a, dgain_b, dpool_b, dsqueeze_b, dmid_b, dtable_b]
+        [((tokens, width), BF16)],
+        [*pieces, dq_a, dm_a, doutput_a, n_a, x, attend_gain_a, project_a, pooling_a, squeeze_a, dmid_a, dtable_a,
+         dgain_b, dpool_b, dsqueeze_b, dmid_b, dtable_b]
         + ([] if dsqueeze_given is None else [dsqueeze_given]),
         (),
         [((2, 4, width), F32), ((2, 4, width), F32), ((128, LANES), F32)],
         stage=(2, half_plane, 1, tensor * tail_each + small_each, LANES),
     )
-    last = spread(after(sum_cores(keep, give), first), ACROSS)
-    cross, first = sum_first(cross), sum_first(first)
-    last = sum_first(last)[0]
-    small = jnp.broadcast_to(last[None, tensor * tail_each :], (tensor, small_each, LANES))
-    last = last[: tensor * tail_each].reshape(tensor, tail_each, LANES)
-    last = spread(jnp.concatenate([cross, first, last, small], axis=1), "tensor")
+    last = sum_cores(keep, give)
+    last = jnp.concatenate([first.reshape(half_plane, -1, LANES), last[:, 0]], axis=1)
+    leaving, = call("exit", exit_body, [(arrived.shape, BF16)], [order, after(grad_x, last), m_b, *out_sums])
+    last = spread(last, ACROSS)
+    early = sum_first(early)
+    cross = halve(early[hidden_each:].reshape(tensor, cross_each, LANES), "tensor")
+    early = gather_across(jnp.concatenate([early[:hidden_each], cross], axis=0))
+    last, cross, leaving = lax.optimization_barrier((last, cross, leaving))
+    last = sum_first(last)
+    first_rows = tensor * first_each
+    first = last[:first_rows].reshape(tensor, first_each, LANES)
+    small = jnp.broadcast_to(last[None, first_rows + tensor * tail_each :], (tensor, small_each, LANES))
+    last = last[first_rows : first_rows + tensor * tail_each].reshape(tensor, tail_each, LANES)
+    last = jnp.concatenate([first, last, small], axis=1)
     leaving = after(leaving, last)
-    late = gather_plane(sum_first(last))
+    last = gather_across(halve(last, "tensor"))
     returned = swap(spread(leaving.reshape(plan.group, -1, width), home))
     x_rows = plan.frames * plan.rows * plan.cols
     grad_input = returned[:, :x_rows].reshape(clips_in.shape).astype(F32)
     result = returned[:, x_rows:].reshape(cotangent.shape).astype(F32)
+    early, last, grad_input, result = lax.optimization_barrier((early, last, grad_input, result))
+    early, last = both_cores(early), both_cores(last)
     column = lambda rows, columns: ((rows, columns), F32)
-    (
-        grad_project_b, grad_shortcut_b, grad_output_b, grad_expand_a, grad_reduce_a, grad_project_a, grad_output_a,
-        *small,
-    ) = call(
-        "unpack",
-        functools.partial(unpack_body, [(cross_each, 3), (first_each, 2), (tail_each, 2)]),
+    grad_expand_b, grad_reduce_b, grad_project_b, grad_shortcut_b, grad_output_b = call(
+        "unpack_early",
+        functools.partial(unpack_body, [(hidden_each, 2), (cross_each, 3)]),
         [
-            column(share, 3 * wide), column(share, wide), column(wide // tensor, wide), (expand_a.shape, F32),
-            (reduce_a.shape, F32), column(share, 3 * width), column(share, width),
+            (expand_b.shape, F32), (reduce_b.shape, F32),
+            column(share, 3 * wide), column(share, wide), column(wide // tensor, wide),
+        ],
+        early,
+        (),
+        [((2, half_plane, hidden_each + cross_each, LANES), BF16)],
+    )
+    grad_expand_a, grad_reduce_a, grad_project_a, grad_output_a, *small = call(
+        "unpack_last",
+        functools.partial(unpack_body, [(first_each, 2), (tail_each, 2)]),
+        [
+            (expand_a.shape, F32), (reduce_a.shape, F32), column(share, 3 * width), column(share, width),
             ((width,), F32), (pooling_a.shape, F32), (squeeze_a.shape, F32), (offsets_a.shape, F32), ((width,), F32),
             ((width,), F32), (pooling_b.shape, F32), (squeeze_b.shape, F32), (offsets_b.shape, F32), ((wide,), F32),
         ],
-        late,
+        last,
         (),
-        [((128, LANES), F32), ((2, half_plane, cross_each + first_each + tail_each + small_each, LANES), BF16)],
+        [((128, LANES), F32), ((2, half_plane, first_each + tail_each + small_each, LANES), BF16)],
     )
     return (
         result,

time: 322 us -> 300 us (0.932)
  blocking collectives: 24.8 us -> 0 us
  waiting for transfers between devices: 116 us -> 110 us
  local copies, waits for them, and re-layouts: 7.99 us -> 13.5 us
  Pallas kernels: 67.3 us -> 71.4 us
    all_to_all x8 -> x4, waiting for transfers between devices: 79.5 us -> 30.4 us  [spread(): return lax.all_to_all(values, axes, 0, 0, tiled=True)]
    ppermute x42 -> x46, waiting for transfers between devices: 16.5 us -> 63.6 us  [exchange(): lax.ppermute(values, tuple(order), [(i, int(where[p ^ by])) for i, p in e...]
    all_gather x1 -> x0, blocking collectives: 24.8 us -> none  [local(): rows_all = lax.all_gather(rows_b, 'tensor', axis=0, tiled=True)]
    ppermute x42 -> x46, starting transfers between devices: 23.5 us -> 41.7 us  [exchange(): lax.ppermute(values, tuple(order), [(i, int(where[p ^ by])) for i, p in e...]
    all_to_all x8 -> x4, starting transfers between devices: 44.4 us -> 29.7 us  [spread(): return lax.all_to_all(values, axes, 0, 0, tiled=True)]
    convert_element_type x4 -> x3, other arithmetic: 7.78 us -> 2.13 us  [sum_pair(): return (keep.astype(F32) + other.astype(F32)).astype(BF16)]
    unnamed x114 -> x104, local copies, waits for them, and re-layouts: 4.29 us -> 8.59 us
    pallas_call x11 -> x13, Pallas kernels: 67.3 us -> 71.4 us  [call(): pl.pallas_call(body, out_shape=[jax.ShapeDtypeStruct(shape, dtype) for sh...]
  transfers between devices with their start and end apart: 60 -> 60, of which waited for: 23 -> 32; matrix products, arithmetic and copies ran while one was open for 3% -> 2% of each run, Pallas kernels for 12% -> 11%
where the time goes in v3:
time: 300 us; the launch traced here: 299 us
  waiting for transfers between devices  110 us (37%)
  starting transfers between devices  91.3 us (30%)
  Pallas kernels  71.4 us (24%)
  local copies, waits for them, and re-layouts  13.5 us (4%)
  other arithmetic  11 us (4%)
    pallas_call x13, Pallas kernels, call(): pl.pallas_call(body, out_shape=[jax.ShapeDtypeStruct(shape, dtype) for sh...  71.4 us
    ppermute x46, waiting for transfers between devices, exchange(): lax.ppermute(values, tuple(order), [(i, int(where[p ^ by])) for i, p in e...  63.6 us
    ppermute x46, starting transfers between devices, exchange(): lax.ppermute(values, tuple(order), [(i, int(where[p ^ by])) for i, p in e...  41.7 us
    all_to_all x4, waiting for transfers between devices, spread(): return lax.all_to_all(values, axes, 0, 0, tiled=True)  30.4 us
    all_to_all x4, starting transfers between devices, spread(): return lax.all_to_all(values, axes, 0, 0, tiled=True)  29.7 us
    ppermute x8, starting transfers between devices, shift(): return lax.ppermute(values, EVERY, pairs)  17.8 us
    ppermute x8, waiting for transfers between devices, shift(): return lax.ppermute(values, EVERY, pairs)  16.3 us
    unnamed x104, local copies, waits for them, and re-layouts  8.59 us
  transfers between devices with their start and end apart: 60, of which 32 were waited for; matrix products, arithmetic and copies ran while one was open for 2% of the time, Pallas kernels for 11%

profile of v3, /device:TPU:0, one launch (start us, length us, event | category | flops | bytes accessed | tf_op | source)
XLA Modules:
  0.0 299.0 jit_solution(13439611612173880383)
XLA Ops:
  4.1 12.6 %all-to-all-start = ((bf16[8,48,384]{2,1,0:T(8,128)(2,1)}), bf16[8,48,384]{2,1,0:T(8,128)(2,1)S(1)}, u32[]{:S(2)}, u32[]{:S(2)}) async-start(bf16[8,48,384]{2,1,0:T(8,128)(2,1)} %collective-permute-done), calls=%async_computation | async-start | bytes 589824 | tf_op jit(solution)/shard_map/all_to_all | solution.py:837
  16.8 10.3 %all-to-all-done = bf16[8,48,384]{2,1,0:T(8,128)(2,1)S(1)} async-done(((bf16[8,48,384]{2,1,0:T(8,128)(2,1)}), bf16[8,48,384]{2,1,0:T(8,128)(2,1)S(1)}, u32[]{:S(2)}, u32[]{:S(2)}) %all-to-all-start) | async-done | bytes 294944 | tf_op jit(solution)/shard_map/all_to_all | solution.py:837
  36.0 5.1 %collective-permute-done.2 = bf16[192,384]{1,0:T(8,128)(2,1)S(1)} collective-permute-done((bf16[192,384]{1,0:T(8,128)(2,1)S(1)}, bf16[192,384]{1,0:T(8,128)(2,1)S(1)}, u32[]{:S(2)}, u32[]{:S(2)}) %collective-permute-start.2) | collective-permute-done | bytes 147488 | tf_op jit(solution)/shard_map/ppermute | solution.py:738
  45.1 3.8 %collective-permute-start.6 = (bf16[16,768]{1,0:T(8,128)(2,1)}, bf16[16,768]{1,0:T(8,128)(2,1)S(1)}, u32[]{:S(2)}, u32[]{:S(2)}) collective-permute-start(bf16[16,768]{1,0:T(8,128)(2,1)} %get-tuple-element.147), channel_id=1, source_target_pairs={{0,1},{8,9},{1,2},{9,10},{2,3},{10,11},{3,4},{11,12},{4,5},{12,13}... | collective-permute-start | bytes 73736 | tf_op jit(solution)/shard_map/ppermute | solution.py:767
  58.4 4.1 %first.1 = (bf16[256,384]{1,0:T(8,128)(2,1)}, f32[256,384]{1,0:T(8,128)}, bf16[256,384]{1,0:T(8,128)(2,1)}, bf16[1024,192]{1,0:T(8,128)(2,1)}) custom-call(s32[16]{0:T(128)} %resets.7, s32[16]{0:T(128)} %videos.7, bf16[256,384]{1,0:T(8,128)(2,1)} %get-tuple-element.138.refs_0_.refs_10_, bf16[256,384]{1,0:T(8,128)(2,1)} %get-tuple-element.139.refs_1_.refs_6_, ...), custom_call_target="tpu_custom_call" | custom-call | bytes 12000000 | tf_op jit(solution)/shard_map/first/pallas_call | solution.py:318
  66.5 6.2 %between.1 = (f32[256,384]{1,0:T(8,128)}, bf16[256,384]{1,0:T(8,128)(2,1)}, bf16[64,768]{1,0:T(8,128)(2,1)}, f32[64,768]{1,0:T(8,128)}, bf16[64,1536]{1,0:T(8,128)(2,1)}, /*index=5*/bf16[16,1536]{1,0:T(8,128)(2,1)}) custom-call(f32[256,384]{1,0:T(8,128)} %get-tuple-element.156.m_ref.refs_1_, bf16[256,384]{1,0:T(8,128)(2,1)} %get-tuple-element.157.l_ref.refs_2_, ...), custom_call_target="tpu_custom_call" | custom-call | bytes 18000000 | tf_op jit(solution)/shard_map/between/pallas_call | solution.py:318
  74.6 4.7 %collective-permute-start.16 = (bf16[16,1536]{1,0:T(8,128)(2,1)}, bf16[16,1536]{1,0:T(8,128)(2,1)S(1)}, u32[]{:S(2)}, u32[]{:S(2)}) collective-permute-start(bf16[16,1536]{1,0:T(8,128)(2,1)} %get-tuple-element.162), channel_id=1, source_target_pairs={{0,1},{8,9},{1,2},{9,10},{2,3},{10,11},{3,4},{11,12},{4,5},{12,13}... | collective-permute-start | bytes 147464 | tf_op jit(solution)/shard_map/ppermute | solution.py:767
  83.1 7.2 %second.1 = (bf16[64,768]{1,0:T(8,128)(2,1)}, f32[64,768]{1,0:T(8,128)}, bf16[64,768]{1,0:T(8,128)(2,1)}, bf16[512,192]{1,0:T(8,128)(2,1)}) custom-call(s32[16]{0:T(128)} %resets.7, s32[16]{0:T(128)} %videos.7, bf16[64,768]{1,0:T(8,128)(2,1)} %get-tuple-element.160.refs_0_.refs_9_, bf16[64,1536]{1,0:T(8,128)(2,1)} %get-tuple-element.161.refs_1_.refs_11_, ...), custom_call_target="tpu_custom_call" | custom-call | bytes 21000000 | tf_op jit(solution)/shard_map/second/pallas_call | solution.py:318
  90.2 3.8 %collective-permute-start.22 = (bf16[64,768]{1,0:T(8,128)(2,1)}, bf16[64,768]{1,0:T(8,128)(2,1)S(1)}, u32[]{:S(2)}, u32[]{:S(2)}) collective-permute-start(bf16[64,768]{1,0:T(8,128)(2,1)} %get-tuple-element.164.refs_0_), channel_id=1, source_target_pairs={{0,3},{1,2},{2,1},{3,0},{4,7},{5,6},{6,5},{7,4},{8,11},{9,10},{10,... | collective-permute-start | bytes 294920 | tf_op jit(solution)/shard_map/ppermute | solution.py:738
  97.6 6.1 %collective-permute-done.21.refs_2_ = bf16[64,768]{1,0:T(8,128)(2,1)S(1)} collective-permute-done((bf16[64,768]{1,0:T(8,128)(2,1)}, bf16[64,768]{1,0:T(8,128)(2,1)S(1)}, u32[]{:S(2)}, u32[]{:S(2)}) %collective-permute-start.21) | collective-permute-done | bytes 98336 | tf_op jit(solution)/shard_map/ppermute | solution.py:738
  105.0 3.9 %hidden.1 = (bf16[64,768]{1,0:T(8,128)(2,1)}, bf16[64,768]{1,0:T(8,128)(2,1)}, bf16[64,768]{1,0:T(8,128)(2,1)}, bf16[64,768]{1,0:T(8,128)(2,1)}, bf16[256,768]{1,0:T(8,128)(2,1)}, /*index=5*/bf16[256,768]{1,0:T(8,128)(2,1)}) custom-call(bf16[768,768]{1,0:T(8,128)(2,1)} %up.1, bf16[768,768]{1,0:T(8,128)(2,1)} %down.3, ...), custom_call_target="tpu_custom_call" | custom-call | bytes 12000000 | tf_op jit(solution)/shard_map/hidden/pallas_call | solution.py:318
  115.1 5.3 %collective-permute-done.24.refs_2_ = bf16[64,768]{1,0:T(8,128)(2,1)S(1)} collective-permute-done((bf16[64,768]{1,0:T(8,128)(2,1)}, bf16[64,768]{1,0:T(8,128)(2,1)S(1)}, u32[]{:S(2)}, u32[]{:S(2)}) %collective-permute-start.24) | collective-permute-done | bytes 98336 | tf_op jit(solution)/shard_map/ppermute | solution.py:738
  121.1 9.0 %second_back.1 = (f32[64,768]{1,0:T(8,128)}, f32[1,768]{1,0:T(1,128)}, bf16[768,768]{1,0:T(8,128)(2,1)}, f32[64,768]{1,0:T(8,128)}, f32[8,128]{1,0:T(8,128)}, /*...) custom-call(s32[16]{0:T(128)} %resets.7, s32[16]{0:T(128)} %videos.7, ...), custom_call_target="tpu_custom_call" | custom-call | bytes 27000000 | tf_op jit(solution)/shard_map/second_back/pallas_call | solution.py:318
  133.0 4.5 %collective-permute-done.27.refs_2_ = bf16[32,1536]{1,0:T(8,128)(2,1)S(1)} collective-permute-done((bf16[32,1536]{1,0:T(8,128)(2,1)}, bf16[32,1536]{1,0:T(8,128)(2,1)S(1)}, u32[]{:S(2)}, u32[]{:S(2)}) %collective-permute-start.27) | collective-permute-done | bytes 98336 | tf_op jit(solution)/shard_map/ppermute | solution.py:767
  137.5 4.2 %collective-permute-done.29.refs_4_ = bf16[32,1536]{1,0:T(8,128)(2,1)S(1)} collective-permute-done((bf16[32,1536]{1,0:T(8,128)(2,1)}, bf16[32,1536]{1,0:T(8,128)(2,1)S(1)}, u32[]{:S(2)}, u32[]{:S(2)}) %collective-permute-start.29) | collective-permute-done | bytes 98336 | tf_op jit(solution)/shard_map/ppermute | solution.py:767
  143.7 8.2 %cross.1 = (f32[256,384]{1,0:T(8,128)}, f32[3,4,768]{2,1,0:T(4,128)}, f32[2,4,768]{2,1,0:T(4,128)}, f32[1,384]{1,0:T(1,128)}, bf16[4,4,144,384]{3,2,1,0:T(8,128)(2,1)}, /*index=5*/bf16[4,4,144,384]{3,2,1,0:T(8,128)(2,1)}) custom-call(f32[64,1536]{1,0:T(8,128)} %get-tuple-element.177.refs_0_, bf16[64,1536]{1,0:T(8,128)(2,1)} %copy-done.24, ...), custom_call_target="tpu_custom_call" | custom-call | bytes 24000000 | tf_op jit(solution)/shard_map/cross/pallas_call | solution.py:318
  152.1 4.8 %hidden_rest.1 = (bf16[64,768]{1,0:T(8,128)(2,1)}, bf16[64,768]{1,0:T(8,128)(2,1)}, bf16[64,768]{1,0:T(8,128)(2,1)}, bf16[64,768]{1,0:T(8,128)(2,1)}, bf16[4,1,3...) custom-call(bf16[768,768]{1,0:T(8,128)(2,1)} %down.3, bf16[256,768]{1,0:T(8,128)(2,1)} %get-tuple-element.187.hidden_ref, ...), custom_call_target="tpu_custom_call" | custom-call | bytes 15000000 | tf_op jit(solution)/shard_map/hidden_rest/pallas_call | solution.py:318
  164.2 5.2 %all-to-all-start.1 = ((bf16[4,960,384]{2,1,0:T(8,128)(2,1)}), bf16[4,960,384]{2,1,0:T(8,128)(2,1)S(1)}, u32[]{:S(2)}, u32[]{:S(2)}) async-start(bf16[4,960,384]{2,1,0:T(8,128)(2,1)} %pad_maximum_fusion), calls=%async_computation.1 | async-start | bytes 5898240 | tf_op jit(solution)/shard_map/all_to_all | solution.py:837
  169.4 10.2 %first_back.1 = (f32[1,384]{1,0:T(1,128)}, f32[256,384]{1,0:T(8,128)}, bf16[384,384]{1,0:T(8,128)(2,1)}, f32[256,384]{1,0:T(8,128)}, f32[8,128]{1,0:T(8,128)}, /...) custom-call(s32[16]{0:T(128)} %resets.7, ...), custom_call_target="tpu_custom_call" | custom-call | bytes 30000000 | tf_op jit(solution)/shard_map/first_back/pallas_call | solution.py:318
  180.0 3.6 %collective-permute-start.34 = (bf16[64,768]{1,0:T(8,128)(2,1)S(1)}, bf16[64,768]{1,0:T(8,128)(2,1)S(1)}, u32[]{:S(2)}, u32[]{:S(2)}) collective-permute-start(bf16[64,768]{1,0:T(8,128)(2,1)S(1)} %copy-done.49), channel_id=1, source_target_pairs={{0,2},{1,3},{2,0},{3,1},{4,6},{5,7},{6,4},{7,5},{8,10},{9,11},{10,... | collective-permute-start | bytes 294920 | tf_op jit(solution)/shard_map/ppermute | solution.py:738
  187.9 3.6 %collective-permute-done.34.refs_2_ = bf16[64,768]{1,0:T(8,128)(2,1)S(1)} collective-permute-done((bf16[64,768]{1,0:T(8,128)(2,1)S(1)}, bf16[64,768]{1,0:T(8,128)(2,1)S(1)}, u32[]{:S(2)}, u32[]{:S(2)}) %collective-permute-start.34) | collective-permute-done | bytes 98336 | tf_op jit(solution)/shard_map/ppermute | solution.py:738
  192.0 3.9 %collective-permute-done.45.refs_4_ = bf16[32,768]{1,0:T(8,128)(2,1)S(1)} collective-permute-done((bf16[32,768]{1,0:T(8,128)(2,1)}, bf16[32,768]{1,0:T(8,128)(2,1)S(1)}, u32[]{:S(2)}, u32[]{:S(2)}) %collective-permute-start.45) | collective-permute-done | bytes 49184 | tf_op jit(solution)/shard_map/ppermute | solution.py:767
  196.0 8.2 %all-to-all-done.1 = bf16[4,960,384]{2,1,0:T(8,128)(2,1)S(1)} async-done(((bf16[4,960,384]{2,1,0:T(8,128)(2,1)}), bf16[4,960,384]{2,1,0:T(8,128)(2,1)S(1)}, u32[]{:S(2)}, u32[]{:S(2)}) %all-to-all-start.1) | async-done | bytes 2949152 | tf_op jit(solution)/shard_map/all_to_all | solution.py:837
  204.9 4.9 %leave.1 = (bf16[256,384]{1,0:T(8,128)(2,1)}, bf16[4,1,208,384]{3,2,1,0:T(8,128)(2,1)}, bf16[4,1,208,384]{3,2,1,0:T(8,128)(2,1)}) custom-call(f32[64,768]{1,0:T(8,128)} %get-tuple-element.206.refs_0_, bf16[64,768]{1,0:T(8,128)(2,1)} %copy-done.29, bf16[32,768]{1,0:T(8,128)(2,1)} %copy-done.44, bf16[32,768]{1,0:T(8,128)(2,1)} %copy-done.46, ...), custom_call_target="tpu_custom_call" | custom-call | bytes 15000000 | tf_op jit(solution)/shard_map/leave/pallas_call | solution.py:318
  213.7 4.4 %all-to-all-start.2 = ((bf16[4,592,384]{2,1,0:T(8,128)(2,1)}), bf16[4,592,384]{2,1,0:T(8,128)(2,1)}, u32[]{:S(2)}, u32[]{:S(2)}) async-start(bf16[4,592,384]{2,1,0:T(8,128)(2,1)} %pad_maximum_fusion.1), calls=%async_computation.2 | async-start | bytes 3637248 | tf_op jit(solution)/shard_map/all_to_all | solution.py:837
  219.5 7.5 %collective-permute-done.36 = bf16[2,144,384]{2,1,0:T(8,128)(2,1)S(1)} collective-permute-done((bf16[2,144,384]{2,1,0:T(8,128)(2,1)S(1)}, bf16[2,144,384]{2,1,0:T(8,128)(2,1)S(1)}, u32[]{:S(2)}, u32[]{:S(2)}) %collective-permute-start.36) | collective-permute-done | bytes 221216 | tf_op jit(solution)/shard_map/ppermute | solution.py:738
  227.0 4.6 %collective-permute-start.37 = (bf16[1,144,384]{2,1,0:T(8,128)(2,1)S(1)}, bf16[1,144,384]{2,1,0:T(8,128)(2,1)S(1)}, u32[]{:S(2)}, u32[]{:S(2)}) collective-permute-start(bf16[1,144,384]{2,1,0:T(8,128)(2,1)S(1)} %slice_bitcast_fusion.7), channel_id=1, source_target_pairs={{0,2},{1,3},{2,0},{3,1},{4,6},{5,7},{6,4},{7,5},{8,10},{9,11},{10,... | collective-permute-start | bytes 331784 | tf_op jit(solution)/shard_map/ppermute | solution.py:738
  231.6 5.3 %collective-permute-done.37 = bf16[1,144,384]{2,1,0:T(8,128)(2,1)S(1)} collective-permute-done((bf16[1,144,384]{2,1,0:T(8,128)(2,1)S(1)}, bf16[1,144,384]{2,1,0:T(8,128)(2,1)S(1)}, u32[]{:S(2)}, u32[]{:S(2)}) %collective-permute-start.37) | collective-permute-done | bytes 110624 | tf_op jit(solution)/shard_map/ppermute | solution.py:738
  247.2 7.5 %all-to-all-start.3 = ((bf16[8,48,384]{2,1,0:T(8,128)(2,1)}), bf16[8,48,384]{2,1,0:T(8,128)(2,1)S(1)}, u32[]{:S(2)}, u32[]{:S(2)}) async-start(bf16[8,48,384]{2,1,0:T(8,128)(2,1)} %bitcast.33), calls=%async_computation.3 | async-start | bytes 589824 | tf_op jit(solution)/shard_map/all_to_all | solution.py:837
  257.8 10.5 %all-to-all-done.3 = bf16[8,48,384]{2,1,0:T(8,128)(2,1)S(1)} async-done(((bf16[8,48,384]{2,1,0:T(8,128)(2,1)}), bf16[8,48,384]{2,1,0:T(8,128)(2,1)S(1)}, u32[]{:S(2)}, u32[]{:S(2)}) %all-to-all-start.3) | async-done | bytes 294944 | tf_op jit(solution)/shard_map/all_to_all | solution.py:837
  285.7 3.7 %collective-permute-done.54.refs_1_ = bf16[4,160,384]{2,1,0:T(8,128)(2,1)S(1)} collective-permute-done((bf16[4,160,384]{2,1,0:T(8,128)(2,1)S(1)}, bf16[4,160,384]{2,1,0:T(8,128)(2,1)S(1)}, u32[]{:S(2)}, u32[]{:S(2)}) %collective-permute-start.54) | collective-permute-done | bytes 491552 | tf_op jit(solution)/shard_map/ppermute | solution.py:738
  293.9 5.1 %unpack_early.1 = (f32[768,768]{1,0:T(8,128)}, f32[768,768]{1,0:T(8,128)}, f32[96,2304]{1,0:T(8,128)}, f32[96,768]{1,0:T(8,128)}, f32[192,768]{1,0:T(8,128)}) custom-call(bf16[4,528,384]{2,1,0:T(8,128)(2,1)} %copy-done, bf16[4,528,384]{2,1,0:T(8,128)(2,1)} %copy-done.10), custom_call_target="tpu_custom_call" | custom-call | bytes 12000000 | tf_op jit(solution)/shard_map/unpack_early/pallas_call | solution.py:318
  (241 shorter events, 105.5 us)
Async XLA Ops:
  4.1 23.0 %all-to-all-start = ((bf16[8,48,384]{2,1,0:T(8,128)(2,1)}), bf16[8,48,384]{2,1,0:T(8,128)(2,1)S(1)}, u32[]{:S(2)}, u32[]{:S(2)}) async-start(bf16[8,48,384]{2,1,0:T(8,128)(2,1)} %collective-permute-done), calls=%async_computation | async-start | bytes 589824 | tf_op jit(solution)/shard_map/all_to_all | solution.py:837
  27.1 8.8 %collective-permute-start.3 = (bf16[192,384]{1,0:T(8,128)(2,1)S(1)}, bf16[192,384]{1,0:T(8,128)(2,1)S(1)}, u32[]{:S(2)}, u32[]{:S(2)}) collective-permute-start(bf16[192,384]{1,0:T(8,128)(2,1)S(1)} %dynamic-slice_bitcast_fusion), channel_id=1, source_target_pairs={{0,3},{1,2},{2,1},{3,0},{4,7},{5,6},{6,5},{7,4},{8,11},{9,10},{10,... | collective-permute-start | bytes 442376 | tf_op jit(solution)/shard_map/ppermute | solution.py:738
  28.4 12.7 %collective-permute-start.2 = (bf16[192,384]{1,0:T(8,128)(2,1)S(1)}, bf16[192,384]{1,0:T(8,128)(2,1)S(1)}, u32[]{:S(2)}, u32[]{:S(2)}) collective-permute-start(bf16[192,384]{1,0:T(8,128)(2,1)S(1)} %dynamic-slice_bitcast_fusion), channel_id=1, source_target_pairs={{0,2},{1,3},{2,0},{3,1},{4,6},{5,7},{6,4},{7,5},{8,10},{9,11},{10,... | collective-permute-start | bytes 442376 | tf_op jit(solution)/shard_map/ppermute | solution.py:738
  28.5 12.6 %collective-permute-start.1 = (bf16[192,384]{1,0:T(8,128)(2,1)S(1)}, bf16[192,384]{1,0:T(8,128)(2,1)S(1)}, u32[]{:S(2)}, u32[]{:S(2)}) collective-permute-start(bf16[192,384]{1,0:T(8,128)(2,1)S(1)} %dynamic-slice_bitcast_fusion), channel_id=1, source_target_pairs={{0,1},{1,0},{2,3},{3,2},{4,5},{5,4},{6,7},{7,6},{8,9},{9,8},{10,11... | collective-permute-start | bytes 442376 | tf_op jit(solution)/shard_map/ppermute | solution.py:738
  41.2 12.2 %collective-permute-start.5 = (bf16[576,384]{1,0:T(8,128)(2,1)S(1)}, bf16[576,384]{1,0:T(8,128)(2,1)S(1)}, u32[]{:S(2)}, u32[]{:S(2)}) collective-permute-start(bf16[576,384]{1,0:T(8,128)(2,1)S(1)} %constant_dynamic-update-slice_fusion.refs_0_.refs_10_), channel_id=1, source_target_pairs={{0,4},{4,0},{1,5},{5,1},{2,6},{6,2},{3,7},{7,3},{8,12},{12,8},{9,1... | collective-permute-start | bytes 1327112 | tf_op jit(solution)/shard_map/ppermute | solution.py:738
  53.5 12.1 %collective-permute-start.13 = (bf16[576,384]{1,0:T(8,128)(2,1)S(1)}, bf16[576,384]{1,0:T(8,128)(2,1)S(1)}, u32[]{:S(2)}, u32[]{:S(2)}) collective-permute-start(bf16[576,384]{1,0:T(8,128)(2,1)S(1)} %constant_dynamic-update-slice_fusion.refs_0_.refs_10_), channel_id=1, source_target_pairs={{0,8},{8,0},{1,9},{9,1},{2,10},{10,2},{3,11},{11,3},{4,12},{12,4},... | collective-permute-start | bytes 1327112 | tf_op jit(solution)/shard_map/ppermute | solution.py:738
  53.5 12.1 %collective-permute-start.14 = (bf16[576,384]{1,0:T(8,128)(2,1)S(1)}, bf16[576,384]{1,0:T(8,128)(2,1)S(1)}, u32[]{:S(2)}, u32[]{:S(2)}) collective-permute-start(bf16[576,384]{1,0:T(8,128)(2,1)S(1)} %collective-permute-done.5.refs_1_.refs_11_), channel_id=1, source_target_pairs={{0,8},{8,0},{1,9},{9,1},{2,10},{10,2},{3,11},{11,3},{4,12},{12,4},... | collective-permute-start | bytes 1327112 | tf_op jit(solution)/shard_map/ppermute | solution.py:738
  55.5 10.1 %collective-permute-start.11 = (bf16[64,768]{1,0:T(8,128)(2,1)}, bf16[64,768]{1,0:T(8,128)(2,1)S(1)}, u32[]{:S(2)}, u32[]{:S(2)}) collective-permute-start(bf16[64,768]{1,0:T(8,128)(2,1)} %get-tuple-element.165.refs_4_), channel_id=1, source_target_pairs={{0,2},{1,3},{2,0},{3,1},{4,6},{5,7},{6,4},{7,5},{8,10},{9,11},{10,... | collective-permute-start | bytes 294920 | tf_op jit(solution)/shard_map/ppermute | solution.py:738
  56.2 9.3 %collective-permute-start.10 = (bf16[64,768]{1,0:T(8,128)(2,1)}, bf16[64,768]{1,0:T(8,128)(2,1)S(1)}, u32[]{:S(2)}, u32[]{:S(2)}) collective-permute-start(bf16[64,768]{1,0:T(8,128)(2,1)} %get-tuple-element.165.refs_4_), channel_id=1, source_target_pairs={{0,1},{1,0},{2,3},{3,2},{4,5},{5,4},{6,7},{7,6},{8,9},{9,8},{10,11... | collective-permute-start | bytes 294920 | tf_op jit(solution)/shard_map/ppermute | solution.py:738
  72.7 9.7 %collective-permute-start.15 = (bf16[64,1536]{1,0:T(8,128)(2,1)}, bf16[64,1536]{1,0:T(8,128)(2,1)S(1)}, u32[]{:S(2)}, u32[]{:S(2)}) collective-permute-start(bf16[64,1536]{1,0:T(8,128)(2,1)} %get-tuple-element.161.refs_1_.refs_11_), channel_id=1, source_target_pairs={{0,8},{8,0},{1,9},{9,1},{2,10},{10,2},{3,11},{11,3},{4,12},{12,4},... | collective-permute-start | bytes 589832 | tf_op jit(solution)/shard_map/ppermute | solution.py:738
  94.1 9.6 %collective-permute-start.21 = (bf16[64,768]{1,0:T(8,128)(2,1)}, bf16[64,768]{1,0:T(8,128)(2,1)S(1)}, u32[]{:S(2)}, u32[]{:S(2)}) collective-permute-start(bf16[64,768]{1,0:T(8,128)(2,1)} %get-tuple-element.164.refs_0_), channel_id=1, source_target_pairs={{0,2},{1,3},{2,0},{3,1},{4,6},{5,7},{6,4},{7,5},{8,10},{9,11},{10,... | collective-permute-start | bytes 294920 | tf_op jit(solution)/shard_map/ppermute | solution.py:738
  94.6 9.1 %collective-permute-start.20 = (bf16[64,768]{1,0:T(8,128)(2,1)}, bf16[64,768]{1,0:T(8,128)(2,1)S(1)}, u32[]{:S(2)}, u32[]{:S(2)}) collective-permute-start(bf16[64,768]{1,0:T(8,128)(2,1)} %get-tuple-element.164.refs_0_), channel_id=1, source_target_pairs={{0,1},{1,0},{2,3},{3,2},{4,5},{5,4},{6,7},{7,6},{8,9},{9,8},{10,11... | collective-permute-start | bytes 294920 | tf_op jit(solution)/shard_map/ppermute | solution.py:738
  109.3 11.1 %collective-permute-start.24 = (bf16[64,768]{1,0:T(8,128)(2,1)}, bf16[64,768]{1,0:T(8,128)(2,1)S(1)}, u32[]{:S(2)}, u32[]{:S(2)}) collective-permute-start(bf16[64,768]{1,0:T(8,128)(2,1)} %get-tuple-element.172), channel_id=1, source_target_pairs={{0,2},{1,3},{2,0},{3,1},{4,6},{5,7},{6,4},{7,5},{8,10},{9,11},{10,... | collective-permute-start | bytes 294920 | tf_op jit(solution)/shard_map/ppermute | solution.py:738
  131.4 10.3 %collective-permute-start.29 = (bf16[32,1536]{1,0:T(8,128)(2,1)}, bf16[32,1536]{1,0:T(8,128)(2,1)S(1)}, u32[]{:S(2)}, u32[]{:S(2)}) collective-permute-start(bf16[32,1536]{1,0:T(8,128)(2,1)} %get-tuple-element.180), channel_id=1, source_target_pairs={{2,0},{10,8},{3,1},{11,9},{4,2},{12,10},{5,3},{13,11},{6,4},{14,12... | collective-permute-start | bytes 294920 | tf_op jit(solution)/shard_map/ppermute | solution.py:767
  132.9 10.1 %collective-permute-start.26 = (bf16[64,1536]{1,0:T(8,128)(2,1)}, bf16[64,1536]{1,0:T(8,128)(2,1)S(1)}, u32[]{:S(2)}, u32[]{:S(2)}) collective-permute-start(bf16[64,1536]{1,0:T(8,128)(2,1)} %get-tuple-element.178), channel_id=1, source_target_pairs={{0,8},{8,0},{1,9},{9,1},{2,10},{10,2},{3,11},{11,3},{4,12},{12,4},... | collective-permute-start | bytes 589832 | tf_op jit(solution)/shard_map/ppermute | solution.py:738
  151.9 9.9 %collective-permute-start.32 = (bf16[4,4,144,384]{3,2,1,0:T(8,128)(2,1)}, bf16[4,4,144,384]{3,2,1,0:T(8,128)(2,1)S(1)}, u32[]{:S(2)}, u32[]{:S(2)}) collective-permute-start(bf16[4,4,144,384]{3,2,1,0:T(8,128)(2,1)} %get-tuple-element.192), channel_id=1, source_target_pairs={{0,8},{8,0},{1,9},{9,1},{2,10},{10,2},{3,11},{11,3},{4,12},{12,4},... | collective-permute-start | bytes 5308424 | tf_op jit(solution)/shard_map/ppermute | solution.py:738
  164.2 39.9 %all-to-all-start.1 = ((bf16[4,960,384]{2,1,0:T(8,128)(2,1)}), bf16[4,960,384]{2,1,0:T(8,128)(2,1)S(1)}, u32[]{:S(2)}, u32[]{:S(2)}) async-start(bf16[4,960,384]{2,1,0:T(8,128)(2,1)} %pad_maximum_fusion), calls=%async_computation.1 | async-start | bytes 5898240 | tf_op jit(solution)/shard_map/all_to_all | solution.py:837
  179.6 30.2 %collective-permute-start.41 = (bf16[4,4,96,384]{3,2,1,0:T(8,128)(2,1)}, bf16[4,4,96,384]{3,2,1,0:T(8,128)(2,1)}, u32[]{:S(2)}, u32[]{:S(2)}) collective-permute-start(bf16[4,4,96,384]{3,2,1,0:T(8,128)(2,1)} %get-tuple-element.205), channel_id=1, source_target_pairs={{0,8},{8,0},{1,9},{9,1},{2,10},{10,2},{3,11},{11,3},{4,12},{12,4},... | collective-permute-start | bytes 3538952 | tf_op jit(solution)/shard_map/ppermute | solution.py:738
  180.0 11.5 %collective-permute-start.34 = (bf16[64,768]{1,0:T(8,128)(2,1)S(1)}, bf16[64,768]{1,0:T(8,128)(2,1)S(1)}, u32[]{:S(2)}, u32[]{:S(2)}) collective-permute-start(bf16[64,768]{1,0:T(8,128)(2,1)S(1)} %copy-done.49), channel_id=1, source_target_pairs={{0,2},{1,3},{2,0},{3,1},{4,6},{5,7},{6,4},{7,5},{8,10},{9,11},{10,... | collective-permute-start | bytes 294920 | tf_op jit(solution)/shard_map/ppermute | solution.py:738
  183.5 12.4 %collective-permute-start.35 = (bf16[64,768]{1,0:T(8,128)(2,1)S(1)}, bf16[64,768]{1,0:T(8,128)(2,1)S(1)}, u32[]{:S(2)}, u32[]{:S(2)}) collective-permute-start(bf16[64,768]{1,0:T(8,128)(2,1)S(1)} %copy-done.48), channel_id=1, source_target_pairs={{0,3},{1,2},{2,1},{3,0},{4,7},{5,6},{6,5},{7,4},{8,11},{9,10},{10,... | collective-permute-start | bytes 294920 | tf_op jit(solution)/shard_map/ppermute | solution.py:738
  186.3 9.6 %collective-permute-start.45 = (bf16[32,768]{1,0:T(8,128)(2,1)}, bf16[32,768]{1,0:T(8,128)(2,1)S(1)}, u32[]{:S(2)}, u32[]{:S(2)}) collective-permute-start(bf16[32,768]{1,0:T(8,128)(2,1)} %get-tuple-element.209), channel_id=1, source_target_pairs={{2,0},{10,8},{3,1},{11,9},{4,2},{12,10},{5,3},{13,11},{6,4},{14,12... | collective-permute-start | bytes 147464 | tf_op jit(solution)/shard_map/ppermute | solution.py:767
  191.5 12.7 %collective-permute-start.42 = (bf16[64,768]{1,0:T(8,128)(2,1)}, bf16[64,768]{1,0:T(8,128)(2,1)S(1)}, u32[]{:S(2)}, u32[]{:S(2)}) collective-permute-start(bf16[64,768]{1,0:T(8,128)(2,1)} %get-tuple-element.207), channel_id=1, source_target_pairs={{0,8},{8,0},{1,9},{9,1},{2,10},{10,2},{3,11},{11,3},{4,12},{12,4},... | collective-permute-start | bytes 294920 | tf_op jit(solution)/shard_map/ppermute | solution.py:738
  191.8 12.4 %collective-permute-start.44 = (bf16[32,768]{1,0:T(8,128)(2,1)S(1)}, bf16[32,768]{1,0:T(8,128)(2,1)S(1)}, u32[]{:S(2)}, u32[]{:S(2)}) collective-permute-start(bf16[32,768]{1,0:T(8,128)(2,1)S(1)} %collective-permute-done.43.refs_2_), channel_id=1, source_target_pairs={{0,8},{8,0},{1,9},{9,1},{2,10},{10,2},{3,11},{11,3},{4,12},{12,4},... | collective-permute-start | bytes 147464 | tf_op jit(solution)/shard_map/ppermute | solution.py:738
  213.7 26.9 %all-to-all-start.2 = ((bf16[4,592,384]{2,1,0:T(8,128)(2,1)}), bf16[4,592,384]{2,1,0:T(8,128)(2,1)}, u32[]{:S(2)}, u32[]{:S(2)}) async-start(bf16[4,592,384]{2,1,0:T(8,128)(2,1)} %pad_maximum_fusion.1), calls=%async_computation.2 | async-start | bytes 3637248 | tf_op jit(solution)/shard_map/all_to_all | solution.py:837
  227.0 9.9 %collective-permute-start.37 = (bf16[1,144,384]{2,1,0:T(8,128)(2,1)S(1)}, bf16[1,144,384]{2,1,0:T(8,128)(2,1)S(1)}, u32[]{:S(2)}, u32[]{:S(2)}) collective-permute-start(bf16[1,144,384]{2,1,0:T(8,128)(2,1)S(1)} %slice_bitcast_fusion.7), channel_id=1, source_target_pairs={{0,2},{1,3},{2,0},{3,1},{4,6},{5,7},{6,4},{7,5},{8,10},{9,11},{10,... | collective-permute-start | bytes 331784 | tf_op jit(solution)/shard_map/ppermute | solution.py:738
  242.5 12.3 %collective-permute-start.48 = (bf16[2,160,384]{2,1,0:T(8,128)(2,1)S(1)}, bf16[2,160,384]{2,1,0:T(8,128)(2,1)S(1)}, u32[]{:S(2)}, u32[]{:S(2)}) collective-permute-start(bf16[2,160,384]{2,1,0:T(8,128)(2,1)S(1)} %slice_bitcast_fusion.1), channel_id=1, source_target_pairs={{0,1},{1,0},{2,3},{3,2},{4,5},{5,4},{6,7},{7,6},{8,9},{9,8},{10,11... | collective-permute-start | bytes 737288 | tf_op jit(solution)/shard_map/ppermute | solution.py:738
  243.6 28.3 %collective-permute-start.39 = (bf16[528,384]{1,0:T(8,128)(2,1)S(1)}, bf16[528,384]{1,0:T(8,128)(2,1)S(1)}, u32[]{:S(2)}, u32[]{:S(2)}) collective-permute-start(bf16[528,384]{1,0:T(8,128)(2,1)S(1)} %get-tuple-element.254), channel_id=1, source_target_pairs={{0,16},{4,20},{16,0},{20,4},{1,17},{5,21},{17,1},{21,5},{2,18},{6,... | collective-permute-start | bytes 1216520 | tf_op jit(solution)/shard_map/ppermute | solution.py:738
  245.1 28.3 %collective-permute-start.38 = (bf16[528,384]{1,0:T(8,128)(2,1)S(1)}, bf16[528,384]{1,0:T(8,128)(2,1)S(1)}, u32[]{:S(2)}, u32[]{:S(2)}) collective-permute-start(bf16[528,384]{1,0:T(8,128)(2,1)S(1)} %get-tuple-element.254), channel_id=1, source_target_pairs={{0,4},{4,0},{16,20},{20,16},{1,5},{5,1},{17,21},{21,17},{2,6},{6,2... | collective-permute-start | bytes 1216520 | tf_op jit(solution)/shard_map/ppermute | solution.py:738
  245.9 28.1 %collective-permute-start.40 = (bf16[528,384]{1,0:T(8,128)(2,1)S(1)}, bf16[528,384]{1,0:T(8,128)(2,1)S(1)}, u32[]{:S(2)}, u32[]{:S(2)}) collective-permute-start(bf16[528,384]{1,0:T(8,128)(2,1)S(1)} %get-tuple-element.254), channel_id=1, source_target_pairs={{0,20},{4,16},{16,4},{20,0},{1,21},{5,17},{17,5},{21,1},{2,22},{6,... | collective-permute-start | bytes 1216520 | tf_op jit(solution)/shard_map/ppermute | solution.py:738
  247.2 21.2 %all-to-all-start.3 = ((bf16[8,48,384]{2,1,0:T(8,128)(2,1)}), bf16[8,48,384]{2,1,0:T(8,128)(2,1)S(1)}, u32[]{:S(2)}, u32[]{:S(2)}) async-start(bf16[8,48,384]{2,1,0:T(8,128)(2,1)} %bitcast.33), calls=%async_computation.3 | async-start | bytes 589824 | tf_op jit(solution)/shard_map/all_to_all | solution.py:837
  254.8 15.6 %collective-permute-start.49 = (bf16[1,160,384]{2,1,0:T(8,128)(2,1)S(1)}, bf16[1,160,384]{2,1,0:T(8,128)(2,1)S(1)}, u32[]{:S(2)}, u32[]{:S(2)}) collective-permute-start(bf16[1,160,384]{2,1,0:T(8,128)(2,1)S(1)} %slice_bitcast_fusion.5), channel_id=1, source_target_pairs={{0,2},{1,3},{2,0},{3,1},{4,6},{5,7},{6,4},{7,5},{8,10},{9,11},{10,... | collective-permute-start | bytes 368648 | tf_op jit(solution)/shard_map/ppermute | solution.py:738
  268.3 13.4 %collective-permute-start.53 = (bf16[8,48,384]{2,1,0:T(8,128)(2,1)S(1)}, bf16[8,48,384]{2,1,0:T(8,128)(2,1)S(1)}, u32[]{:S(2)}, u32[]{:S(2)}) collective-permute-start(bf16[8,48,384]{2,1,0:T(8,128)(2,1)S(1)} %all-to-all-done.3), channel_id=1, source_target_pairs={{0,0},{4,8},{8,4},{12,12},{1,1},{5,9},{9,5},{13,13},{2,2},{6,10},{... | collective-permute-start | bytes 884744 | tf_op jit(solution)/shard_map/ppermute | solution.py:749
  (79 other events, 585.9 us)

commit v4 on v3

--- a/solution.py
+++ b/solution.py
@@ -1011,7 +1011,6 @@
         dsqueeze_b = dsqueeze_given
     pieces, dsqueeze_given = return_pairs(plan, back, pairs_a, squeeze_a)
     out_sums = everyone(out_shares, "tensor")
-    early, dq_a, out_sums = lax.optimization_barrier((early, dq_a, out_sums))
     first = sum_cores(keep, give)
     tail_each, small_each = padded(4 * share, plane), padded(128, plane)
     grad_x, keep, give = call(
@@ -1027,6 +1026,7 @@
     )
     last = sum_cores(keep, give)
     last = jnp.concatenate([first.reshape(half_plane, -1, LANES), last[:, 0]], axis=1)
+    last, early = lax.optimization_barrier((last, early))
     leaving, = call("exit", exit_body, [(arrived.shape, BF16)], [order, after(grad_x, last), m_b, *out_sums])
     last = spread(last, ACROSS)
     early = sum_first(early)
@@ -1041,12 +1041,11 @@
     last = jnp.concatenate([first, last, small], axis=1)
     leaving = after(leaving, last)
     last = gather_across(halve(last, "tensor"))
-    returned = swap(spread(leaving.reshape(plan.group, -1, width), home))
+    returned, early = lax.optimization_barrier((spread(leaving.reshape(plan.group, -1, width), home), early))
+    returned, early = swap(returned), both_cores(early)
     x_rows = plan.frames * plan.rows * plan.cols
     grad_input = returned[:, :x_rows].reshape(clips_in.shape).astype(F32)
     result = returned[:, x_rows:].reshape(cotangent.shape).astype(F32)
-    early, last, grad_input, result = lax.optimization_barrier((early, last, grad_input, result))
-    early, last = both_cores(early), both_cores(last)
     column = lambda rows, columns: ((rows, columns), F32)
     grad_expand_b, grad_reduce_b, grad_project_b, grad_shortcut_b, grad_output_b = call(
         "unpack_early",
@@ -1059,6 +1058,8 @@
         (),
         [((2, half_plane, hidden_each + cross_each, LANES), BF16)],
     )
+    last, grad_expand_b, grad_input, result = lax.optimization_barrier((last, grad_expand_b, grad_input, result))
+    last = both_cores(last)
     grad_expand_a, grad_reduce_a, grad_project_a, grad_output_a, *small = call(
         "unpack_last",
         functools.partial(unpack_body, [(first_each, 2), (tail_each, 2)]),

time: 300 us -> 287 us (0.957)
  waiting for transfers between devices: 110 us -> 98.7 us
    all_to_all x4, waiting for transfers between devices: 30.4 us -> 14.4 us  [spread(): return lax.all_to_all(values, axes, 0, 0, tiled=True)]
    ppermute x46, waiting for transfers between devices: 63.6 us -> 67.2 us  [exchange(): lax.ppermute(values, tuple(order), [(i, int(where[p ^ by])) for i, p in e...]
    all_to_all x4, starting transfers between devices: 29.7 us -> 26.7 us  [spread(): return lax.all_to_all(values, axes, 0, 0, tiled=True)]
    unnamed x104 -> x98, local copies, waits for them, and re-layouts: 8.59 us -> 6.49 us
  transfers between devices with their start and end apart: 60 -> 60, of which waited for: 32 -> 32; matrix products, arithmetic and copies ran while one was open for 2% -> 4% of each run, Pallas kernels for 11% -> 10%
where the time goes in v4:
time: 287 us; the launch traced here: 286 us
  waiting for transfers between devices  98.7 us (34%)
  starting transfers between devices  90.8 us (32%)
  Pallas kernels  71.3 us (25%)
  other arithmetic  12.2 us (4%)
  local copies, waits for them, and re-layouts  11.1 us (4%)
    pallas_call x13, Pallas kernels, call(): pl.pallas_call(body, out_shape=[jax.ShapeDtypeStruct(shape, dtype) for sh...  71.3 us
    ppermute x46, waiting for transfers between devices, exchange(): lax.ppermute(values, tuple(order), [(i, int(where[p ^ by])) for i, p in e...  67.2 us
    ppermute x46, starting transfers between devices, exchange(): lax.ppermute(values, tuple(order), [(i, int(where[p ^ by])) for i, p in e...  43.3 us
    all_to_all x4, starting transfers between devices, spread(): return lax.all_to_all(values, axes, 0, 0, tiled=True)  26.7 us
    ppermute x8, starting transfers between devices, shift(): return lax.ppermute(values, EVERY, pairs)  17.8 us
    ppermute x8, waiting for transfers between devices, shift(): return lax.ppermute(values, EVERY, pairs)  17.1 us
    all_to_all x4, waiting for transfers between devices, spread(): return lax.all_to_all(values, axes, 0, 0, tiled=True)  14.4 us
    unnamed x98, local copies, waits for them, and re-layouts  6.49 us
  transfers between devices with their start and end apart: 60, of which 32 were waited for; matrix products, arithmetic and copies ran while one was open for 4% of the time, Pallas kernels for 10%

profile of v4, /device:TPU:0, one launch (start us, length us, event | category | flops | bytes accessed | tf_op | source)
XLA Modules:
  0.0 285.7 jit_solution(14006638643182083150)
XLA Ops:
  4.1 12.6 %all-to-all-start = ((bf16[8,48,384]{2,1,0:T(8,128)(2,1)}), bf16[8,48,384]{2,1,0:T(8,128)(2,1)S(1)}, u32[]{:S(2)}, u32[]{:S(2)}) async-start(bf16[8,48,384]{2,1,0:T(8,128)(2,1)} %collective-permute-done), calls=%async_computation | async-start | bytes 589824 | tf_op jit(solution)/shard_map/all_to_all | solution.py:837
  16.8 10.3 %all-to-all-done = bf16[8,48,384]{2,1,0:T(8,128)(2,1)S(1)} async-done(((bf16[8,48,384]{2,1,0:T(8,128)(2,1)}), bf16[8,48,384]{2,1,0:T(8,128)(2,1)S(1)}, u32[]{:S(2)}, u32[]{:S(2)}) %all-to-all-start) | async-done | bytes 294944 | tf_op jit(solution)/shard_map/all_to_all | solution.py:837
  28.5 3.0 %collective-permute-start.1 = (bf16[192,384]{1,0:T(8,128)(2,1)S(1)}, bf16[192,384]{1,0:T(8,128)(2,1)S(1)}, u32[]{:S(2)}, u32[]{:S(2)}) collective-permute-start(bf16[192,384]{1,0:T(8,128)(2,1)S(1)} %dynamic-slice_bitcast_fusion), channel_id=1, source_target_pairs={{0,1},{1,0},{2,3},{3,2},{4,5},{5,4},{6,7},{7,6},{8,9},{9,8},{10,11... | collective-permute-start | bytes 442376 | tf_op jit(solution)/shard_map/ppermute | solution.py:738
  36.0 5.1 %collective-permute-done.2 = bf16[192,384]{1,0:T(8,128)(2,1)S(1)} collective-permute-done((bf16[192,384]{1,0:T(8,128)(2,1)S(1)}, bf16[192,384]{1,0:T(8,128)(2,1)S(1)}, u32[]{:S(2)}, u32[]{:S(2)}) %collective-permute-start.2) | collective-permute-done | bytes 147488 | tf_op jit(solution)/shard_map/ppermute | solution.py:738
  45.1 3.8 %collective-permute-start.6 = (bf16[16,768]{1,0:T(8,128)(2,1)}, bf16[16,768]{1,0:T(8,128)(2,1)S(1)}, u32[]{:S(2)}, u32[]{:S(2)}) collective-permute-start(bf16[16,768]{1,0:T(8,128)(2,1)} %get-tuple-element.145), channel_id=1, source_target_pairs={{0,1},{8,9},{1,2},{9,10},{2,3},{10,11},{3,4},{11,12},{4,5},{12,13}... | collective-permute-start | bytes 73736 | tf_op jit(solution)/shard_map/ppermute | solution.py:767
  58.4 4.1 %first.1 = (bf16[256,384]{1,0:T(8,128)(2,1)}, f32[256,384]{1,0:T(8,128)}, bf16[256,384]{1,0:T(8,128)(2,1)}, bf16[1024,192]{1,0:T(8,128)(2,1)}) custom-call(s32[16]{0:T(128)} %resets.7, s32[16]{0:T(128)} %videos.7, bf16[256,384]{1,0:T(8,128)(2,1)} %get-tuple-element.136.refs_0_.refs_10_, bf16[256,384]{1,0:T(8,128)(2,1)} %get-tuple-element.137.refs_1_.refs_6_, ...), custom_call_target="tpu_custom_call" | custom-call | bytes 12000000 | tf_op jit(solution)/shard_map/first/pallas_call | solution.py:318
  66.5 6.2 %between.1 = (f32[256,384]{1,0:T(8,128)}, bf16[256,384]{1,0:T(8,128)(2,1)}, bf16[64,768]{1,0:T(8,128)(2,1)}, f32[64,768]{1,0:T(8,128)}, bf16[64,1536]{1,0:T(8,128)(2,1)}, /*index=5*/bf16[16,1536]{1,0:T(8,128)(2,1)}) custom-call(f32[256,384]{1,0:T(8,128)} %get-tuple-element.154.m_ref.refs_1_, bf16[256,384]{1,0:T(8,128)(2,1)} %get-tuple-element.155.l_ref.refs_2_, ...), custom_call_target="tpu_custom_call" | custom-call | bytes 18000000 | tf_op jit(solution)/shard_map/between/pallas_call | solution.py:318
  74.6 4.7 %collective-permute-start.16 = (bf16[16,1536]{1,0:T(8,128)(2,1)}, bf16[16,1536]{1,0:T(8,128)(2,1)S(1)}, u32[]{:S(2)}, u32[]{:S(2)}) collective-permute-start(bf16[16,1536]{1,0:T(8,128)(2,1)} %get-tuple-element.160), channel_id=1, source_target_pairs={{0,1},{8,9},{1,2},{9,10},{2,3},{10,11},{3,4},{11,12},{4,5},{12,13}... | collective-permute-start | bytes 147464 | tf_op jit(solution)/shard_map/ppermute | solution.py:767
  83.1 7.2 %second.1 = (bf16[64,768]{1,0:T(8,128)(2,1)}, f32[64,768]{1,0:T(8,128)}, bf16[64,768]{1,0:T(8,128)(2,1)}, bf16[512,192]{1,0:T(8,128)(2,1)}) custom-call(s32[16]{0:T(128)} %resets.7, s32[16]{0:T(128)} %videos.7, bf16[64,768]{1,0:T(8,128)(2,1)} %get-tuple-element.158.refs_0_.refs_9_, bf16[64,1536]{1,0:T(8,128)(2,1)} %get-tuple-element.159.refs_1_.refs_11_, ...), custom_call_target="tpu_custom_call" | custom-call | bytes 21000000 | tf_op jit(solution)/shard_map/second/pallas_call | solution.py:318
  90.3 3.8 %collective-permute-start.22 = (bf16[64,768]{1,0:T(8,128)(2,1)}, bf16[64,768]{1,0:T(8,128)(2,1)S(1)}, u32[]{:S(2)}, u32[]{:S(2)}) collective-permute-start(bf16[64,768]{1,0:T(8,128)(2,1)} %get-tuple-element.162.refs_0_), channel_id=1, source_target_pairs={{0,3},{1,2},{2,1},{3,0},{4,7},{5,6},{6,5},{7,4},{8,11},{9,10},{10,... | collective-permute-start | bytes 294920 | tf_op jit(solution)/shard_map/ppermute | solution.py:738
  97.7 6.1 %collective-permute-done.21.refs_2_ = bf16[64,768]{1,0:T(8,128)(2,1)S(1)} collective-permute-done((bf16[64,768]{1,0:T(8,128)(2,1)}, bf16[64,768]{1,0:T(8,128)(2,1)S(1)}, u32[]{:S(2)}, u32[]{:S(2)}) %collective-permute-start.21) | collective-permute-done | bytes 98336 | tf_op jit(solution)/shard_map/ppermute | solution.py:738
  105.0 3.9 %hidden.1 = (bf16[64,768]{1,0:T(8,128)(2,1)}, bf16[64,768]{1,0:T(8,128)(2,1)}, bf16[64,768]{1,0:T(8,128)(2,1)}, bf16[64,768]{1,0:T(8,128)(2,1)}, bf16[256,768]{1,0:T(8,128)(2,1)}, /*index=5*/bf16[256,768]{1,0:T(8,128)(2,1)}) custom-call(bf16[768,768]{1,0:T(8,128)(2,1)} %up.1, bf16[768,768]{1,0:T(8,128)(2,1)} %down.3, ...), custom_call_target="tpu_custom_call" | custom-call | bytes 12000000 | tf_op jit(solution)/shard_map/hidden/pallas_call | solution.py:318
  109.4 3.3 %collective-permute-start.24 = (bf16[64,768]{1,0:T(8,128)(2,1)}, bf16[64,768]{1,0:T(8,128)(2,1)S(1)}, u32[]{:S(2)}, u32[]{:S(2)}) collective-permute-start(bf16[64,768]{1,0:T(8,128)(2,1)} %get-tuple-element.170), channel_id=1, source_target_pairs={{0,2},{1,3},{2,0},{3,1},{4,6},{5,7},{6,4},{7,5},{8,10},{9,11},{10,... | collective-permute-start | bytes 294920 | tf_op jit(solution)/shard_map/ppermute | solution.py:738
  115.2 5.3 %collective-permute-done.24.refs_2_ = bf16[64,768]{1,0:T(8,128)(2,1)S(1)} collective-permute-done((bf16[64,768]{1,0:T(8,128)(2,1)}, bf16[64,768]{1,0:T(8,128)(2,1)S(1)}, u32[]{:S(2)}, u32[]{:S(2)}) %collective-permute-start.24) | collective-permute-done | bytes 98336 | tf_op jit(solution)/shard_map/ppermute | solution.py:738
  121.1 9.0 %second_back.1 = (f32[64,768]{1,0:T(8,128)}, f32[1,768]{1,0:T(1,128)}, bf16[768,768]{1,0:T(8,128)(2,1)}, f32[64,768]{1,0:T(8,128)}, f32[8,128]{1,0:T(8,128)}, /*...) custom-call(s32[16]{0:T(128)} %resets.7, s32[16]{0:T(128)} %videos.7, ...), custom_call_target="tpu_custom_call" | custom-call | bytes 27000000 | tf_op jit(solution)/shard_map/second_back/pallas_call | solution.py:318
  133.0 4.5 %collective-permute-done.27.refs_2_ = bf16[32,1536]{1,0:T(8,128)(2,1)S(1)} collective-permute-done((bf16[32,1536]{1,0:T(8,128)(2,1)}, bf16[32,1536]{1,0:T(8,128)(2,1)S(1)}, u32[]{:S(2)}, u32[]{:S(2)}) %collective-permute-start.27) | collective-permute-done | bytes 98336 | tf_op jit(solution)/shard_map/ppermute | solution.py:767
  137.5 4.2 %collective-permute-done.29.refs_4_ = bf16[32,1536]{1,0:T(8,128)(2,1)S(1)} collective-permute-done((bf16[32,1536]{1,0:T(8,128)(2,1)}, bf16[32,1536]{1,0:T(8,128)(2,1)S(1)}, u32[]{:S(2)}, u32[]{:S(2)}) %collective-permute-start.29) | collective-permute-done | bytes 98336 | tf_op jit(solution)/shard_map/ppermute | solution.py:767
  143.7 8.2 %cross.1 = (f32[256,384]{1,0:T(8,128)}, f32[3,4,768]{2,1,0:T(4,128)}, f32[2,4,768]{2,1,0:T(4,128)}, f32[1,384]{1,0:T(1,128)}, bf16[4,4,144,384]{3,2,1,0:T(8,128)(2,1)}, /*index=5*/bf16[4,4,144,384]{3,2,1,0:T(8,128)(2,1)}) custom-call(f32[64,1536]{1,0:T(8,128)} %get-tuple-element.175.refs_0_, bf16[64,1536]{1,0:T(8,128)(2,1)} %copy-done.21, ...), custom_call_target="tpu_custom_call" | custom-call | bytes 24000000 | tf_op jit(solution)/shard_map/cross/pallas_call | solution.py:318
  152.1 4.8 %hidden_rest.1 = (bf16[64,768]{1,0:T(8,128)(2,1)}, bf16[64,768]{1,0:T(8,128)(2,1)}, bf16[64,768]{1,0:T(8,128)(2,1)}, bf16[64,768]{1,0:T(8,128)(2,1)}, bf16[4,1,3...) custom-call(bf16[768,768]{1,0:T(8,128)(2,1)} %down.3, bf16[256,768]{1,0:T(8,128)(2,1)} %get-tuple-element.185.hidden_ref, ...), custom_call_target="tpu_custom_call" | custom-call | bytes 15000000 | tf_op jit(solution)/shard_map/hidden_rest/pallas_call | solution.py:318
  164.3 5.2 %all-to-all-start.1 = ((bf16[4,960,384]{2,1,0:T(8,128)(2,1)}), bf16[4,960,384]{2,1,0:T(8,128)(2,1)S(1)}, u32[]{:S(2)}, u32[]{:S(2)}) async-start(bf16[4,960,384]{2,1,0:T(8,128)(2,1)} %pad_maximum_fusion), calls=%async_computation.1 | async-start | bytes 5898240 | tf_op jit(solution)/shard_map/all_to_all | solution.py:837
  169.5 10.1 %first_back.1 = (f32[1,384]{1,0:T(1,128)}, f32[256,384]{1,0:T(8,128)}, bf16[384,384]{1,0:T(8,128)(2,1)}, f32[256,384]{1,0:T(8,128)}, f32[8,128]{1,0:T(8,128)}, /...) custom-call(s32[16]{0:T(128)} %resets.7, ...), custom_call_target="tpu_custom_call" | custom-call | bytes 30000000 | tf_op jit(solution)/shard_map/first_back/pallas_call | solution.py:318
  189.9 4.9 %leave.1 = (bf16[256,384]{1,0:T(8,128)(2,1)}, bf16[4,1,208,384]{3,2,1,0:T(8,128)(2,1)}, bf16[4,1,208,384]{3,2,1,0:T(8,128)(2,1)}) custom-call(f32[64,768]{1,0:T(8,128)} %get-tuple-element.197.refs_0_, bf16[64,768]{1,0:T(8,128)(2,1)} %copy-done.26, bf16[32,768]{1,0:T(8,128)(2,1)} %copy-done.41, bf16[32,768]{1,0:T(8,128)(2,1)} %copy-done.43, ...), custom_call_target="tpu_custom_call" | custom-call | bytes 15000000 | tf_op jit(solution)/shard_map/leave/pallas_call | solution.py:318
  200.2 4.0 %all-to-all-done.1 = bf16[4,960,384]{2,1,0:T(8,128)(2,1)S(1)} async-done(((bf16[4,960,384]{2,1,0:T(8,128)(2,1)}), bf16[4,960,384]{2,1,0:T(8,128)(2,1)S(1)}, u32[]{:S(2)}, u32[]{:S(2)}) %all-to-all-start.1) | async-done | bytes 2949152 | tf_op jit(solution)/shard_map/all_to_all | solution.py:837
  205.5 4.6 %all-to-all-start.2 = ((bf16[4,592,384]{2,1,0:T(8,128)(2,1)}), bf16[4,592,384]{2,1,0:T(8,128)(2,1)S(1)}, u32[]{:S(2)}, u32[]{:S(2)}) async-start(bf16[4,592,384]{2,1,0:T(8,128)(2,1)} %pad_maximum_fusion.1), calls=%async_computation.2 | async-start | bytes 3637248 | tf_op jit(solution)/shard_map/all_to_all | solution.py:837
  212.2 3.5 %collective-permute-start.43 = (bf16[64,768]{1,0:T(8,128)(2,1)S(1)}, bf16[64,768]{1,0:T(8,128)(2,1)S(1)}, u32[]{:S(2)}, u32[]{:S(2)}) collective-permute-start(bf16[64,768]{1,0:T(8,128)(2,1)S(1)} %copy-done.46), channel_id=1, source_target_pairs={{0,2},{1,3},{2,0},{3,1},{4,6},{5,7},{6,4},{7,5},{8,10},{9,11},{10,... | collective-permute-start | bytes 294920 | tf_op jit(solution)/shard_map/ppermute | solution.py:738
  217.2 3.3 %collective-permute-done.40 = bf16[2,144,384]{2,1,0:T(8,128)(2,1)S(1)} collective-permute-done((bf16[2,144,384]{2,1,0:T(8,128)(2,1)S(1)}, bf16[2,144,384]{2,1,0:T(8,128)(2,1)S(1)}, u32[]{:S(2)}, u32[]{:S(2)}) %collective-permute-start.40) | collective-permute-done | bytes 221216 | tf_op jit(solution)/shard_map/ppermute | solution.py:738
  220.6 4.1 %collective-permute-start.41 = (bf16[1,144,384]{2,1,0:T(8,128)(2,1)S(1)}, bf16[1,144,384]{2,1,0:T(8,128)(2,1)S(1)}, u32[]{:S(2)}, u32[]{:S(2)}) collective-permute-start(bf16[1,144,384]{2,1,0:T(8,128)(2,1)S(1)} %slice_bitcast_fusion.7), channel_id=1, source_target_pairs={{0,2},{1,3},{2,0},{3,1},{4,6},{5,7},{6,4},{7,5},{8,10},{9,11},{10,... | collective-permute-start | bytes 331784 | tf_op jit(solution)/shard_map/ppermute | solution.py:738
  235.5 4.3 %all-to-all-start.3 = ((bf16[8,48,384]{2,1,0:T(8,128)(2,1)}), bf16[8,48,384]{2,1,0:T(8,128)(2,1)}, u32[]{:S(2)}, u32[]{:S(2)}) async-start(bf16[8,48,384]{2,1,0:T(8,128)(2,1)} %bitcast.28), calls=%async_computation.3 | async-start | bytes 589824 | tf_op jit(solution)/shard_map/all_to_all | solution.py:837
  244.2 9.2 %collective-permute-done.50 = bf16[528,384]{1,0:T(8,128)(2,1)S(1)} collective-permute-done((bf16[528,384]{1,0:T(8,128)(2,1)}, bf16[528,384]{1,0:T(8,128)(2,1)S(1)}, u32[]{:S(2)}, u32[]{:S(2)}) %collective-permute-start.50) | collective-permute-done | bytes 405536 | tf_op jit(solution)/shard_map/ppermute | solution.py:738
  258.2 6.2 %collective-permute-done.46 = bf16[1,160,384]{2,1,0:T(8,128)(2,1)S(1)} collective-permute-done((bf16[1,160,384]{2,1,0:T(8,128)(2,1)S(1)}, bf16[1,160,384]{2,1,0:T(8,128)(2,1)S(1)}, u32[]{:S(2)}, u32[]{:S(2)}) %collective-permute-start.46) | collective-permute-done | bytes 122912 | tf_op jit(solution)/shard_map/ppermute | solution.py:738
  268.1 3.6 %collective-permute-done.49 = bf16[160,384]{1,0:T(8,128)(2,1)S(1)} collective-permute-done((bf16[160,384]{1,0:T(8,128)(2,1)S(1)}, bf16[160,384]{1,0:T(8,128)(2,1)S(1)}, u32[]{:S(2)}, u32[]{:S(2)}) %collective-permute-start.49) | collective-permute-done | bytes 122912 | tf_op jit(solution)/shard_map/ppermute | solution.py:738
  275.2 5.1 %unpack_early.1 = (f32[768,768]{1,0:T(8,128)}, f32[768,768]{1,0:T(8,128)}, f32[96,2304]{1,0:T(8,128)}, f32[96,768]{1,0:T(8,128)}, f32[192,768]{1,0:T(8,128)}) custom-call(bf16[4,528,384]{2,1,0:T(8,128)(2,1)} %copy-done, bf16[4,528,384]{2,1,0:T(8,128)(2,1)} %collective-permute-done.53.refs_1_), custom_call_target="tpu_custom_call" | custom-call | bytes 12000000 | tf_op jit(solution)/shard_map/unpack_early/pallas_call | solution.py:318
  (235 shorter events, 105.8 us)
Async XLA Ops:
  4.1 23.0 %all-to-all-start = ((bf16[8,48,384]{2,1,0:T(8,128)(2,1)}), bf16[8,48,384]{2,1,0:T(8,128)(2,1)S(1)}, u32[]{:S(2)}, u32[]{:S(2)}) async-start(bf16[8,48,384]{2,1,0:T(8,128)(2,1)} %collective-permute-done), calls=%async_computation | async-start | bytes 589824 | tf_op jit(solution)/shard_map/all_to_all | solution.py:837
  27.1 8.8 %collective-permute-start.3 = (bf16[192,384]{1,0:T(8,128)(2,1)S(1)}, bf16[192,384]{1,0:T(8,128)(2,1)S(1)}, u32[]{:S(2)}, u32[]{:S(2)}) collective-permute-start(bf16[192,384]{1,0:T(8,128)(2,1)S(1)} %dynamic-slice_bitcast_fusion), channel_id=1, source_target_pairs={{0,3},{1,2},{2,1},{3,0},{4,7},{5,6},{6,5},{7,4},{8,11},{9,10},{10,... | collective-permute-start | bytes 442376 | tf_op jit(solution)/shard_map/ppermute | solution.py:738
  28.4 12.7 %collective-permute-start.2 = (bf16[192,384]{1,0:T(8,128)(2,1)S(1)}, bf16[192,384]{1,0:T(8,128)(2,1)S(1)}, u32[]{:S(2)}, u32[]{:S(2)}) collective-permute-start(bf16[192,384]{1,0:T(8,128)(2,1)S(1)} %dynamic-slice_bitcast_fusion), channel_id=1, source_target_pairs={{0,2},{1,3},{2,0},{3,1},{4,6},{5,7},{6,4},{7,5},{8,10},{9,11},{10,... | collective-permute-start | bytes 442376 | tf_op jit(solution)/shard_map/ppermute | solution.py:738
  28.5 12.6 %collective-permute-start.1 = (bf16[192,384]{1,0:T(8,128)(2,1)S(1)}, bf16[192,384]{1,0:T(8,128)(2,1)S(1)}, u32[]{:S(2)}, u32[]{:S(2)}) collective-permute-start(bf16[192,384]{1,0:T(8,128)(2,1)S(1)} %dynamic-slice_bitcast_fusion), channel_id=1, source_target_pairs={{0,1},{1,0},{2,3},{3,2},{4,5},{5,4},{6,7},{7,6},{8,9},{9,8},{10,11... | collective-permute-start | bytes 442376 | tf_op jit(solution)/shard_map/ppermute | solution.py:738
  41.2 12.2 %collective-permute-start.5 = (bf16[576,384]{1,0:T(8,128)(2,1)S(1)}, bf16[576,384]{1,0:T(8,128)(2,1)S(1)}, u32[]{:S(2)}, u32[]{:S(2)}) collective-permute-start(bf16[576,384]{1,0:T(8,128)(2,1)S(1)} %constant_dynamic-update-slice_fusion.refs_0_.refs_10_), channel_id=1, source_target_pairs={{0,4},{4,0},{1,5},{5,1},{2,6},{6,2},{3,7},{7,3},{8,12},{12,8},{9,1... | collective-permute-start | bytes 1327112 | tf_op jit(solution)/shard_map/ppermute | solution.py:738
  53.5 12.1 %collective-permute-start.13 = (bf16[576,384]{1,0:T(8,128)(2,1)S(1)}, bf16[576,384]{1,0:T(8,128)(2,1)S(1)}, u32[]{:S(2)}, u32[]{:S(2)}) collective-permute-start(bf16[576,384]{1,0:T(8,128)(2,1)S(1)} %constant_dynamic-update-slice_fusion.refs_0_.refs_10_), channel_id=1, source_target_pairs={{0,8},{8,0},{1,9},{9,1},{2,10},{10,2},{3,11},{11,3},{4,12},{12,4},... | collective-permute-start | bytes 1327112 | tf_op jit(solution)/shard_map/ppermute | solution.py:738
  53.5 12.1 %collective-permute-start.14 = (bf16[576,384]{1,0:T(8,128)(2,1)S(1)}, bf16[576,384]{1,0:T(8,128)(2,1)S(1)}, u32[]{:S(2)}, u32[]{:S(2)}) collective-permute-start(bf16[576,384]{1,0:T(8,128)(2,1)S(1)} %collective-permute-done.5.refs_1_.refs_11_), channel_id=1, source_target_pairs={{0,8},{8,0},{1,9},{9,1},{2,10},{10,2},{3,11},{11,3},{4,12},{12,4},... | collective-permute-start | bytes 1327112 | tf_op jit(solution)/shard_map/ppermute | solution.py:738
  54.0 8.5 %collective-permute-start.12 = (bf16[64,768]{1,0:T(8,128)(2,1)}, bf16[64,768]{1,0:T(8,128)(2,1)S(1)}, u32[]{:S(2)}, u32[]{:S(2)}) collective-permute-start(bf16[64,768]{1,0:T(8,128)(2,1)} %get-tuple-element.163.refs_4_), channel_id=1, source_target_pairs={{0,3},{1,2},{2,1},{3,0},{4,7},{5,6},{6,5},{7,4},{8,11},{9,10},{10,... | collective-permute-start | bytes 294920 | tf_op jit(solution)/shard_map/ppermute | solution.py:738
  55.5 10.1 %collective-permute-start.11 = (bf16[64,768]{1,0:T(8,128)(2,1)}, bf16[64,768]{1,0:T(8,128)(2,1)S(1)}, u32[]{:S(2)}, u32[]{:S(2)}) collective-permute-start(bf16[64,768]{1,0:T(8,128)(2,1)} %get-tuple-element.163.refs_4_), channel_id=1, source_target_pairs={{0,2},{1,3},{2,0},{3,1},{4,6},{5,7},{6,4},{7,5},{8,10},{9,11},{10,... | collective-permute-start | bytes 294920 | tf_op jit(solution)/shard_map/ppermute | solution.py:738
  56.2 9.3 %collective-permute-start.10 = (bf16[64,768]{1,0:T(8,128)(2,1)}, bf16[64,768]{1,0:T(8,128)(2,1)S(1)}, u32[]{:S(2)}, u32[]{:S(2)}) collective-permute-start(bf16[64,768]{1,0:T(8,128)(2,1)} %get-tuple-element.163.refs_4_), channel_id=1, source_target_pairs={{0,1},{1,0},{2,3},{3,2},{4,5},{5,4},{6,7},{7,6},{8,9},{9,8},{10,11... | collective-permute-start | bytes 294920 | tf_op jit(solution)/shard_map/ppermute | solution.py:738
  72.7 9.7 %collective-permute-start.15 = (bf16[64,1536]{1,0:T(8,128)(2,1)}, bf16[64,1536]{1,0:T(8,128)(2,1)S(1)}, u32[]{:S(2)}, u32[]{:S(2)}) collective-permute-start(bf16[64,1536]{1,0:T(8,128)(2,1)} %get-tuple-element.159.refs_1_.refs_11_), channel_id=1, source_target_pairs={{0,8},{8,0},{1,9},{9,1},{2,10},{10,2},{3,11},{11,3},{4,12},{12,4},... | collective-permute-start | bytes 589832 | tf_op jit(solution)/shard_map/ppermute | solution.py:738
  94.1 9.6 %collective-permute-start.21 = (bf16[64,768]{1,0:T(8,128)(2,1)}, bf16[64,768]{1,0:T(8,128)(2,1)S(1)}, u32[]{:S(2)}, u32[]{:S(2)}) collective-permute-start(bf16[64,768]{1,0:T(8,128)(2,1)} %get-tuple-element.162.refs_0_), channel_id=1, source_target_pairs={{0,2},{1,3},{2,0},{3,1},{4,6},{5,7},{6,4},{7,5},{8,10},{9,11},{10,... | collective-permute-start | bytes 294920 | tf_op jit(solution)/shard_map/ppermute | solution.py:738
  94.7 9.1 %collective-permute-start.20 = (bf16[64,768]{1,0:T(8,128)(2,1)}, bf16[64,768]{1,0:T(8,128)(2,1)S(1)}, u32[]{:S(2)}, u32[]{:S(2)}) collective-permute-start(bf16[64,768]{1,0:T(8,128)(2,1)} %get-tuple-element.162.refs_0_), channel_id=1, source_target_pairs={{0,1},{1,0},{2,3},{3,2},{4,5},{5,4},{6,7},{7,6},{8,9},{9,8},{10,11... | collective-permute-start | bytes 294920 | tf_op jit(solution)/shard_map/ppermute | solution.py:738
  109.4 11.0 %collective-permute-start.24 = (bf16[64,768]{1,0:T(8,128)(2,1)}, bf16[64,768]{1,0:T(8,128)(2,1)S(1)}, u32[]{:S(2)}, u32[]{:S(2)}) collective-permute-start(bf16[64,768]{1,0:T(8,128)(2,1)} %get-tuple-element.170), channel_id=1, source_target_pairs={{0,2},{1,3},{2,0},{3,1},{4,6},{5,7},{6,4},{7,5},{8,10},{9,11},{10,... | collective-permute-start | bytes 294920 | tf_op jit(solution)/shard_map/ppermute | solution.py:738
  131.4 10.3 %collective-permute-start.29 = (bf16[32,1536]{1,0:T(8,128)(2,1)}, bf16[32,1536]{1,0:T(8,128)(2,1)S(1)}, u32[]{:S(2)}, u32[]{:S(2)}) collective-permute-start(bf16[32,1536]{1,0:T(8,128)(2,1)} %get-tuple-element.178), channel_id=1, source_target_pairs={{2,0},{10,8},{3,1},{11,9},{4,2},{12,10},{5,3},{13,11},{6,4},{14,12... | collective-permute-start | bytes 294920 | tf_op jit(solution)/shard_map/ppermute | solution.py:767
  132.9 10.1 %collective-permute-start.26 = (bf16[64,1536]{1,0:T(8,128)(2,1)}, bf16[64,1536]{1,0:T(8,128)(2,1)S(1)}, u32[]{:S(2)}, u32[]{:S(2)}) collective-permute-start(bf16[64,1536]{1,0:T(8,128)(2,1)} %get-tuple-element.176), channel_id=1, source_target_pairs={{0,8},{8,0},{1,9},{9,1},{2,10},{10,2},{3,11},{11,3},{4,12},{12,4},... | collective-permute-start | bytes 589832 | tf_op jit(solution)/shard_map/ppermute | solution.py:738
  151.9 9.9 %collective-permute-start.32 = (bf16[4,4,144,384]{3,2,1,0:T(8,128)(2,1)}, bf16[4,4,144,384]{3,2,1,0:T(8,128)(2,1)S(1)}, u32[]{:S(2)}, u32[]{:S(2)}) collective-permute-start(bf16[4,4,144,384]{3,2,1,0:T(8,128)(2,1)} %get-tuple-element.190), channel_id=1, source_target_pairs={{0,8},{8,0},{1,9},{9,1},{2,10},{10,2},{3,11},{11,3},{4,12},{12,4},... | collective-permute-start | bytes 5308424 | tf_op jit(solution)/shard_map/ppermute | solution.py:738
  164.3 39.9 %all-to-all-start.1 = ((bf16[4,960,384]{2,1,0:T(8,128)(2,1)}), bf16[4,960,384]{2,1,0:T(8,128)(2,1)S(1)}, u32[]{:S(2)}, u32[]{:S(2)}) async-start(bf16[4,960,384]{2,1,0:T(8,128)(2,1)} %pad_maximum_fusion), calls=%async_computation.1 | async-start | bytes 5898240 | tf_op jit(solution)/shard_map/all_to_all | solution.py:837
  179.5 18.9 %collective-permute-start.33 = (bf16[4,4,96,384]{3,2,1,0:T(8,128)(2,1)}, bf16[4,4,96,384]{3,2,1,0:T(8,128)(2,1)S(1)}, u32[]{:S(2)}, u32[]{:S(2)}) collective-permute-start(bf16[4,4,96,384]{3,2,1,0:T(8,128)(2,1)} %get-tuple-element.196), channel_id=1, source_target_pairs={{0,8},{8,0},{1,9},{9,1},{2,10},{10,2},{3,11},{11,3},{4,12},{12,4},... | collective-permute-start | bytes 3538952 | tf_op jit(solution)/shard_map/ppermute | solution.py:738
  205.5 29.8 %all-to-all-start.2 = ((bf16[4,592,384]{2,1,0:T(8,128)(2,1)}), bf16[4,592,384]{2,1,0:T(8,128)(2,1)S(1)}, u32[]{:S(2)}, u32[]{:S(2)}) async-start(bf16[4,592,384]{2,1,0:T(8,128)(2,1)} %pad_maximum_fusion.1), calls=%async_computation.2 | async-start | bytes 3637248 | tf_op jit(solution)/shard_map/all_to_all | solution.py:837
  210.1 10.4 %collective-permute-start.40 = (bf16[2,144,384]{2,1,0:T(8,128)(2,1)S(1)}, bf16[2,144,384]{2,1,0:T(8,128)(2,1)S(1)}, u32[]{:S(2)}, u32[]{:S(2)}) collective-permute-start(bf16[2,144,384]{2,1,0:T(8,128)(2,1)S(1)} %slice_bitcast_fusion.3), channel_id=1, source_target_pairs={{0,1},{1,0},{2,3},{3,2},{4,5},{5,4},{6,7},{7,6},{8,9},{9,8},{10,11... | collective-permute-start | bytes 663560 | tf_op jit(solution)/shard_map/ppermute | solution.py:738
  210.2 14.6 %collective-permute-start.42 = (bf16[64,768]{1,0:T(8,128)(2,1)S(1)}, bf16[64,768]{1,0:T(8,128)(2,1)S(1)}, u32[]{:S(2)}, u32[]{:S(2)}) collective-permute-start(bf16[64,768]{1,0:T(8,128)(2,1)S(1)} %copy-done.47), channel_id=1, source_target_pairs={{0,1},{1,0},{2,3},{3,2},{4,5},{5,4},{6,7},{7,6},{8,9},{9,8},{10,11... | collective-permute-start | bytes 294920 | tf_op jit(solution)/shard_map/ppermute | solution.py:738
  212.2 12.6 %collective-permute-start.43 = (bf16[64,768]{1,0:T(8,128)(2,1)S(1)}, bf16[64,768]{1,0:T(8,128)(2,1)S(1)}, u32[]{:S(2)}, u32[]{:S(2)}) collective-permute-start(bf16[64,768]{1,0:T(8,128)(2,1)S(1)} %copy-done.46), channel_id=1, source_target_pairs={{0,2},{1,3},{2,0},{3,1},{4,6},{5,7},{6,4},{7,5},{8,10},{9,11},{10,... | collective-permute-start | bytes 294920 | tf_op jit(solution)/shard_map/ppermute | solution.py:738
  215.7 12.0 %collective-permute-start.44 = (bf16[64,768]{1,0:T(8,128)(2,1)S(1)}, bf16[64,768]{1,0:T(8,128)(2,1)S(1)}, u32[]{:S(2)}, u32[]{:S(2)}) collective-permute-start(bf16[64,768]{1,0:T(8,128)(2,1)S(1)} %copy-done.45), channel_id=1, source_target_pairs={{0,3},{1,2},{2,1},{3,0},{4,7},{5,6},{6,5},{7,4},{8,11},{9,10},{10,... | collective-permute-start | bytes 294920 | tf_op jit(solution)/shard_map/ppermute | solution.py:738
  220.6 10.2 %collective-permute-start.41 = (bf16[1,144,384]{2,1,0:T(8,128)(2,1)S(1)}, bf16[1,144,384]{2,1,0:T(8,128)(2,1)S(1)}, u32[]{:S(2)}, u32[]{:S(2)}) collective-permute-start(bf16[1,144,384]{2,1,0:T(8,128)(2,1)S(1)} %slice_bitcast_fusion.7), channel_id=1, source_target_pairs={{0,2},{1,3},{2,0},{3,1},{4,6},{5,7},{6,4},{7,5},{8,10},{9,11},{10,... | collective-permute-start | bytes 331784 | tf_op jit(solution)/shard_map/ppermute | solution.py:738
  231.7 12.5 %collective-permute-start.51 = (bf16[528,384]{1,0:T(8,128)(2,1)}, bf16[528,384]{1,0:T(8,128)(2,1)S(1)}, u32[]{:S(2)}, u32[]{:S(2)}) collective-permute-start(bf16[528,384]{1,0:T(8,128)(2,1)} %get-tuple-element.250), channel_id=1, source_target_pairs={{0,16},{4,20},{16,0},{20,4},{1,17},{5,21},{17,1},{21,5},{2,18},{6,... | collective-permute-start | bytes 1216520 | tf_op jit(solution)/shard_map/ppermute | solution.py:738
  233.8 19.6 %collective-permute-start.50 = (bf16[528,384]{1,0:T(8,128)(2,1)}, bf16[528,384]{1,0:T(8,128)(2,1)S(1)}, u32[]{:S(2)}, u32[]{:S(2)}) collective-permute-start(bf16[528,384]{1,0:T(8,128)(2,1)} %get-tuple-element.250), channel_id=1, source_target_pairs={{0,4},{4,0},{16,20},{20,16},{1,5},{5,1},{17,21},{21,17},{2,6},{6,2... | collective-permute-start | bytes 1216520 | tf_op jit(solution)/shard_map/ppermute | solution.py:738
  235.1 18.3 %collective-permute-start.52 = (bf16[528,384]{1,0:T(8,128)(2,1)}, bf16[528,384]{1,0:T(8,128)(2,1)}, u32[]{:S(2)}, u32[]{:S(2)}) collective-permute-start(bf16[528,384]{1,0:T(8,128)(2,1)} %get-tuple-element.250), channel_id=1, source_target_pairs={{0,20},{4,16},{16,4},{20,0},{1,21},{5,17},{17,5},{21,1},{2,22},{6,... | collective-permute-start | bytes 1216520 | tf_op jit(solution)/shard_map/ppermute | solution.py:738
  235.5 19.1 %all-to-all-start.3 = ((bf16[8,48,384]{2,1,0:T(8,128)(2,1)}), bf16[8,48,384]{2,1,0:T(8,128)(2,1)}, u32[]{:S(2)}, u32[]{:S(2)}) async-start(bf16[8,48,384]{2,1,0:T(8,128)(2,1)} %bitcast.28), calls=%async_computation.3 | async-start | bytes 589824 | tf_op jit(solution)/shard_map/all_to_all | solution.py:837
  240.7 14.1 %collective-permute-start.45 = (bf16[2,160,384]{2,1,0:T(8,128)(2,1)}, bf16[2,160,384]{2,1,0:T(8,128)(2,1)}, u32[]{:S(2)}, u32[]{:S(2)}) collective-permute-start(bf16[2,160,384]{2,1,0:T(8,128)(2,1)} %slice_bitcast_fusion.1), channel_id=1, source_target_pairs={{0,1},{1,0},{2,3},{3,2},{4,5},{5,4},{6,7},{7,6},{8,9},{9,8},{10,11... | collective-permute-start | bytes 737288 | tf_op jit(solution)/shard_map/ppermute | solution.py:738
  254.6 20.6 %collective-permute-start.53 = (bf16[4,528,384]{2,1,0:T(8,128)(2,1)S(1)}, bf16[4,528,384]{2,1,0:T(8,128)(2,1)}, u32[]{:S(2)}, u32[]{:S(2)}) collective-permute-start(bf16[4,528,384]{2,1,0:T(8,128)(2,1)S(1)} %pad_maximum_fusion.2.refs_0_), channel_id=1, source_target_pairs={{0,8},{8,0},{1,9},{9,1},{2,10},{10,2},{3,11},{11,3},{4,12},{12,4},... | collective-permute-start | bytes 4866056 | tf_op jit(solution)/shard_map/ppermute | solution.py:738
  256.6 16.8 %collective-permute-start.54 = (bf16[8,48,384]{2,1,0:T(8,128)(2,1)}, bf16[8,48,384]{2,1,0:T(8,128)(2,1)S(1)}, u32[]{:S(2)}, u32[]{:S(2)}) collective-permute-start(bf16[8,48,384]{2,1,0:T(8,128)(2,1)} %all-to-all-done.3), channel_id=1, source_target_pairs={{0,0},{4,8},{8,4},{12,12},{1,1},{5,9},{9,5},{13,13},{2,2},{6,10},{... | collective-permute-start | bytes 884744 | tf_op jit(solution)/shard_map/ppermute | solution.py:749
  (76 other events, 477.3 us)

commit v5 on v4

--- a/solution.py
+++ b/solution.py
@@ -914,7 +914,7 @@
     )
     pairs_a = share_pairs(plan, pair_a, squeeze_a)
     hidden = [((tensor, width, expand_a.shape[1]), BF16), ((tensor, reduce_a.shape[0], width), BF16)]
-    mine, pairs_a[1] = lax.optimization_barrier((mine, pairs_a[1]))
+    mine, pairs_a[2] = lax.optimization_barrier((mine, pairs_a[2]))
     mine = jnp.concatenate(mine, axis=0)
     weights = [mine, exchange(mine, "near", 1)]
     weights, cots, pairs_a = lax.optimization_barrier((weights, cot, pairs_a))
@@ -928,7 +928,6 @@
         [resets, videos],
         [((8, 128), F32)],
     )
-    m_a, cots = lax.optimization_barrier((m_a, cots))
     y_a, n_b, q_b, base, *pair_b = call(
         "between",
         functools.partial(between_body, plan),
@@ -937,6 +936,7 @@
         (),
         hidden,
     )
+    pair_b, cots = lax.optimization_barrier((pair_b, cots))
     pairs_b = share_pairs(plan, pair_b, squeeze_b)
     or_b, m_b, l_b, probs_b = call(
         "second",

time: 287 us -> 285 us (level)
    ppermute x46, waiting for transfers between devices: 67.2 us -> 62.5 us  [exchange(): lax.ppermute(values, tuple(order), [(i, int(where[p ^ by])) for i, p in e...]
  transfers between devices with their start and end apart: 60 -> 60, of which waited for: 32 -> 32; matrix products, arithmetic and copies ran while one was open for 4% -> 4% of each run, Pallas kernels for 10% -> 12%
where the time goes in v5:
time: 285 us; the launch traced here: 284 us
  waiting for transfers between devices  97.2 us (34%)
  starting transfers between devices  90.6 us (32%)
  Pallas kernels  71.3 us (25%)
  other arithmetic  12.2 us (4%)
  local copies, waits for them, and re-layouts  11.1 us (4%)
    pallas_call x13, Pallas kernels, call(): pl.pallas_call(body, out_shape=[jax.ShapeDtypeStruct(shape, dtype) for sh...  71.3 us
    ppermute x46, waiting for transfers between devices, exchange(): lax.ppermute(values, tuple(order), [(i, int(where[p ^ by])) for i, p in e...  62.5 us
    ppermute x46, starting transfers between devices, exchange(): lax.ppermute(values, tuple(order), [(i, int(where[p ^ by])) for i, p in e...  45.5 us
    all_to_all x4, starting transfers between devices, spread(): return lax.all_to_all(values, axes, 0, 0, tiled=True)  26.8 us
    ppermute x8, waiting for transfers between devices, shift(): return lax.ppermute(values, EVERY, pairs)  19.6 us
    ppermute x8, starting transfers between devices, shift(): return lax.ppermute(values, EVERY, pairs)  15.3 us
    all_to_all x4, waiting for transfers between devices, spread(): return lax.all_to_all(values, axes, 0, 0, tiled=True)  15.1 us
    unnamed x98, local copies, waits for them, and re-layouts  6.47 us
  transfers between devices with their start and end apart: 60, of which 32 were waited for; matrix products, arithmetic and copies ran while one was open for 4% of the time, Pallas kernels for 12%

profile of v5, /device:TPU:0, one launch (start us, length us, event | category | flops | bytes accessed | tf_op | source)
XLA Modules:
  0.0 284.1 jit_solution(1085568244020263309)
XLA Ops:
  4.1 12.6 %all-to-all-start = ((bf16[8,48,384]{2,1,0:T(8,128)(2,1)}), bf16[8,48,384]{2,1,0:T(8,128)(2,1)S(1)}, u32[]{:S(2)}, u32[]{:S(2)}) async-start(bf16[8,48,384]{2,1,0:T(8,128)(2,1)} %collective-permute-done), calls=%async_computation | async-start | bytes 589824 | tf_op jit(solution)/shard_map/all_to_all | solution.py:837
  16.8 10.3 %all-to-all-done = bf16[8,48,384]{2,1,0:T(8,128)(2,1)S(1)} async-done(((bf16[8,48,384]{2,1,0:T(8,128)(2,1)}), bf16[8,48,384]{2,1,0:T(8,128)(2,1)S(1)}, u32[]{:S(2)}, u32[]{:S(2)}) %all-to-all-start) | async-done | bytes 294944 | tf_op jit(solution)/shard_map/all_to_all | solution.py:837
  28.5 3.0 %collective-permute-start.1 = (bf16[192,384]{1,0:T(8,128)(2,1)S(1)}, bf16[192,384]{1,0:T(8,128)(2,1)S(1)}, u32[]{:S(2)}, u32[]{:S(2)}) collective-permute-start(bf16[192,384]{1,0:T(8,128)(2,1)S(1)} %dynamic-slice_bitcast_fusion), channel_id=1, source_target_pairs={{0,1},{1,0},{2,3},{3,2},{4,5},{5,4},{6,7},{7,6},{8,9},{9,8},{10,11... | collective-permute-start | bytes 442376 | tf_op jit(solution)/shard_map/ppermute | solution.py:738
  41.5 3.8 %collective-permute-start.5 = (bf16[576,384]{1,0:T(8,128)(2,1)S(1)}, bf16[576,384]{1,0:T(8,128)(2,1)S(1)}, u32[]{:S(2)}, u32[]{:S(2)}) collective-permute-start(bf16[576,384]{1,0:T(8,128)(2,1)S(1)} %constant_dynamic-update-slice_fusion.refs_0_.refs_10_), channel_id=1, source_target_pairs={{0,4},{4,0},{1,5},{5,1},{2,6},{6,2},{3,7},{7,3},{8,12},{12,8},{9,1... | collective-permute-start | bytes 1327112 | tf_op jit(solution)/shard_map/ppermute | solution.py:738
  49.7 3.8 %collective-permute-done.5.refs_1_.refs_11_ = bf16[576,384]{1,0:T(8,128)(2,1)S(1)} collective-permute-done((bf16[576,384]{1,0:T(8,128)(2,1)S(1)}, bf16[576,384]{1,0:T(8,128)(2,1)S(1)}, u32[]{:S(2)}, u32[]{:S(2)}) %collective-permute-start.5) | collective-permute-done | bytes 442400 | tf_op jit(solution)/shard_map/ppermute | solution.py:738
  58.4 4.1 %first.1 = (bf16[256,384]{1,0:T(8,128)(2,1)}, f32[256,384]{1,0:T(8,128)}, bf16[256,384]{1,0:T(8,128)(2,1)}, bf16[1024,192]{1,0:T(8,128)(2,1)}) custom-call(s32[16]{0:T(128)} %resets.7, s32[16]{0:T(128)} %videos.7, bf16[256,384]{1,0:T(8,128)(2,1)} %get-tuple-element.137.refs_0_.refs_10_, bf16[256,384]{1,0:T(8,128)(2,1)} %get-tuple-element.138.refs_1_.refs_6_, ...), custom_call_target="tpu_custom_call" | custom-call | bytes 12000000 | tf_op jit(solution)/shard_map/first/pallas_call | solution.py:318
  63.4 6.2 %between.1 = (f32[256,384]{1,0:T(8,128)}, bf16[256,384]{1,0:T(8,128)(2,1)}, bf16[64,768]{1,0:T(8,128)(2,1)}, f32[64,768]{1,0:T(8,128)}, bf16[64,1536]{1,0:T(8,128)(2,1)}, /*index=5*/bf16[16,1536]{1,0:T(8,128)(2,1)}) custom-call(f32[256,384]{1,0:T(8,128)} %get-tuple-element.153.m_ref.refs_1_, bf16[256,384]{1,0:T(8,128)(2,1)} %get-tuple-element.154.l_ref.refs_2_, ...), custom_call_target="tpu_custom_call" | custom-call | bytes 18000000 | tf_op jit(solution)/shard_map/between/pallas_call | solution.py:318
  72.2 4.1 %collective-permute-start.16 = (bf16[16,1536]{1,0:T(8,128)(2,1)}, bf16[16,1536]{1,0:T(8,128)(2,1)S(1)}, u32[]{:S(2)}, u32[]{:S(2)}) collective-permute-start(bf16[16,1536]{1,0:T(8,128)(2,1)} %get-tuple-element.162), channel_id=1, source_target_pairs={{0,1},{8,9},{1,2},{9,10},{2,3},{10,11},{3,4},{11,12},{4,5},{12,13}... | collective-permute-start | bytes 147464 | tf_op jit(solution)/shard_map/ppermute | solution.py:767
  80.1 7.2 %second.1 = (bf16[64,768]{1,0:T(8,128)(2,1)}, f32[64,768]{1,0:T(8,128)}, bf16[64,768]{1,0:T(8,128)(2,1)}, bf16[512,192]{1,0:T(8,128)(2,1)}) custom-call(s32[16]{0:T(128)} %resets.7, s32[16]{0:T(128)} %videos.7, bf16[64,768]{1,0:T(8,128)(2,1)} %get-tuple-element.157.refs_0_.refs_9_, bf16[64,1536]{1,0:T(8,128)(2,1)} %get-tuple-element.161.refs_1_.refs_11_, ...), custom_call_target="tpu_custom_call" | custom-call | bytes 21000000 | tf_op jit(solution)/shard_map/second/pallas_call | solution.py:318
  87.3 3.8 %collective-permute-start.22 = (bf16[64,768]{1,0:T(8,128)(2,1)}, bf16[64,768]{1,0:T(8,128)(2,1)S(1)}, u32[]{:S(2)}, u32[]{:S(2)}) collective-permute-start(bf16[64,768]{1,0:T(8,128)(2,1)} %get-tuple-element.164.refs_0_), channel_id=1, source_target_pairs={{0,3},{1,2},{2,1},{3,0},{4,7},{5,6},{6,5},{7,4},{8,11},{9,10},{10,... | collective-permute-start | bytes 294920 | tf_op jit(solution)/shard_map/ppermute | solution.py:738
  94.6 6.1 %collective-permute-done.21.refs_2_ = bf16[64,768]{1,0:T(8,128)(2,1)S(1)} collective-permute-done((bf16[64,768]{1,0:T(8,128)(2,1)}, bf16[64,768]{1,0:T(8,128)(2,1)S(1)}, u32[]{:S(2)}, u32[]{:S(2)}) %collective-permute-start.21) | collective-permute-done | bytes 98336 | tf_op jit(solution)/shard_map/ppermute | solution.py:738
  102.0 3.9 %hidden.1 = (bf16[64,768]{1,0:T(8,128)(2,1)}, bf16[64,768]{1,0:T(8,128)(2,1)}, bf16[64,768]{1,0:T(8,128)(2,1)}, bf16[64,768]{1,0:T(8,128)(2,1)}, bf16[256,768]{1,0:T(8,128)(2,1)}, /*index=5*/bf16[256,768]{1,0:T(8,128)(2,1)}) custom-call(bf16[768,768]{1,0:T(8,128)(2,1)} %up.1, bf16[768,768]{1,0:T(8,128)(2,1)} %down.3, ...), custom_call_target="tpu_custom_call" | custom-call | bytes 12000000 | tf_op jit(solution)/shard_map/hidden/pallas_call | solution.py:318
  106.4 3.3 %collective-permute-start.24 = (bf16[64,768]{1,0:T(8,128)(2,1)}, bf16[64,768]{1,0:T(8,128)(2,1)S(1)}, u32[]{:S(2)}, u32[]{:S(2)}) collective-permute-start(bf16[64,768]{1,0:T(8,128)(2,1)} %get-tuple-element.172), channel_id=1, source_target_pairs={{0,2},{1,3},{2,0},{3,1},{4,6},{5,7},{6,4},{7,5},{8,10},{9,11},{10,... | collective-permute-start | bytes 294920 | tf_op jit(solution)/shard_map/ppermute | solution.py:738
  112.1 5.3 %collective-permute-done.24.refs_2_ = bf16[64,768]{1,0:T(8,128)(2,1)S(1)} collective-permute-done((bf16[64,768]{1,0:T(8,128)(2,1)}, bf16[64,768]{1,0:T(8,128)(2,1)S(1)}, u32[]{:S(2)}, u32[]{:S(2)}) %collective-permute-start.24) | collective-permute-done | bytes 98336 | tf_op jit(solution)/shard_map/ppermute | solution.py:738
  118.1 9.0 %second_back.1 = (f32[64,768]{1,0:T(8,128)}, f32[1,768]{1,0:T(1,128)}, bf16[768,768]{1,0:T(8,128)(2,1)}, f32[64,768]{1,0:T(8,128)}, f32[8,128]{1,0:T(8,128)}, /*...) custom-call(s32[16]{0:T(128)} %resets.7, s32[16]{0:T(128)} %videos.7, ...), custom_call_target="tpu_custom_call" | custom-call | bytes 27000000 | tf_op jit(solution)/shard_map/second_back/pallas_call | solution.py:318
  130.0 4.5 %collective-permute-done.27.refs_2_ = bf16[32,1536]{1,0:T(8,128)(2,1)S(1)} collective-permute-done((bf16[32,1536]{1,0:T(8,128)(2,1)}, bf16[32,1536]{1,0:T(8,128)(2,1)S(1)}, u32[]{:S(2)}, u32[]{:S(2)}) %collective-permute-start.27) | collective-permute-done | bytes 98336 | tf_op jit(solution)/shard_map/ppermute | solution.py:767
  134.5 4.3 %collective-permute-done.29.refs_4_ = bf16[32,1536]{1,0:T(8,128)(2,1)S(1)} collective-permute-done((bf16[32,1536]{1,0:T(8,128)(2,1)}, bf16[32,1536]{1,0:T(8,128)(2,1)S(1)}, u32[]{:S(2)}, u32[]{:S(2)}) %collective-permute-start.29) | collective-permute-done | bytes 98336 | tf_op jit(solution)/shard_map/ppermute | solution.py:767
  140.8 8.2 %cross.1 = (f32[256,384]{1,0:T(8,128)}, f32[3,4,768]{2,1,0:T(4,128)}, f32[2,4,768]{2,1,0:T(4,128)}, f32[1,384]{1,0:T(1,128)}, bf16[4,4,144,384]{3,2,1,0:T(8,128)(2,1)}, /*index=5*/bf16[4,4,144,384]{3,2,1,0:T(8,128)(2,1)}) custom-call(f32[64,1536]{1,0:T(8,128)} %get-tuple-element.177.refs_0_, bf16[64,1536]{1,0:T(8,128)(2,1)} %copy-done.21, ...), custom_call_target="tpu_custom_call" | custom-call | bytes 24000000 | tf_op jit(solution)/shard_map/cross/pallas_call | solution.py:318
  149.2 4.8 %hidden_rest.1 = (bf16[64,768]{1,0:T(8,128)(2,1)}, bf16[64,768]{1,0:T(8,128)(2,1)}, bf16[64,768]{1,0:T(8,128)(2,1)}, bf16[64,768]{1,0:T(8,128)(2,1)}, bf16[4,1,3...) custom-call(bf16[768,768]{1,0:T(8,128)(2,1)} %down.3, bf16[256,768]{1,0:T(8,128)(2,1)} %get-tuple-element.187.hidden_ref, ...), custom_call_target="tpu_custom_call" | custom-call | bytes 15000000 | tf_op jit(solution)/shard_map/hidden_rest/pallas_call | solution.py:318
  161.3 5.1 %all-to-all-start.1 = ((bf16[4,960,384]{2,1,0:T(8,128)(2,1)}), bf16[4,960,384]{2,1,0:T(8,128)(2,1)S(1)}, u32[]{:S(2)}, u32[]{:S(2)}) async-start(bf16[4,960,384]{2,1,0:T(8,128)(2,1)} %pad_maximum_fusion), calls=%async_computation.1 | async-start | bytes 5898240 | tf_op jit(solution)/shard_map/all_to_all | solution.py:837
  166.5 10.1 %first_back.1 = (f32[1,384]{1,0:T(1,128)}, f32[256,384]{1,0:T(8,128)}, bf16[384,384]{1,0:T(8,128)(2,1)}, f32[256,384]{1,0:T(8,128)}, f32[8,128]{1,0:T(8,128)}, /...) custom-call(s32[16]{0:T(128)} %resets.7, ...), custom_call_target="tpu_custom_call" | custom-call | bytes 30000000 | tf_op jit(solution)/shard_map/first_back/pallas_call | solution.py:318
  186.9 4.9 %leave.1 = (bf16[256,384]{1,0:T(8,128)(2,1)}, bf16[4,1,208,384]{3,2,1,0:T(8,128)(2,1)}, bf16[4,1,208,384]{3,2,1,0:T(8,128)(2,1)}) custom-call(f32[64,768]{1,0:T(8,128)} %get-tuple-element.199.refs_0_, bf16[64,768]{1,0:T(8,128)(2,1)} %copy-done.26, bf16[32,768]{1,0:T(8,128)(2,1)} %copy-done.41, bf16[32,768]{1,0:T(8,128)(2,1)} %copy-done.43, ...), custom_call_target="tpu_custom_call" | custom-call | bytes 15000000 | tf_op jit(solution)/shard_map/leave/pallas_call | solution.py:318
  197.2 4.7 %all-to-all-done.1 = bf16[4,960,384]{2,1,0:T(8,128)(2,1)S(1)} async-done(((bf16[4,960,384]{2,1,0:T(8,128)(2,1)}), bf16[4,960,384]{2,1,0:T(8,128)(2,1)S(1)}, u32[]{:S(2)}, u32[]{:S(2)}) %all-to-all-start.1) | async-done | bytes 2949152 | tf_op jit(solution)/shard_map/all_to_all | solution.py:837
  203.1 5.0 %all-to-all-start.2 = ((bf16[4,592,384]{2,1,0:T(8,128)(2,1)}), bf16[4,592,384]{2,1,0:T(8,128)(2,1)S(1)}, u32[]{:S(2)}, u32[]{:S(2)}) async-start(bf16[4,592,384]{2,1,0:T(8,128)(2,1)} %pad_maximum_fusion.1), calls=%async_computation.2 | async-start | bytes 3637248 | tf_op jit(solution)/shard_map/all_to_all | solution.py:837
  210.3 3.5 %collective-permute-start.43 = (bf16[64,768]{1,0:T(8,128)(2,1)S(1)}, bf16[64,768]{1,0:T(8,128)(2,1)S(1)}, u32[]{:S(2)}, u32[]{:S(2)}) collective-permute-start(bf16[64,768]{1,0:T(8,128)(2,1)S(1)} %copy-done.46), channel_id=1, source_target_pairs={{0,2},{1,3},{2,0},{3,1},{4,6},{5,7},{6,4},{7,5},{8,10},{9,11},{10,... | collective-permute-start | bytes 294920 | tf_op jit(solution)/shard_map/ppermute | solution.py:738
  215.2 3.4 %collective-permute-done.40 = bf16[2,144,384]{2,1,0:T(8,128)(2,1)S(1)} collective-permute-done((bf16[2,144,384]{2,1,0:T(8,128)(2,1)S(1)}, bf16[2,144,384]{2,1,0:T(8,128)(2,1)S(1)}, u32[]{:S(2)}, u32[]{:S(2)}) %collective-permute-start.40) | collective-permute-done | bytes 221216 | tf_op jit(solution)/shard_map/ppermute | solution.py:738
  218.7 4.2 %collective-permute-start.41 = (bf16[1,144,384]{2,1,0:T(8,128)(2,1)S(1)}, bf16[1,144,384]{2,1,0:T(8,128)(2,1)S(1)}, u32[]{:S(2)}, u32[]{:S(2)}) collective-permute-start(bf16[1,144,384]{2,1,0:T(8,128)(2,1)S(1)} %slice_bitcast_fusion.7), channel_id=1, source_target_pairs={{0,2},{1,3},{2,0},{3,1},{4,6},{5,7},{6,4},{7,5},{8,10},{9,11},{10,... | collective-permute-start | bytes 331784 | tf_op jit(solution)/shard_map/ppermute | solution.py:738
  234.0 4.1 %all-to-all-start.3 = ((bf16[8,48,384]{2,1,0:T(8,128)(2,1)}), bf16[8,48,384]{2,1,0:T(8,128)(2,1)}, u32[]{:S(2)}, u32[]{:S(2)}) async-start(bf16[8,48,384]{2,1,0:T(8,128)(2,1)} %bitcast.28), calls=%async_computation.3 | async-start | bytes 589824 | tf_op jit(solution)/shard_map/all_to_all | solution.py:837
  242.7 9.3 %collective-permute-done.50 = bf16[528,384]{1,0:T(8,128)(2,1)S(1)} collective-permute-done((bf16[528,384]{1,0:T(8,128)(2,1)}, bf16[528,384]{1,0:T(8,128)(2,1)S(1)}, u32[]{:S(2)}, u32[]{:S(2)}) %collective-permute-start.50) | collective-permute-done | bytes 405536 | tf_op jit(solution)/shard_map/ppermute | solution.py:738
  256.5 6.3 %collective-permute-done.46 = bf16[1,160,384]{2,1,0:T(8,128)(2,1)S(1)} collective-permute-done((bf16[1,160,384]{2,1,0:T(8,128)(2,1)S(1)}, bf16[1,160,384]{2,1,0:T(8,128)(2,1)S(1)}, u32[]{:S(2)}, u32[]{:S(2)}) %collective-permute-start.46) | collective-permute-done | bytes 122912 | tf_op jit(solution)/shard_map/ppermute | solution.py:738
  266.4 3.6 %collective-permute-done.49 = bf16[160,384]{1,0:T(8,128)(2,1)S(1)} collective-permute-done((bf16[160,384]{1,0:T(8,128)(2,1)S(1)}, bf16[160,384]{1,0:T(8,128)(2,1)S(1)}, u32[]{:S(2)}, u32[]{:S(2)}) %collective-permute-start.49) | collective-permute-done | bytes 122912 | tf_op jit(solution)/shard_map/ppermute | solution.py:738
  273.6 5.1 %unpack_early.1 = (f32[768,768]{1,0:T(8,128)}, f32[768,768]{1,0:T(8,128)}, f32[96,2304]{1,0:T(8,128)}, f32[96,768]{1,0:T(8,128)}, f32[192,768]{1,0:T(8,128)}) custom-call(bf16[4,528,384]{2,1,0:T(8,128)(2,1)} %copy-done, bf16[4,528,384]{2,1,0:T(8,128)(2,1)} %collective-permute-done.53.refs_1_), custom_call_target="tpu_custom_call" | custom-call | bytes 12000000 | tf_op jit(solution)/shard_map/unpack_early/pallas_call | solution.py:318
  (235 shorter events, 104.9 us)
Async XLA Ops:
  4.1 23.0 %all-to-all-start = ((bf16[8,48,384]{2,1,0:T(8,128)(2,1)}), bf16[8,48,384]{2,1,0:T(8,128)(2,1)S(1)}, u32[]{:S(2)}, u32[]{:S(2)}) async-start(bf16[8,48,384]{2,1,0:T(8,128)(2,1)} %collective-permute-done), calls=%async_computation | async-start | bytes 589824 | tf_op jit(solution)/shard_map/all_to_all | solution.py:837
  27.1 11.6 %collective-permute-start.3 = (bf16[192,384]{1,0:T(8,128)(2,1)S(1)}, bf16[192,384]{1,0:T(8,128)(2,1)S(1)}, u32[]{:S(2)}, u32[]{:S(2)}) collective-permute-start(bf16[192,384]{1,0:T(8,128)(2,1)S(1)} %dynamic-slice_bitcast_fusion), channel_id=1, source_target_pairs={{0,3},{1,2},{2,1},{3,0},{4,7},{5,6},{6,5},{7,4},{8,11},{9,10},{10,... | collective-permute-start | bytes 442376 | tf_op jit(solution)/shard_map/ppermute | solution.py:738
  28.4 13.0 %collective-permute-start.2 = (bf16[192,384]{1,0:T(8,128)(2,1)S(1)}, bf16[192,384]{1,0:T(8,128)(2,1)S(1)}, u32[]{:S(2)}, u32[]{:S(2)}) collective-permute-start(bf16[192,384]{1,0:T(8,128)(2,1)S(1)} %dynamic-slice_bitcast_fusion), channel_id=1, source_target_pairs={{0,2},{1,3},{2,0},{3,1},{4,6},{5,7},{6,4},{7,5},{8,10},{9,11},{10,... | collective-permute-start | bytes 442376 | tf_op jit(solution)/shard_map/ppermute | solution.py:738
  28.5 12.9 %collective-permute-start.1 = (bf16[192,384]{1,0:T(8,128)(2,1)S(1)}, bf16[192,384]{1,0:T(8,128)(2,1)S(1)}, u32[]{:S(2)}, u32[]{:S(2)}) collective-permute-start(bf16[192,384]{1,0:T(8,128)(2,1)S(1)} %dynamic-slice_bitcast_fusion), channel_id=1, source_target_pairs={{0,1},{1,0},{2,3},{3,2},{4,5},{5,4},{6,7},{7,6},{8,9},{9,8},{10,11... | collective-permute-start | bytes 442376 | tf_op jit(solution)/shard_map/ppermute | solution.py:738
  41.5 11.9 %collective-permute-start.5 = (bf16[576,384]{1,0:T(8,128)(2,1)S(1)}, bf16[576,384]{1,0:T(8,128)(2,1)S(1)}, u32[]{:S(2)}, u32[]{:S(2)}) collective-permute-start(bf16[576,384]{1,0:T(8,128)(2,1)S(1)} %constant_dynamic-update-slice_fusion.refs_0_.refs_10_), channel_id=1, source_target_pairs={{0,4},{4,0},{1,5},{5,1},{2,6},{6,2},{3,7},{7,3},{8,12},{12,8},{9,1... | collective-permute-start | bytes 1327112 | tf_op jit(solution)/shard_map/ppermute | solution.py:738
  53.4 9.0 %collective-permute-start.10 = (bf16[576,384]{1,0:T(8,128)(2,1)S(1)}, bf16[576,384]{1,0:T(8,128)(2,1)S(1)}, u32[]{:S(2)}, u32[]{:S(2)}) collective-permute-start(bf16[576,384]{1,0:T(8,128)(2,1)S(1)} %constant_dynamic-update-slice_fusion.refs_0_.refs_10_), channel_id=1, source_target_pairs={{0,8},{8,0},{1,9},{9,1},{2,10},{10,2},{3,11},{11,3},{4,12},{12,4},... | collective-permute-start | bytes 1327112 | tf_op jit(solution)/shard_map/ppermute | solution.py:738
  53.4 9.1 %collective-permute-start.11 = (bf16[576,384]{1,0:T(8,128)(2,1)S(1)}, bf16[576,384]{1,0:T(8,128)(2,1)S(1)}, u32[]{:S(2)}, u32[]{:S(2)}) collective-permute-start(bf16[576,384]{1,0:T(8,128)(2,1)S(1)} %collective-permute-done.5.refs_1_.refs_11_), channel_id=1, source_target_pairs={{0,8},{8,0},{1,9},{9,1},{2,10},{10,2},{3,11},{11,3},{4,12},{12,4},... | collective-permute-start | bytes 1327112 | tf_op jit(solution)/shard_map/ppermute | solution.py:738
  53.9 15.7 %collective-permute-start.14 = (bf16[64,768]{1,0:T(8,128)(2,1)}, bf16[64,768]{1,0:T(8,128)(2,1)S(1)}, u32[]{:S(2)}, u32[]{:S(2)}) collective-permute-start(bf16[64,768]{1,0:T(8,128)(2,1)} %get-tuple-element.165.refs_4_), channel_id=1, source_target_pairs={{0,3},{1,2},{2,1},{3,0},{4,7},{5,6},{6,5},{7,4},{8,11},{9,10},{10,... | collective-permute-start | bytes 294920 | tf_op jit(solution)/shard_map/ppermute | solution.py:738
  55.9 13.7 %collective-permute-start.13 = (bf16[64,768]{1,0:T(8,128)(2,1)}, bf16[64,768]{1,0:T(8,128)(2,1)S(1)}, u32[]{:S(2)}, u32[]{:S(2)}) collective-permute-start(bf16[64,768]{1,0:T(8,128)(2,1)} %get-tuple-element.165.refs_4_), channel_id=1, source_target_pairs={{0,2},{1,3},{2,0},{3,1},{4,6},{5,7},{6,4},{7,5},{8,10},{9,11},{10,... | collective-permute-start | bytes 294920 | tf_op jit(solution)/shard_map/ppermute | solution.py:738
  55.9 13.7 %collective-permute-start.12 = (bf16[64,768]{1,0:T(8,128)(2,1)}, bf16[64,768]{1,0:T(8,128)(2,1)S(1)}, u32[]{:S(2)}, u32[]{:S(2)}) collective-permute-start(bf16[64,768]{1,0:T(8,128)(2,1)} %get-tuple-element.165.refs_4_), channel_id=1, source_target_pairs={{0,1},{1,0},{2,3},{3,2},{4,5},{5,4},{6,7},{7,6},{8,9},{9,8},{10,11... | collective-permute-start | bytes 294920 | tf_op jit(solution)/shard_map/ppermute | solution.py:738
  69.7 9.7 %collective-permute-start.15 = (bf16[64,1536]{1,0:T(8,128)(2,1)}, bf16[64,1536]{1,0:T(8,128)(2,1)S(1)}, u32[]{:S(2)}, u32[]{:S(2)}) collective-permute-start(bf16[64,1536]{1,0:T(8,128)(2,1)} %get-tuple-element.161.refs_1_.refs_11_), channel_id=1, source_target_pairs={{0,8},{8,0},{1,9},{9,1},{2,10},{10,2},{3,11},{11,3},{4,12},{12,4},... | collective-permute-start | bytes 589832 | tf_op jit(solution)/shard_map/ppermute | solution.py:738
  91.1 9.6 %collective-permute-start.21 = (bf16[64,768]{1,0:T(8,128)(2,1)}, bf16[64,768]{1,0:T(8,128)(2,1)S(1)}, u32[]{:S(2)}, u32[]{:S(2)}) collective-permute-start(bf16[64,768]{1,0:T(8,128)(2,1)} %get-tuple-element.164.refs_0_), channel_id=1, source_target_pairs={{0,2},{1,3},{2,0},{3,1},{4,6},{5,7},{6,4},{7,5},{8,10},{9,11},{10,... | collective-permute-start | bytes 294920 | tf_op jit(solution)/shard_map/ppermute | solution.py:738
  91.7 9.1 %collective-permute-start.20 = (bf16[64,768]{1,0:T(8,128)(2,1)}, bf16[64,768]{1,0:T(8,128)(2,1)S(1)}, u32[]{:S(2)}, u32[]{:S(2)}) collective-permute-start(bf16[64,768]{1,0:T(8,128)(2,1)} %get-tuple-element.164.refs_0_), channel_id=1, source_target_pairs={{0,1},{1,0},{2,3},{3,2},{4,5},{5,4},{6,7},{7,6},{8,9},{9,8},{10,11... | collective-permute-start | bytes 294920 | tf_op jit(solution)/shard_map/ppermute | solution.py:738
  106.4 11.1 %collective-permute-start.24 = (bf16[64,768]{1,0:T(8,128)(2,1)}, bf16[64,768]{1,0:T(8,128)(2,1)S(1)}, u32[]{:S(2)}, u32[]{:S(2)}) collective-permute-start(bf16[64,768]{1,0:T(8,128)(2,1)} %get-tuple-element.172), channel_id=1, source_target_pairs={{0,2},{1,3},{2,0},{3,1},{4,6},{5,7},{6,4},{7,5},{8,10},{9,11},{10,... | collective-permute-start | bytes 294920 | tf_op jit(solution)/shard_map/ppermute | solution.py:738
  128.4 10.3 %collective-permute-start.29 = (bf16[32,1536]{1,0:T(8,128)(2,1)}, bf16[32,1536]{1,0:T(8,128)(2,1)S(1)}, u32[]{:S(2)}, u32[]{:S(2)}) collective-permute-start(bf16[32,1536]{1,0:T(8,128)(2,1)} %get-tuple-element.180), channel_id=1, source_target_pairs={{2,0},{10,8},{3,1},{11,9},{4,2},{12,10},{5,3},{13,11},{6,4},{14,12... | collective-permute-start | bytes 294920 | tf_op jit(solution)/shard_map/ppermute | solution.py:767
  129.9 10.1 %collective-permute-start.26 = (bf16[64,1536]{1,0:T(8,128)(2,1)}, bf16[64,1536]{1,0:T(8,128)(2,1)S(1)}, u32[]{:S(2)}, u32[]{:S(2)}) collective-permute-start(bf16[64,1536]{1,0:T(8,128)(2,1)} %get-tuple-element.178), channel_id=1, source_target_pairs={{0,8},{8,0},{1,9},{9,1},{2,10},{10,2},{3,11},{11,3},{4,12},{12,4},... | collective-permute-start | bytes 589832 | tf_op jit(solution)/shard_map/ppermute | solution.py:738
  149.0 9.9 %collective-permute-start.32 = (bf16[4,4,144,384]{3,2,1,0:T(8,128)(2,1)}, bf16[4,4,144,384]{3,2,1,0:T(8,128)(2,1)S(1)}, u32[]{:S(2)}, u32[]{:S(2)}) collective-permute-start(bf16[4,4,144,384]{3,2,1,0:T(8,128)(2,1)} %get-tuple-element.192), channel_id=1, source_target_pairs={{0,8},{8,0},{1,9},{9,1},{2,10},{10,2},{3,11},{11,3},{4,12},{12,4},... | collective-permute-start | bytes 5308424 | tf_op jit(solution)/shard_map/ppermute | solution.py:738
  161.3 40.6 %all-to-all-start.1 = ((bf16[4,960,384]{2,1,0:T(8,128)(2,1)}), bf16[4,960,384]{2,1,0:T(8,128)(2,1)S(1)}, u32[]{:S(2)}, u32[]{:S(2)}) async-start(bf16[4,960,384]{2,1,0:T(8,128)(2,1)} %pad_maximum_fusion), calls=%async_computation.1 | async-start | bytes 5898240 | tf_op jit(solution)/shard_map/all_to_all | solution.py:837
  176.5 18.9 %collective-permute-start.33 = (bf16[4,4,96,384]{3,2,1,0:T(8,128)(2,1)}, bf16[4,4,96,384]{3,2,1,0:T(8,128)(2,1)S(1)}, u32[]{:S(2)}, u32[]{:S(2)}) collective-permute-start(bf16[4,4,96,384]{3,2,1,0:T(8,128)(2,1)} %get-tuple-element.198), channel_id=1, source_target_pairs={{0,8},{8,0},{1,9},{9,1},{2,10},{10,2},{3,11},{11,3},{4,12},{12,4},... | collective-permute-start | bytes 3538952 | tf_op jit(solution)/shard_map/ppermute | solution.py:738
  203.1 30.6 %all-to-all-start.2 = ((bf16[4,592,384]{2,1,0:T(8,128)(2,1)}), bf16[4,592,384]{2,1,0:T(8,128)(2,1)S(1)}, u32[]{:S(2)}, u32[]{:S(2)}) async-start(bf16[4,592,384]{2,1,0:T(8,128)(2,1)} %pad_maximum_fusion.1), calls=%async_computation.2 | async-start | bytes 3637248 | tf_op jit(solution)/shard_map/all_to_all | solution.py:837
  208.2 10.4 %collective-permute-start.40 = (bf16[2,144,384]{2,1,0:T(8,128)(2,1)S(1)}, bf16[2,144,384]{2,1,0:T(8,128)(2,1)S(1)}, u32[]{:S(2)}, u32[]{:S(2)}) collective-permute-start(bf16[2,144,384]{2,1,0:T(8,128)(2,1)S(1)} %slice_bitcast_fusion.3), channel_id=1, source_target_pairs={{0,1},{1,0},{2,3},{3,2},{4,5},{5,4},{6,7},{7,6},{8,9},{9,8},{10,11... | collective-permute-start | bytes 663560 | tf_op jit(solution)/shard_map/ppermute | solution.py:738
  208.3 14.7 %collective-permute-start.42 = (bf16[64,768]{1,0:T(8,128)(2,1)S(1)}, bf16[64,768]{1,0:T(8,128)(2,1)S(1)}, u32[]{:S(2)}, u32[]{:S(2)}) collective-permute-start(bf16[64,768]{1,0:T(8,128)(2,1)S(1)} %copy-done.47), channel_id=1, source_target_pairs={{0,1},{1,0},{2,3},{3,2},{4,5},{5,4},{6,7},{7,6},{8,9},{9,8},{10,11... | collective-permute-start | bytes 294920 | tf_op jit(solution)/shard_map/ppermute | solution.py:738
  210.3 12.7 %collective-permute-start.43 = (bf16[64,768]{1,0:T(8,128)(2,1)S(1)}, bf16[64,768]{1,0:T(8,128)(2,1)S(1)}, u32[]{:S(2)}, u32[]{:S(2)}) collective-permute-start(bf16[64,768]{1,0:T(8,128)(2,1)S(1)} %copy-done.46), channel_id=1, source_target_pairs={{0,2},{1,3},{2,0},{3,1},{4,6},{5,7},{6,4},{7,5},{8,10},{9,11},{10,... | collective-permute-start | bytes 294920 | tf_op jit(solution)/shard_map/ppermute | solution.py:738
  213.8 12.0 %collective-permute-start.44 = (bf16[64,768]{1,0:T(8,128)(2,1)S(1)}, bf16[64,768]{1,0:T(8,128)(2,1)S(1)}, u32[]{:S(2)}, u32[]{:S(2)}) collective-permute-start(bf16[64,768]{1,0:T(8,128)(2,1)S(1)} %copy-done.45), channel_id=1, source_target_pairs={{0,3},{1,2},{2,1},{3,0},{4,7},{5,6},{6,5},{7,4},{8,11},{9,10},{10,... | collective-permute-start | bytes 294920 | tf_op jit(solution)/shard_map/ppermute | solution.py:738
  218.7 10.2 %collective-permute-start.41 = (bf16[1,144,384]{2,1,0:T(8,128)(2,1)S(1)}, bf16[1,144,384]{2,1,0:T(8,128)(2,1)S(1)}, u32[]{:S(2)}, u32[]{:S(2)}) collective-permute-start(bf16[1,144,384]{2,1,0:T(8,128)(2,1)S(1)} %slice_bitcast_fusion.7), channel_id=1, source_target_pairs={{0,2},{1,3},{2,0},{3,1},{4,6},{5,7},{6,4},{7,5},{8,10},{9,11},{10,... | collective-permute-start | bytes 331784 | tf_op jit(solution)/shard_map/ppermute | solution.py:738
  229.9 12.8 %collective-permute-start.51 = (bf16[528,384]{1,0:T(8,128)(2,1)}, bf16[528,384]{1,0:T(8,128)(2,1)S(1)}, u32[]{:S(2)}, u32[]{:S(2)}) collective-permute-start(bf16[528,384]{1,0:T(8,128)(2,1)} %get-tuple-element.252), channel_id=1, source_target_pairs={{0,16},{4,20},{16,0},{20,4},{1,17},{5,21},{17,1},{21,5},{2,18},{6,... | collective-permute-start | bytes 1216520 | tf_op jit(solution)/shard_map/ppermute | solution.py:738
  232.3 19.8 %collective-permute-start.50 = (bf16[528,384]{1,0:T(8,128)(2,1)}, bf16[528,384]{1,0:T(8,128)(2,1)S(1)}, u32[]{:S(2)}, u32[]{:S(2)}) collective-permute-start(bf16[528,384]{1,0:T(8,128)(2,1)} %get-tuple-element.252), channel_id=1, source_target_pairs={{0,4},{4,0},{16,20},{20,16},{1,5},{5,1},{17,21},{21,17},{2,6},{6,2... | collective-permute-start | bytes 1216520 | tf_op jit(solution)/shard_map/ppermute | solution.py:738
  233.1 18.9 %collective-permute-start.52 = (bf16[528,384]{1,0:T(8,128)(2,1)}, bf16[528,384]{1,0:T(8,128)(2,1)}, u32[]{:S(2)}, u32[]{:S(2)}) collective-permute-start(bf16[528,384]{1,0:T(8,128)(2,1)} %get-tuple-element.252), channel_id=1, source_target_pairs={{0,20},{4,16},{16,4},{20,0},{1,21},{5,17},{17,5},{21,1},{2,22},{6,... | collective-permute-start | bytes 1216520 | tf_op jit(solution)/shard_map/ppermute | solution.py:738
  234.0 19.2 %all-to-all-start.3 = ((bf16[8,48,384]{2,1,0:T(8,128)(2,1)}), bf16[8,48,384]{2,1,0:T(8,128)(2,1)}, u32[]{:S(2)}, u32[]{:S(2)}) async-start(bf16[8,48,384]{2,1,0:T(8,128)(2,1)} %bitcast.28), calls=%async_computation.3 | async-start | bytes 589824 | tf_op jit(solution)/shard_map/all_to_all | solution.py:837
  238.9 14.5 %collective-permute-start.45 = (bf16[2,160,384]{2,1,0:T(8,128)(2,1)}, bf16[2,160,384]{2,1,0:T(8,128)(2,1)}, u32[]{:S(2)}, u32[]{:S(2)}) collective-permute-start(bf16[2,160,384]{2,1,0:T(8,128)(2,1)} %slice_bitcast_fusion.1), channel_id=1, source_target_pairs={{0,1},{1,0},{2,3},{3,2},{4,5},{5,4},{6,7},{7,6},{8,9},{9,8},{10,11... | collective-permute-start | bytes 737288 | tf_op jit(solution)/shard_map/ppermute | solution.py:738
  253.3 20.3 %collective-permute-start.53 = (bf16[4,528,384]{2,1,0:T(8,128)(2,1)S(1)}, bf16[4,528,384]{2,1,0:T(8,128)(2,1)}, u32[]{:S(2)}, u32[]{:S(2)}) collective-permute-start(bf16[4,528,384]{2,1,0:T(8,128)(2,1)S(1)} %pad_maximum_fusion.2.refs_0_), channel_id=1, source_target_pairs={{0,8},{8,0},{1,9},{9,1},{2,10},{10,2},{3,11},{11,3},{4,12},{12,4},... | collective-permute-start | bytes 4866056 | tf_op jit(solution)/shard_map/ppermute | solution.py:738
  254.9 16.9 %collective-permute-start.54 = (bf16[8,48,384]{2,1,0:T(8,128)(2,1)}, bf16[8,48,384]{2,1,0:T(8,128)(2,1)S(1)}, u32[]{:S(2)}, u32[]{:S(2)}) collective-permute-start(bf16[8,48,384]{2,1,0:T(8,128)(2,1)} %all-to-all-done.3), channel_id=1, source_target_pairs={{0,0},{4,8},{8,4},{12,12},{1,1},{5,9},{9,5},{13,13},{2,2},{6,10},{... | collective-permute-start | bytes 884744 | tf_op jit(solution)/shard_map/ppermute | solution.py:749
  (76 other events, 447.5 us)
